TPU v7x, 32 devices: a whole 2x2x4 slice. The times are simulated.
32 devices in a mesh: row: 8 (over z, core), col: 4 (over y, x).
Axes of the slice: x: 2, y: 2, z: 4, core: 2. Of those that a mesh axis runs over, the one named last changes fastest.
Arguments:
- matrix: float32 [8192, 4096], P('row', 'col'), may hold values from -6 to 166
Outputs:
- updated: float32 [8192, 4096], P('row', 'col')
All inputs are finite; a program needn't handle non-finite values.
Results may differ from a plain program's by a relative error of at most 0.0003.
Values sent between devices are 32-bit elements; how exact they have to be, the bound alone decides.
No kernel may reach another device: no remote copies, remote signals or barrier semaphores. Data moves between devices by JAX's collectives and lax.ppermute only.
A program may use at most 64 MiB of HBM per device.

v0:
```python
import jax
import jax.numpy as jnp
from jax import lax
from jax.sharding import PartitionSpec as P

NB = 128


def from_root(value, axis, source):
    kept = jnp.where(lax.axis_index(axis) == source, value, 0).astype(value.dtype)
    return lax.psum(kept, axis)


def factor(corner):
    symmetric = jnp.tril(corner) + jnp.tril(corner, -1).T
    lower_factor = jnp.linalg.cholesky(symmetric)
    identity = jnp.eye(corner.shape[0], dtype=jnp.float32)
    inverse = jax.scipy.linalg.solve_triangular(lower_factor, identity, lower=True)
    return (lower_factor, inverse)


def body(matrix):
    rows_here = lax.axis_size("row")
    cols_here = lax.axis_size("col")
    row_index = lax.axis_index("row")
    col_index = lax.axis_index("col")
    row_blocks = matrix.shape[0] // NB
    col_blocks = matrix.shape[1] // NB
    corner = matrix[:NB, :NB]
    local_factor, local_inverse = factor(corner)
    stacked = from_root(jnp.stack([local_factor, local_inverse]), "row", 0)
    lower_factor = stacked[0]
    inverse = stacked[1]
    panel = lax.dot_general(
        matrix[:, :NB],
        inverse,
        (((1,), (1,)), ((), ())),
        precision=lax.Precision.HIGHEST,
        preferred_element_type=jnp.float32,
    )
    panel = panel.at[:NB].set(jnp.where(row_index == 0, lower_factor, panel[:NB]))
    panel = from_root(panel, "col", 0)
    whole = lax.all_gather(panel, "row", axis=0, tiled=True)
    all_blocks = whole.reshape(rows_here * row_blocks, NB, NB)
    wanted = jnp.arange(col_blocks, dtype=jnp.int32) * cols_here + col_index
    source_rows = wanted % rows_here * row_blocks + wanted // rows_here
    mirror = jnp.take(all_blocks, source_rows, axis=0).reshape(col_blocks * NB, NB)
    product = lax.dot_general(
        panel,
        mirror,
        (((1,), (1,)), ((), ())),
        precision=lax.Precision.HIGHEST,
        preferred_element_type=jnp.float32,
    )
    fresh = matrix - product
    global_rows = jnp.arange(row_blocks, dtype=jnp.int32) * rows_here + row_index
    global_cols = jnp.arange(col_blocks, dtype=jnp.int32) * cols_here + col_index
    keep_mask = (global_rows[:, None] >= global_cols[None, :]) & (global_cols[None, :] >= 1)
    shaped_old = matrix.reshape(row_blocks, NB, col_blocks, NB)
    shaped_new = fresh.reshape(row_blocks, NB, col_blocks, NB)
    result = jnp.where(keep_mask[:, None, :, None], shaped_new, shaped_old).reshape(matrix.shape)
    result = result.at[:, :NB].set(jnp.where(col_index == 0, panel, result[:, :NB]))
    return result


def solution(mesh):
    return jax.shard_map(
        body,
        mesh=mesh,
        in_specs=(P("row", "col"),),
        out_specs=P("row", "col"),
        check_vma=False,
    )
```

profile of v0, /device:TPU:6, one launch (start us, length us, event | category | flops | bytes accessed | tf_op | source)
XLA Modules:
  0.0 204.3 jit_solution(1696970586358199093)
XLA Ops:
  6.5 0.0 all-reduce.3.cloned.1.call-start
  6.5 0.8 slice.64
  7.4 0.1 copy.8
  7.5 0.9 bitcast_add_fusion.1
  8.3 0.1 copy.5
  8.5 11.7 %cholesky.19 = f32[128,128]{1,0:T(8,128)S(1)} custom-call(f32[128,128]{1,0:T(8,128)S(1)} %fusion.4), custom_call_target="Cholesky" | custom-call | tf_op jit(solution)/shard_map/jit(cholesky)/cholesky | solution.py:16
  20.2 0.6 compare_reduce_fusion.1
  20.9 0.7 fusion.5
  21.5 9.8 %custom-call.7 = f32[1,128,128]{1,2,0:T(8,128)S(1)} custom-call(f32[1,128,128]{2,1,0:T(8,128)S(1)} %get-tuple-element.30), custom_call_target="InvertDiagBlocksLowerTriangular" | custom-call | tf_op jit(solution)/shard_map/jit(_solve_triangular)/triangular_solve | solution.py:18
  31.3 0.2 convolution_bitcast_fusion.1
  31.6 0.7 maximum_select_fusion
  32.3 0.0 all-reduce.3.cloned.1.call-update
  32.3 0.0 all-reduce.5.cloned.1.call-start
  32.3 55.5 %all-reduce.3.cloned.1.call-done = f32[2,128,128]{2,1,0:T(8,128)} async-done(((f32[2,128,128]{2,1,0:T(8,128)}), f32[2,128,128]{2,1,0:T(8,128)}) %all-reduce.3.cloned.1.call-update) | async-done | bytes 131088 | tf_op jit(solution)/shard_map/psum | solution.py:11
  87.8 1.7 convolution_bitcast_fusion
  89.5 0.9 fusion.2
  90.3 0.8 broadcast_select_fusion
  91.2 0.0 all-reduce.5.cloned.1.call-update
  91.2 0.0 all-gather.2.cloned.1.call-start
  91.2 43.5 %all-reduce.5.cloned.1.call-done = f32[1024,128]{1,0:T(8,128)} async-done(((f32[1024,128]{1,0:T(8,128)}), f32[1024,128]{1,0:T(8,128)}) %all-reduce.5.cloned.1.call-update) | async-done | bytes 524304 | tf_op jit(solution)/shard_map/psum | solution.py:11
  134.8 0.0 all-gather.2.cloned.1.call-update
  134.8 0.6 compare_reduce_fusion
  135.5 0.1 broadcast_bitcast_fusion
  135.5 0.1 compare_and_fusion
  135.6 48.9 %all-gather.2.cloned.1.call-done = f32[8192,128]{1,0:T(8,128)} async-done(((f32[1024,128]{1,0:T(8,128)}), f32[8192,128]{1,0:T(8,128)}) %all-gather.2.cloned.1.call-update) | async-done | bytes 4194320 | tf_op jit(solution)/shard_map/all_gather | solution.py:43
  184.6 2.8 %gather_fusion = f32[8,128,128]{2,1,0:T(8,128)S(1)} fusion(f32[64,128,128]{2,1,0:T(8,128)} %bitcast.38, s32[1024]{0:T(1024)S(1)} %pad_clamp_fusion), kind=kCustom, calls=%fused_computation | custom fusion | bytes 1048608 | tf_op jit(solution)/shard_map/jit(_take)/gather | solution.py:47
  187.3 0.2 bitcast_select_fusion
  187.5 0.3 broadcast_in_dim.44
  187.9 0.0 copy-start
  187.9 7.4 %subtract_select_fusion = f32[1024,1024]{1,0:T(8,128)} fusion(f32[1024,1024]{1,0:T(8,128)} %param.5, pred[128,8,8,128]{3,2,1,0:T(8,128)(4,1)S(1)} %bitcast.37, f32[1024,128]{1,0:T(8,128)} %all-reduce.5.cloned.1.call-done, f32[1024,128]{1,0:T(8,128)S(1)} %bitcast_select_fusion), kind=kOutput, calls=%fused_computation.1 | convolution fusion | flops 1612709888 | bytes 10485760 | tf_op jit(solution)/shard_map/dot_general | solution.py:48
  195.3 0.0 copy-done
  195.3 2.5 %fusion = f32[1024,1024]{1,0:T(8,128)} fusion(f32[1024,1024]{1,0:T(8,128)} %subtract_select_fusion, f32[1024,128]{1,0:T(8,128)S(1)} %copy-done, pred[]{:T(512)} %compare_reduce_fusion, pred[]{:T(512)S(6)} %eq.6), kind=kLoop, calls=%fused_computation.5 | loop fusion | flops 262144 | bytes 1573377 | tf_op jit(solution)/shard_map/scatter | solution.py:62
  (9 shorter events, 0.1 us)
Async XLA Ops:
  6.5 81.3 %all-reduce.3.cloned.1.call-start = ((), (), s32[]{:S(2)}) async-start(), calls=%async_computation | async-start | bytes 262144 | tf_op jit(solution)/shard_map/psum | solution.py:11
  32.3 102.5 %all-reduce.5.cloned.1.call-start = ((), (), s32[]{:S(2)}) async-start(), calls=%async_computation.1 | async-start | bytes 1048576 | tf_op jit(solution)/shard_map/psum | solution.py:11
  91.2 93.4 %all-gather.2.cloned.1.call-start = ((), (), s32[]{:S(2)}) async-start(), calls=%async_computation.2 | async-start | bytes 4718592 | tf_op jit(solution)/shard_map/all_gather | solution.py:43
  187.9 7.4 %copy-start = (f32[1024,128]{1,0:T(8,128)S(1)}, f32[1024,128]{1,0:T(8,128)}, u32[]{:S(2)}) copy-start(f32[1024,128]{1,0:T(8,128)} %all-reduce.5.cloned.1.call-done) | copy-start | bytes 1572868
Sparse Core Ops, SparseCore 0:
  32.4 55.3 all-reduce.2
  91.3 43.4 all-reduce.4
  136.4 48.0 all-gather.1
where the time goes:
time: 206 us; the launch traced here: 204 us
  waiting for transfers between devices  148 us (72%)
  other arithmetic  29.5 us (14%)
  between operations  13.2 us (6%)
  matrix products  9.34 us (5%)
  local copies, waits for them, and re-layouts  4.2 us (2%)
    psum x2, waiting for transfers between devices, from_root(): return lax.psum(kept, axis)  99 us
    all_gather x1, waiting for transfers between devices, body(): whole = lax.all_gather(panel, 'row', axis=0, tiled=True)  48.9 us
    another operation x3, other arithmetic, factor(): lower_factor = jnp.linalg.cholesky(symmetric)  12.4 us
    another operation x1, other arithmetic, factor(): jax.scipy.linalg.solve_triangular(lower_factor, identity, lower=True)  9.81 us
    dot_general x1, matrix products, body(): lax.dot_general(panel, mirror, (((1,), (1,)), ((), ())), precision=lax.Pr...  7.42 us
  transfers between devices with their start and end apart: 3, of which 3 were waited for; matrix products, arithmetic and copies ran while one was open for 0% of the time, Pallas kernels for 0%

commit v1 on v0

v1 whole, which is shorter than its diff:
```python
import functools

import jax
import jax.numpy as jnp
from jax import lax
from jax.experimental import pallas as pl
from jax.experimental.pallas import tpu as pltpu
from jax.sharding import PartitionSpec as P

NB = 128
AXES = ("row", "col")
HIGHEST = lax.Precision.HIGHEST
TRANS_B = (((1,), (1,)), ((), ()))


def factor_kernel(place_ref, corner_ref, lower_ref, inverse_ref):
    on_root = (place_ref[0] == 0) & (place_ref[1] == 0)

    @pl.when(jnp.logical_not(on_root))
    def _():
        lower_ref[...] = jnp.zeros_like(lower_ref)
        inverse_ref[...] = jnp.zeros_like(inverse_ref)

    @pl.when(on_root)
    def _():
        rows = lax.broadcasted_iota(jnp.int32, (NB, NB), 0)
        cols = lax.broadcasted_iota(jnp.int32, (NB, NB), 1)
        corner = corner_ref[...]
        left = jnp.where(rows >= cols, corner, corner.T)
        right = jnp.where(rows == cols, 1.0, 0.0).astype(jnp.float32)
        lefts = [left[8 * b:8 * b + 8, :] for b in range(NB // 8)]
        rights = [right[8 * b:8 * b + 8, :] for b in range(NB // 8)]
        sub = lax.broadcasted_iota(jnp.int32, (8, NB), 0)
        for k in range(NB):
            b, o = divmod(k, 8)
            pivot = lefts[b][o:o + 1, k:k + 1]
            inv_pivot = 1.0 / jnp.broadcast_to(pivot, (1, NB))
            row_left = lefts[b][o:o + 1, :]
            row_right = rights[b][o:o + 1, :]
            for i in range(b, NB // 8):
                mult = jnp.broadcast_to(lefts[i][:, k:k + 1], (8, NB)) * inv_pivot
                if i == b:
                    if o == 7:
                        continue
                    mult = jnp.where(sub > o, mult, 0.0)
                lefts[i] = lefts[i] - mult * row_left
                rights[i] = rights[i] - mult * row_right
        upper = jnp.concatenate(lefts, axis=0)
        unit_inverse = jnp.concatenate(rights, axis=0)
        diagonal = jnp.sum(jnp.where(rows == cols, upper, 0.0), axis=1, keepdims=True)
        scale = 1.0 / jnp.sqrt(jnp.broadcast_to(diagonal, (NB, NB)))
        lower_ref[...] = jnp.where(rows >= cols, (upper * scale).T, 0.0)
        inverse_ref[...] = jnp.where(rows >= cols, unit_inverse * scale, 0.0)


def factor(place, corner):
    return pl.pallas_call(
        factor_kernel,
        out_shape=[jax.ShapeDtypeStruct((NB, NB), jnp.float32)] * 2,
        in_specs=[pl.BlockSpec(memory_space=pltpu.SMEM), pl.BlockSpec(memory_space=pltpu.VMEM)],
        out_specs=[pl.BlockSpec(memory_space=pltpu.VMEM)] * 2,
        cost_estimate=pl.CostEstimate(flops=20_000_000, bytes_accessed=200_000, transcendentals=0),
        name="factor",
    )(place, corner)


def split(value):
    high = value.astype(jnp.bfloat16)
    low = (value - high.astype(jnp.float32)).astype(jnp.bfloat16)
    return high, low


def dot_t(a, b):
    return lax.dot_general(a, b, TRANS_B, preferred_element_type=jnp.float32)


def update_kernel(rows_here, cols_here, sources, place_ref, matrix_ref, panel_ref, mirror_ref,
                  inverse_ref, lower_ref, out_ref, high_ref, low_ref):
    step = pl.program_id(0)
    col_blocks = matrix_ref.shape[1] // NB
    each = col_blocks // sources

    @pl.when(step == 0)
    def _():
        mirror = lax.dot_general(mirror_ref[...], inverse_ref[...], TRANS_B, precision=HIGHEST,
                                 preferred_element_type=jnp.float32)
        high, low = split(mirror)
        high_ref[...] = high
        low_ref[...] = low

    panel = lax.dot_general(panel_ref[...], inverse_ref[...], TRANS_B, precision=HIGHEST,
                            preferred_element_type=jnp.float32)
    high, low = split(panel)
    row = step * rows_here + place_ref[0]
    for t in range(col_blocks):
        block = (t % sources) * each + t // sources
        here = pl.ds(block * NB, NB)
        product = dot_t(high, high_ref[here, :]) + (
            dot_t(high, low_ref[here, :]) + dot_t(low, high_ref[here, :]))
        col = t * cols_here + place_ref[1]
        keep = (row >= col) & (col >= 1)
        old = matrix_ref[:, t * NB:(t + 1) * NB]
        new = jnp.where(keep, old - product, old)
        if t == 0:
            factor_block = jnp.where(row == 0, lower_ref[...], panel)
            new = jnp.where(col == 0, factor_block, new)
        out_ref[:, t * NB:(t + 1) * NB] = new


def update(place, matrix, panel, mirror, inverse, lower, rows_here, cols_here, sources):
    height, width = matrix.shape
    whole = lambda shape: pl.BlockSpec(shape, lambda s: (0, 0))
    return pl.pallas_call(
        functools.partial(update_kernel, rows_here, cols_here, sources),
        out_shape=jax.ShapeDtypeStruct(matrix.shape, jnp.float32),
        grid=(height // NB,),
        in_specs=[
            pl.BlockSpec(memory_space=pltpu.SMEM),
            pl.BlockSpec((NB, width), lambda s: (s, 0)),
            pl.BlockSpec((NB, NB), lambda s: (s, 0)),
            whole(mirror.shape),
            whole((NB, NB)),
            whole((NB, NB)),
        ],
        out_specs=pl.BlockSpec((NB, width), lambda s: (s, 0)),
        scratch_shapes=[pltpu.VMEM((width, NB), jnp.bfloat16)] * 2,
        compiler_params=pltpu.CompilerParams(dimension_semantics=("arbitrary",)),
        cost_estimate=pl.CostEstimate(flops=2 * height * width * NB * 3,
                                      bytes_accessed=8 * height * width, transcendentals=0),
        name="update",
    )(place, matrix, panel, mirror, inverse, lower)


def body(matrix):
    rows_here = lax.axis_size("row")
    cols_here = lax.axis_size("col")
    row_index = lax.axis_index("row")
    col_index = lax.axis_index("col")
    col_blocks = matrix.shape[1] // NB
    sources = rows_here // cols_here
    place = jnp.stack([row_index, col_index]).astype(jnp.int32)

    def at(r, c):
        return r * cols_here + c

    column = matrix[:, :NB]
    first = column[:NB * (col_blocks // sources)]

    hop = lax.ppermute(first, AXES, [(at(r, 0), at(r ^ 1, r % cols_here)) for r in range(rows_here)])

    panels = []
    held = {0: column}
    step = 1
    while step < cols_here:
        merged = sum(held.values()) if len(held) > 1 else column
        base = range(0, step)
        near = lax.ppermute(merged, "col", [(h, h + step) for h in base])
        panels.append(near)
        if 2 * step < cols_here:
            far = lax.ppermute(merged, "col", [(h, h + 2 * step) for h in base])
            panels.append(far)
            relays = near + far
            pairs = [(at(r, h + (step if r % 2 == 0 else 2 * step)), at(r, h + 3 * step))
                     for r in range(rows_here) for h in base]
            panels.append(lax.ppermute(relays, AXES, pairs))
        held = {0: jnp.where(col_index == 0, column, 0.0), **dict(enumerate(panels, 1))}
        step *= 4

    lower, inverse = factor(place, matrix[:NB, :NB])

    own = [((r ^ 1) % cols_here, r) for r in range(rows_here)]
    mirrors = [[] for _ in range(sources)]
    for k in range(1, rows_here):
        got = lax.ppermute(hop, AXES, [(at(r, c), at((r + k) % rows_here, c)) for c, r in own])
        for q in range(sources):
            origin = (row_index - k) % rows_here
            mine = (origin ^ 1) == col_index + q * cols_here
            mirrors[q].append(jnp.where(mine, got, 0.0))
    for q in range(sources):
        mirrors[q].append(jnp.where((row_index ^ 1) == col_index + q * cols_here, hop, 0.0))
    mirror = jnp.concatenate([sum(parts) for parts in mirrors], axis=0)

    holders = [(0, 0)]
    offsets = []
    bit = rows_here // 2
    while bit >= 2:
        offsets.append((bit, 0))
        bit //= 2
    bit = cols_here // 2
    while bit >= 1:
        offsets.append((0, bit))
        bit //= 2
    offsets.append((1, 0))
    for dr, dc in offsets:
        inverse = inverse + lax.ppermute(
            inverse, AXES, [(at(r, c), at(r + dr, c + dc)) for r, c in holders])
        holders = holders + [(r + dr, c + dc) for r, c in holders]

    panel = jnp.where(col_index == 0, column, 0.0) + sum(panels)
    return update(place, matrix, panel, mirror, inverse, lower, rows_here, cols_here, sources)


def solution(mesh):
    return jax.shard_map(
        body,
        mesh=mesh,
        in_specs=(P("row", "col"),),
        out_specs=P("row", "col"),
        check_vma=False,
    )
```

time: 206 us -> 79.6 us (0.39)
  the two profiles are of different devices: /device:TPU:6 before, /device:TPU:30 now
where the time goes in v1:
time: 79.6 us; the launch traced here: 78.8 us
  waiting for transfers between devices  33.8 us (42%)
  starting transfers between devices  21.8 us (27%)
  Pallas kernels  13.3 us (17%)
  other arithmetic  5.24 us (7%)
  local copies, waits for them, and re-layouts  4.3 us (5%)
    ppermute x5, waiting for transfers between devices, body(): lax.ppermute(inverse, AXES, [(at(r, c), at(r + dr, c + dc)) for r, c in h...  25.2 us
    ppermute x7, starting transfers between devices, body(): lax.ppermute(hop, AXES, [(at(r, c), at((r + k) % rows_here, c)) for c, r...  13.2 us
    pallas_call x1, Pallas kernels, update(): pl.pallas_call(functools.partial(update_kernel, rows_here, cols_here, sou...  11.8 us
    ppermute x1, waiting for transfers between devices, body(): panels.append(lax.ppermute(relays, AXES, pairs))  5.29 us
    ppermute x5, starting transfers between devices, body(): lax.ppermute(inverse, AXES, [(at(r, c), at(r + dr, c + dc)) for r, c in h...  4.56 us
    ppermute x7, waiting for transfers between devices, body(): lax.ppermute(hop, AXES, [(at(r, c), at((r + k) % rows_here, c)) for c, r...  3.36 us
    add x2, other arithmetic, body(): panel = jnp.where(col_index == 0, column, 0.0) + sum(panels)  1.97 us
    slice x1, local copies, waits for them, and re-layouts, body(): column = matrix[:, :NB]  1.87 us
  transfers between devices with their start and end apart: 16, of which 5 were waited for; matrix products, arithmetic and copies ran while one was open for 8% of the time, Pallas kernels for 2%

profile of v1, /device:TPU:30, one launch (start us, length us, event | category | flops | bytes accessed | tf_op | source)
XLA Modules:
  0.0 78.8 jit_solution(4533098413095646324)
XLA Ops:
  0.0 1.0 %slice.11 = f32[512,128]{1,0:T(8,128)S(1)} slice(f32[1024,1024]{1,0:T(8,128)} %matrix_ref.1), slice={[0:512], [0:128]} | slice | bytes 524288 | tf_op jit(solution)/shard_map/slice | solution.py:147
  1.0 1.3 %collective-permute-start.3 = (f32[512,128]{1,0:T(8,128)S(1)}, f32[512,128]{1,0:T(8,128)S(1)}, u32[]{:S(2)}, u32[]{:S(2)}) collective-permute-start(f32[512,128]{1,0:T(8,128)S(1)} %slice.11), channel_id=1, source_target_pairs={{0,4},{4,1},{8,14},{12,11},{16,20},{20,17},{24,30},{28,27}} | collective-permute-start | bytes 786440 | tf_op jit(solution)/shard_map/ppermute | solution.py:149
  2.3 1.9 %slice.10 = f32[1024,128]{1,0:T(8,128)} slice(f32[1024,1024]{1,0:T(8,128)} %matrix_ref.1), slice={[0:1024], [0:128]} | slice | bytes 1048576 | tf_op jit(solution)/shard_map/slice | solution.py:146
  4.1 0.7 collective-permute-start
  4.8 0.7 collective-permute-start.1
  5.5 1.5 %slice.12.corner_ref = f32[128,128]{1,0:T(8,128)} slice(f32[1024,1024]{1,0:T(8,128)} %matrix_ref.1), slice={[0:128], [0:128]} | slice | bytes 131072 | tf_op jit(solution)/shard_map/slice | solution.py:169
  7.0 0.7 pad_add_fusion.place_ref
  7.7 1.5 %factor.1 = (f32[128,128]{1,0:T(8,128)}, f32[128,128]{1,0:T(8,128)}) custom-call(s32[2]{0:T(128)} %pad_add_fusion.place_ref, f32[128,128]{1,0:T(8,128)} %slice.12.corner_ref), custom_call_target="tpu_custom_call" | custom-call | flops 20000000 | bytes 200000 | tf_op jit(solution)/shard_map/factor/pallas_call | solution.py:57
  9.2 0.7 collective-permute-start.11
  9.8 0.0 collective-permute-done.11
  9.8 0.8 %add.138 = f32[128,128]{1,0:T(8,128)S(1)} add(f32[128,128]{1,0:T(8,128)} %get-tuple-element.7, f32[128,128]{1,0:T(8,128)S(1)} %collective-permute-done.11) | non-fusion elementwise | flops 16384 | bytes 196608 | tf_op jit(solution)/shard_map/add | solution.py:195
  10.7 0.7 collective-permute-start.12
  11.4 0.0 collective-permute-done.3
  11.4 1.3 %collective-permute-start.10 = (f32[512,128]{1,0:T(8,128)S(1)}, f32[512,128]{1,0:T(8,128)S(1)}, u32[]{:S(2)}, u32[]{:S(2)}) collective-permute-start(f32[512,128]{1,0:T(8,128)S(1)} %collective-permute-done.3), channel_id=1, source_target_pairs={{1,29},{4,0},{11,7},{14,10},{17,13},{20,16},{27,23},{30,26}} | collective-permute-start | bytes 786440 | tf_op jit(solution)/shard_map/ppermute | solution.py:174
  12.7 1.3 %collective-permute-start.9 = (f32[512,128]{1,0:T(8,128)S(1)}, f32[512,128]{1,0:T(8,128)S(1)}, u32[]{:S(2)}, u32[]{:S(2)}) collective-permute-start(f32[512,128]{1,0:T(8,128)S(1)} %collective-permute-done.3), channel_id=1, source_target_pairs={{1,25},{4,28},{11,3},{14,6},{17,9},{20,12},{27,19},{30,22}} | collective-permute-start | bytes 786440 | tf_op jit(solution)/shard_map/ppermute | solution.py:174
  14.0 0.0 collective-permute-done.12
  14.0 0.7 collective-permute-start.13
  14.7 0.0 collective-permute-done.13
  14.7 1.3 %collective-permute-start.14 = (f32[128,128]{1,0:T(8,128)S(1)}, f32[128,128]{1,0:T(8,128)S(1)}, u32[]{:S(2)}, u32[]{:S(2)}) collective-permute-start(f32[128,128]{1,0:T(8,128)S(1)} %add.140), channel_id=1, source_target_pairs={{0,1},{16,17},{8,9},{24,25},{2,3},{18,19},{10,11},{26,27}} | collective-permute-start | bytes 196616 | tf_op jit(solution)/shard_map/ppermute | solution.py:195
  16.0 24.3 %collective-permute-done.14 = f32[128,128]{1,0:T(8,128)S(1)} collective-permute-done((f32[128,128]{1,0:T(8,128)S(1)}, f32[128,128]{1,0:T(8,128)S(1)}, u32[]{:S(2)}, u32[]{:S(2)}) %collective-permute-start.14) | collective-permute-done | bytes 65568 | tf_op jit(solution)/shard_map/ppermute | solution.py:195
  40.3 1.3 %collective-permute-start.15 = (f32[128,128]{1,0:T(8,128)S(1)}, f32[128,128]{1,0:T(8,128)S(1)}, u32[]{:S(2)}, u32[]{:S(2)}) collective-permute-start(f32[128,128]{1,0:T(8,128)S(1)} %add.141), channel_id=1, source_target_pairs={{0,4},{16,20},{8,12},{24,28},{2,6},{18,22},{10,14},{26,30},{1,5},{... | collective-permute-start | bytes 196616 | tf_op jit(solution)/shard_map/ppermute | solution.py:195
  41.6 0.9 %collective-permute-done.15 = f32[128,128]{1,0:T(8,128)S(1)} collective-permute-done((f32[128,128]{1,0:T(8,128)S(1)}, f32[128,128]{1,0:T(8,128)S(1)}, u32[]{:S(2)}, u32[]{:S(2)}) %collective-permute-start.15) | collective-permute-done | bytes 65568 | tf_op jit(solution)/shard_map/ppermute | solution.py:195
  42.5 1.6 %collective-permute-start.8 = (f32[512,128]{1,0:T(8,128)S(1)}, f32[512,128]{1,0:T(8,128)S(1)}, u32[]{:S(2)}, u32[]{:S(2)}) collective-permute-start(f32[512,128]{1,0:T(8,128)S(1)} %collective-permute-done.3), channel_id=1, source_target_pairs={{1,21},{4,24},{11,31},{14,2},{17,5},{20,8},{27,15},{30,18}} | collective-permute-start | bytes 786440 | tf_op jit(solution)/shard_map/ppermute | solution.py:174
  44.2 0.0 collective-permute-done.10
  44.2 5.1 %collective-permute-start.7 = (f32[512,128]{1,0:T(8,128)S(1)}, f32[512,128]{1,0:T(8,128)S(1)}, u32[]{:S(2)}, u32[]{:S(2)}) collective-permute-start(f32[512,128]{1,0:T(8,128)S(1)} %collective-permute-done.3), channel_id=1, source_target_pairs={{1,17},{4,20},{11,27},{14,30},{17,1},{20,4},{27,11},{30,14}} | collective-permute-start | bytes 786440 | tf_op jit(solution)/shard_map/ppermute | solution.py:174
  49.2 0.0 collective-permute-done.9
  49.3 1.3 %collective-permute-start.6 = (f32[512,128]{1,0:T(8,128)S(1)}, f32[512,128]{1,0:T(8,128)S(1)}, u32[]{:S(2)}, u32[]{:S(2)}) collective-permute-start(f32[512,128]{1,0:T(8,128)S(1)} %collective-permute-done.3), channel_id=1, source_target_pairs={{1,13},{4,16},{11,23},{14,26},{17,29},{20,0},{27,7},{30,10}} | collective-permute-start | bytes 786440 | tf_op jit(solution)/shard_map/ppermute | solution.py:174
  50.6 0.0 collective-permute-done
  50.6 1.3 %collective-permute-start.5 = (f32[512,128]{1,0:T(8,128)S(1)}, f32[512,128]{1,0:T(8,128)S(1)}, u32[]{:S(2)}, u32[]{:S(2)}) collective-permute-start(f32[512,128]{1,0:T(8,128)S(1)} %collective-permute-done.3), channel_id=1, source_target_pairs={{1,9},{4,12},{11,19},{14,22},{17,25},{20,28},{27,3},{30,6}} | collective-permute-start | bytes 786440 | tf_op jit(solution)/shard_map/ppermute | solution.py:174
  51.9 0.0 collective-permute-done.1
  51.9 1.3 %collective-permute-start.4 = (f32[512,128]{1,0:T(8,128)S(1)}, f32[512,128]{1,0:T(8,128)S(1)}, u32[]{:S(2)}, u32[]{:S(2)}) collective-permute-start(f32[512,128]{1,0:T(8,128)S(1)} %collective-permute-done.3), channel_id=1, source_target_pairs={{1,5},{4,8},{11,15},{14,18},{17,21},{20,24},{27,31},{30,2}} | collective-permute-start | bytes 786440 | tf_op jit(solution)/shard_map/ppermute | solution.py:174
  53.4 0.6 add.142.inverse_ref
  54.0 0.1 add.113
  54.1 0.0 collective-permute-done.8
  54.1 1.3 %collective-permute-start.2 = (f32[1024,128]{1,0:T(8,128)S(1)}, f32[1024,128]{1,0:T(8,128)S(1)}, u32[]{:S(2)}, u32[]{:S(2)}) collective-permute-start(f32[1024,128]{1,0:T(8,128)S(1)} %add.113), channel_id=1, source_target_pairs={{1,3},{6,7},{9,11},{14,15},{17,19},{22,23},{25,27},{30,31}} | collective-permute-start | bytes 1572872 | tf_op jit(solution)/shard_map/ppermute | solution.py:165
  55.4 0.0 collective-permute-done.7
  55.4 0.5 collective-permute-done.6
  55.9 2.8 %collective-permute-done.5 = f32[512,128]{1,0:T(8,128)S(1)} collective-permute-done((f32[512,128]{1,0:T(8,128)S(1)}, f32[512,128]{1,0:T(8,128)S(1)}, u32[]{:S(2)}, u32[]{:S(2)}) %collective-permute-start.5) | collective-permute-done | bytes 262176 | tf_op jit(solution)/shard_map/ppermute | solution.py:174
  58.7 0.0 collective-permute-done.4
  58.7 0.1 select_add_fusion
  58.9 0.1 select_add_fusion.1
  59.0 0.8 %pad_maximum_fusion.mirror_ref = f32[1024,128]{1,0:T(8,128)} fusion(f32[512,128]{1,0:T(8,128)S(1)} %select_add_fusion, f32[512,128]{1,0:T(8,128)S(1)} %select_add_fusion.1), kind=kLoop, calls=%fused_computation | loop fusion | flops 131072 | bytes 1048576 | tf_op jit(solution)/shard_map/concatenate | solution.py:181
  59.9 5.3 %collective-permute-done.2 = f32[1024,128]{1,0:T(8,128)S(1)} collective-permute-done((f32[1024,128]{1,0:T(8,128)S(1)}, f32[1024,128]{1,0:T(8,128)S(1)}, u32[]{:S(2)}, u32[]{:S(2)}) %collective-permute-start.2) | collective-permute-done | bytes 524320 | tf_op jit(solution)/shard_map/ppermute | solution.py:165
  65.2 1.9 %add_add_fusion.panel_ref = f32[1024,128]{1,0:T(8,128)} fusion(f32[1024,128]{1,0:T(8,128)S(1)} %add.113, f32[1024,128]{1,0:T(8,128)S(1)} %collective-permute-done.2, pred[]{:T(512)S(6)} %eq.66, f32[1024,1024]{1,0:T(8,128)} %matrix_ref.1), kind=kLoop, calls=%fused_computation.1 | loop fusion | flops 393216 | bytes 2097153 | tf_op jit(solution)/shard_map/add | solution.py:199
  67.1 11.8 %update.1 = f32[1024,1024]{1,0:T(8,128)} custom-call(s32[2]{0:T(128)} %pad_add_fusion.place_ref, f32[1024,1024]{1,0:T(8,128)} %matrix_ref.1, f32[1024,128]{1,0:T(8,128)} %add_add_fusion.panel_ref, f32[1024,128]{1,0:T(8,128)} %pad_maximum_fusion.mirror_ref, f32[128,128]{1,0:T(8,128)} %add.142.inverse_ref, f32[128,128]{1,0:T(8,128)} %get-tuple-element.8.lower_ref), custom_call_target="tpu_custom_call" | custom-call | flops 805306368 | bytes 8388608 | tf_op jit(solution)/shard_map/update/pallas_call | solution.py:113
  (3 shorter events, 0.0 us)
Async XLA Ops:
  1.0 10.4 %collective-permute-start.3 = (f32[512,128]{1,0:T(8,128)S(1)}, f32[512,128]{1,0:T(8,128)S(1)}, u32[]{:S(2)}, u32[]{:S(2)}) collective-permute-start(f32[512,128]{1,0:T(8,128)S(1)} %slice.11), channel_id=1, source_target_pairs={{0,4},{4,1},{8,14},{12,11},{16,20},{20,17},{24,30},{28,27}} | collective-permute-start | bytes 786440 | tf_op jit(solution)/shard_map/ppermute | solution.py:149
  4.1 46.4 %collective-permute-start = (f32[1024,128]{1,0:T(8,128)}, f32[1024,128]{1,0:T(8,128)S(1)}, u32[]{:S(2)}, u32[]{:S(2)}) collective-permute-start(f32[1024,128]{1,0:T(8,128)} %slice.10), channel_id=1, source_target_pairs={{0,1},{4,5},{8,9},{12,13},{16,17},{20,21},{24,25},{28,29}} | collective-permute-start | bytes 1572872 | tf_op jit(solution)/shard_map/ppermute | solution.py:157
  4.8 47.1 %collective-permute-start.1 = (f32[1024,128]{1,0:T(8,128)}, f32[1024,128]{1,0:T(8,128)S(1)}, u32[]{:S(2)}, u32[]{:S(2)}) collective-permute-start(f32[1024,128]{1,0:T(8,128)} %slice.10), channel_id=1, source_target_pairs={{0,2},{4,6},{8,10},{12,14},{16,18},{20,22},{24,26},{28,30}} | collective-permute-start | bytes 1572872 | tf_op jit(solution)/shard_map/ppermute | solution.py:160
  9.2 0.7 collective-permute-start.11
  10.7 3.3 %collective-permute-start.12 = (f32[128,128]{1,0:T(8,128)S(1)}, f32[128,128]{1,0:T(8,128)S(1)}, u32[]{:S(2)}, u32[]{:S(2)}) collective-permute-start(f32[128,128]{1,0:T(8,128)S(1)} %add.138), channel_id=1, source_target_pairs={{0,8},{16,24}} | collective-permute-start | bytes 196616 | tf_op jit(solution)/shard_map/ppermute | solution.py:195
  11.4 32.8 %collective-permute-start.10 = (f32[512,128]{1,0:T(8,128)S(1)}, f32[512,128]{1,0:T(8,128)S(1)}, u32[]{:S(2)}, u32[]{:S(2)}) collective-permute-start(f32[512,128]{1,0:T(8,128)S(1)} %collective-permute-done.3), channel_id=1, source_target_pairs={{1,29},{4,0},{11,7},{14,10},{17,13},{20,16},{27,23},{30,26}} | collective-permute-start | bytes 786440 | tf_op jit(solution)/shard_map/ppermute | solution.py:174
  12.7 36.6 %collective-permute-start.9 = (f32[512,128]{1,0:T(8,128)S(1)}, f32[512,128]{1,0:T(8,128)S(1)}, u32[]{:S(2)}, u32[]{:S(2)}) collective-permute-start(f32[512,128]{1,0:T(8,128)S(1)} %collective-permute-done.3), channel_id=1, source_target_pairs={{1,25},{4,28},{11,3},{14,6},{17,9},{20,12},{27,19},{30,22}} | collective-permute-start | bytes 786440 | tf_op jit(solution)/shard_map/ppermute | solution.py:174
  14.0 0.7 collective-permute-start.13
  14.7 25.6 %collective-permute-start.14 = (f32[128,128]{1,0:T(8,128)S(1)}, f32[128,128]{1,0:T(8,128)S(1)}, u32[]{:S(2)}, u32[]{:S(2)}) collective-permute-start(f32[128,128]{1,0:T(8,128)S(1)} %add.140), channel_id=1, source_target_pairs={{0,1},{16,17},{8,9},{24,25},{2,3},{18,19},{10,11},{26,27}} | collective-permute-start | bytes 196616 | tf_op jit(solution)/shard_map/ppermute | solution.py:195
  40.3 2.2 %collective-permute-start.15 = (f32[128,128]{1,0:T(8,128)S(1)}, f32[128,128]{1,0:T(8,128)S(1)}, u32[]{:S(2)}, u32[]{:S(2)}) collective-permute-start(f32[128,128]{1,0:T(8,128)S(1)} %add.141), channel_id=1, source_target_pairs={{0,4},{16,20},{8,12},{24,28},{2,6},{18,22},{10,14},{26,30},{1,5},{... | collective-permute-start | bytes 196616 | tf_op jit(solution)/shard_map/ppermute | solution.py:195
  42.5 11.5 %collective-permute-start.8 = (f32[512,128]{1,0:T(8,128)S(1)}, f32[512,128]{1,0:T(8,128)S(1)}, u32[]{:S(2)}, u32[]{:S(2)}) collective-permute-start(f32[512,128]{1,0:T(8,128)S(1)} %collective-permute-done.3), channel_id=1, source_target_pairs={{1,21},{4,24},{11,31},{14,2},{17,5},{20,8},{27,15},{30,18}} | collective-permute-start | bytes 786440 | tf_op jit(solution)/shard_map/ppermute | solution.py:174
  44.2 11.2 %collective-permute-start.7 = (f32[512,128]{1,0:T(8,128)S(1)}, f32[512,128]{1,0:T(8,128)S(1)}, u32[]{:S(2)}, u32[]{:S(2)}) collective-permute-start(f32[512,128]{1,0:T(8,128)S(1)} %collective-permute-done.3), channel_id=1, source_target_pairs={{1,17},{4,20},{11,27},{14,30},{17,1},{20,4},{27,11},{30,14}} | collective-permute-start | bytes 786440 | tf_op jit(solution)/shard_map/ppermute | solution.py:174
  49.3 6.7 %collective-permute-start.6 = (f32[512,128]{1,0:T(8,128)S(1)}, f32[512,128]{1,0:T(8,128)S(1)}, u32[]{:S(2)}, u32[]{:S(2)}) collective-permute-start(f32[512,128]{1,0:T(8,128)S(1)} %collective-permute-done.3), channel_id=1, source_target_pairs={{1,13},{4,16},{11,23},{14,26},{17,29},{20,0},{27,7},{30,10}} | collective-permute-start | bytes 786440 | tf_op jit(solution)/shard_map/ppermute | solution.py:174
  50.6 8.2 %collective-permute-start.5 = (f32[512,128]{1,0:T(8,128)S(1)}, f32[512,128]{1,0:T(8,128)S(1)}, u32[]{:S(2)}, u32[]{:S(2)}) collective-permute-start(f32[512,128]{1,0:T(8,128)S(1)} %collective-permute-done.3), channel_id=1, source_target_pairs={{1,9},{4,12},{11,19},{14,22},{17,25},{20,28},{27,3},{30,6}} | collective-permute-start | bytes 786440 | tf_op jit(solution)/shard_map/ppermute | solution.py:174
  51.9 6.8 %collective-permute-start.4 = (f32[512,128]{1,0:T(8,128)S(1)}, f32[512,128]{1,0:T(8,128)S(1)}, u32[]{:S(2)}, u32[]{:S(2)}) collective-permute-start(f32[512,128]{1,0:T(8,128)S(1)} %collective-permute-done.3), channel_id=1, source_target_pairs={{1,5},{4,8},{11,15},{14,18},{17,21},{20,24},{27,31},{30,2}} | collective-permute-start | bytes 786440 | tf_op jit(solution)/shard_map/ppermute | solution.py:174
  54.1 11.1 %collective-permute-start.2 = (f32[1024,128]{1,0:T(8,128)S(1)}, f32[1024,128]{1,0:T(8,128)S(1)}, u32[]{:S(2)}, u32[]{:S(2)}) collective-permute-start(f32[1024,128]{1,0:T(8,128)S(1)} %add.113), channel_id=1, source_target_pairs={{1,3},{6,7},{9,11},{14,15},{17,19},{22,23},{25,27},{30,31}} | collective-permute-start | bytes 1572872 | tf_op jit(solution)/shard_map/ppermute | solution.py:165

commit v2 on v0

v2 whole, which is shorter than its diff:
```python
import functools

import jax
import jax.numpy as jnp
from jax import lax
from jax.experimental import pallas as pl
from jax.experimental.pallas import tpu as pltpu
from jax.sharding import PartitionSpec as P

NB = 128
TILE = 256
AXES = ("row", "col")
HIGHEST = lax.Precision.HIGHEST
TRANS_B = (((1,), (1,)), ((), ()))


def factor_kernel(corner_ref, lower_ref, inverse_ref):
    rows = lax.broadcasted_iota(jnp.int32, (NB, NB), 0)
    cols = lax.broadcasted_iota(jnp.int32, (NB, NB), 1)
    corner = corner_ref[...]
    left = jnp.where(rows >= cols, corner, corner.T)
    right = jnp.where(rows == cols, 1.0, 0.0).astype(jnp.float32)
    lefts = [left[8 * b:8 * b + 8, :] for b in range(NB // 8)]
    rights = [right[8 * b:8 * b + 8, :] for b in range(NB // 8)]
    sub = lax.broadcasted_iota(jnp.int32, (8, NB), 0)
    for k in range(NB):
        b, o = divmod(k, 8)
        pivot = lefts[b][o:o + 1, k:k + 1]
        inv_pivot = 1.0 / jnp.broadcast_to(pivot, (1, NB))
        row_left = lefts[b][o:o + 1, :]
        row_right = rights[b][o:o + 1, :]
        for i in range(b, NB // 8):
            mult = jnp.broadcast_to(lefts[i][:, k:k + 1], (8, NB)) * inv_pivot
            if i == b:
                if o == 7:
                    continue
                mult = jnp.where(sub > o, mult, 0.0)
            lefts[i] = lefts[i] - mult * row_left
            rights[i] = rights[i] - mult * row_right
    upper = jnp.concatenate(lefts, axis=0)
    unit_inverse = jnp.concatenate(rights, axis=0)
    diagonal = jnp.sum(jnp.where(rows == cols, upper, 0.0), axis=1, keepdims=True)
    scale = 1.0 / jnp.sqrt(jnp.broadcast_to(diagonal, (NB, NB)))
    lower_ref[...] = jnp.where(rows >= cols, (upper * scale).T, 0.0)
    inverse_ref[...] = jnp.where(rows >= cols, unit_inverse * scale, 0.0)


def factor(corner):
    return pl.pallas_call(
        factor_kernel,
        out_shape=[jax.ShapeDtypeStruct((NB, NB), jnp.float32)] * 2,
        in_specs=[pl.BlockSpec(memory_space=pltpu.VMEM)],
        out_specs=[pl.BlockSpec(memory_space=pltpu.VMEM)] * 2,
        compiler_params=pltpu.CompilerParams(vmem_limit_bytes=4 * 1024 * 1024),
        cost_estimate=pl.CostEstimate(flops=4_000_000_000, bytes_accessed=40_000_000, transcendentals=0),
        name="factor",
    )(corner)


def split(value):
    high = value.astype(jnp.bfloat16)
    low = (value - high.astype(jnp.float32)).astype(jnp.bfloat16)
    return high, low


def update_kernel(plan, *refs):
    rows_here, cols_here, sources, arrivals, hops = plan
    n_panel, n_mirror = len(arrivals) + 1, hops
    lower_ref, inverse_ref, matrix_ref = refs[:3]
    panel_refs = refs[3:3 + n_panel - 1]
    mirror_refs = refs[3 + n_panel - 1:3 + n_panel - 1 + n_mirror]
    out_ref, old, new, panel, mirror, rhs, in_sems, panel_sems, mirror_sems, out_sems = refs[3 + n_panel - 1 + n_mirror:]
    row_index = lax.axis_index("row")
    col_index = lax.axis_index("col")
    height, width = old.shape
    col_blocks = width // NB
    each = mirror.shape[0] // sources
    tiles = height // TILE
    here = [pl.ds(i * TILE, TILE) for i in range(tiles)]

    pairs = rows_here // 2
    for q in range(sources):
        away = lax.rem(row_index // 2 - (col_index + q * cols_here) // 2 + pairs, pairs)
        for d in range(hops):
            @pl.when(away == d)
            def _(d=d, q=q):
                pltpu.make_async_copy(mirror_refs[d], mirror.at[pl.ds(q * each, each)], mirror_sems.at[q]).start()

    def fetch_panel(source, i):
        pltpu.make_async_copy(source, panel.at[here[i]], panel_sems.at[i]).start()

    for i in range(tiles):
        @pl.when(col_index == 0)
        def _(i=i):
            fetch_panel(matrix_ref.at[here[i], pl.ds(0, NB)], i)
        for n, columns in enumerate(arrivals):
            mine = functools.reduce(jnp.logical_or, [col_index == c for c in columns])

            @pl.when(mine)
            def _(i=i, n=n):
                fetch_panel(panel_refs[n].at[here[i]], i)
        pltpu.make_async_copy(matrix_ref.at[here[i]], old.at[here[i]], in_sems.at[i]).start()

    for q in range(sources):
        pltpu.make_async_copy(mirror_refs[0], mirror.at[pl.ds(q * each, each)], mirror_sems.at[q]).wait()
    for t in range(col_blocks):
        block = (t % sources) * each + (t // sources) * NB
        part = lax.dot_general(inverse_ref[...], mirror[pl.ds(block, NB), :], TRANS_B, precision=HIGHEST,
                               preferred_element_type=jnp.float32)
        high, low = split(part)
        at = pl.ds(t * NB, NB)
        rhs[pl.ds(0, NB), at] = high
        rhs[pl.ds(NB, NB), at] = high
        rhs[pl.ds(2 * NB, NB), at] = low

    for i in range(tiles):
        pltpu.make_async_copy(matrix_ref.at[here[i], pl.ds(0, NB)], panel.at[here[i]], panel_sems.at[i]).wait()
        tall = lax.dot_general(panel[here[i], :], inverse_ref[...], TRANS_B, precision=HIGHEST,
                               preferred_element_type=jnp.float32)
        high, low = split(tall)
        lhs = jnp.concatenate([high, low, high], axis=1)
        product = jnp.dot(lhs, rhs[...], preferred_element_type=jnp.float32)
        pltpu.make_async_copy(matrix_ref.at[here[i]], old.at[here[i]], in_sems.at[i]).wait()
        for s in range(TILE // NB):
            row = (i * (TILE // NB) + s) * rows_here + row_index
            down = pl.ds(i * TILE + s * NB, NB)
            for t in range(col_blocks):
                across = pl.ds(t * NB, NB)
                col = t * cols_here + col_index
                before = old[down, across]
                after = before - product[s * NB:(s + 1) * NB, t * NB:(t + 1) * NB]
                value = jnp.where((row >= col) & (col >= 1), after, before)
                if t == 0:
                    block = jnp.where(row == 0, lower_ref[...], tall[s * NB:(s + 1) * NB, :])
                    value = jnp.where(col == 0, block, value)
                new[down, across] = value
        pltpu.make_async_copy(new.at[here[i]], out_ref.at[here[i]], out_sems.at[i]).start()
    for i in range(tiles):
        pltpu.make_async_copy(new.at[here[i]], out_ref.at[here[i]], out_sems.at[i]).wait()


def update(lower, inverse, matrix, panels, mirrors, plan):
    height, width = matrix.shape
    sources = plan[2]
    tiles = height // TILE
    vmem = pl.BlockSpec(memory_space=pltpu.VMEM)
    anywhere = pl.BlockSpec(memory_space=pl.ANY)
    return pl.pallas_call(
        functools.partial(update_kernel, plan),
        out_shape=jax.ShapeDtypeStruct(matrix.shape, jnp.float32),
        in_specs=[vmem, vmem, pl.BlockSpec(memory_space=pltpu.HBM)] + [anywhere] * (len(panels) + len(mirrors)),
        out_specs=anywhere,
        scratch_shapes=[
            pltpu.VMEM((height, width), jnp.float32),
            pltpu.VMEM((height, width), jnp.float32),
            pltpu.VMEM((height, NB), jnp.float32),
            pltpu.VMEM((width, NB), jnp.float32),
            pltpu.VMEM((3 * NB, width), jnp.bfloat16),
            pltpu.SemaphoreType.DMA((tiles,)),
            pltpu.SemaphoreType.DMA((tiles,)),
            pltpu.SemaphoreType.DMA((sources,)),
            pltpu.SemaphoreType.DMA((tiles,)),
        ],
        compiler_params=pltpu.CompilerParams(vmem_limit_bytes=16 * 1024 * 1024),
        cost_estimate=pl.CostEstimate(flops=2 * height * width * NB * 3,
                                      bytes_accessed=8 * height * width, transcendentals=0),
        name="update",
    )(lower, inverse, matrix, *panels, *mirrors)


def body(matrix):
    rows_here = lax.axis_size("row")
    cols_here = lax.axis_size("col")
    row_index = lax.axis_index("row")
    col_index = lax.axis_index("col")
    col_blocks = matrix.shape[1] // NB
    sources = rows_here // cols_here
    every_row = range(rows_here)

    def at(r, c):
        return r * cols_here + c

    corner = jnp.where((row_index == 0) & (col_index == 0), matrix[:NB, :NB], 0.0)
    holders = [(0, 0)]
    offsets = [(0, 1 << b) for b in range(cols_here.bit_length() - 1)]
    offsets += [(1 << b, 0) for b in reversed(range(rows_here.bit_length() - 1))]
    for dr, dc in offsets:
        corner = corner + lax.ppermute(corner, AXES, [(at(r, c), at(r + dr, c + dc)) for r, c in holders])
        holders = holders + [(r + dr, c + dc) for r, c in holders]

    column = matrix[:, :NB]
    first = column[:NB * (col_blocks // sources)]

    hop = lax.ppermute(first, AXES, [(at(r, 0), at(r ^ 1, r % cols_here)) for r in every_row])
    hop += lax.ppermute(first, AXES, [(at(r, 0), at(r, r % cols_here)) for r in every_row if r % cols_here])
    hop = jnp.where((col_index == 0) & (row_index % cols_here == 0), first, hop)
    mirrors = [hop]
    pairs = rows_here // 2
    for d in range(1, pairs):
        mirrors.append(lax.ppermute(hop, AXES, [
            (at(r, c), at((r + 2 * d) % rows_here, c))
            for r in every_row for c in range(cols_here) if r // 2 in [(c + q * cols_here) // 2 for q in range(sources)]]))

    panels, arrivals = [], []
    merged = column
    step = 1
    while step < cols_here:
        base = range(step)
        near = lax.ppermute(merged, "col", [(h, h + step) for h in base])
        panels.append(near)
        arrivals.append([h + step for h in base])
        if 2 * step < cols_here:
            far = lax.ppermute(merged, "col", [(h, h + 2 * step) for h in base])
            relay = [(at(r, h + (step if r % 2 == 0 else 2 * step)), at(r, h + 3 * step))
                     for r in every_row for h in base]
            last = lax.ppermute(near + far, AXES, relay)
            panels += [far, last]
            arrivals += [[h + 2 * step for h in base], [h + 3 * step for h in base]]
        step *= 4
        if step < cols_here:
            merged = jnp.where(col_index == 0, column, 0.0) + sum(panels)

    lower, inverse = factor(corner)
    return update(lower, inverse, matrix, panels, mirrors, (rows_here, cols_here, sources, arrivals, pairs))


def solution(mesh):
    return jax.shard_map(
        body,
        mesh=mesh,
        in_specs=(P("row", "col"),),
        out_specs=P("row", "col"),
        check_vma=False,
    )
```

time: 206 us -> 66.9 us (0.32)
  the two profiles are of different devices: /device:TPU:6 before, /device:TPU:18 now
where the time goes in v2:
time: 66.9 us; the launch traced here: 66.4 us
  starting transfers between devices  22.8 us (34%)
  waiting for transfers between devices  20.5 us (31%)
  Pallas kernels  18 us (27%)
  other arithmetic  2.8 us (4%)
  local copies, waits for them, and re-layouts  2.05 us (3%)
    ppermute x5, waiting for transfers between devices, body(): lax.ppermute(corner, AXES, [(at(r, c), at(r + dr, c + dc)) for r, c in ho...  20.5 us
    pallas_call x1, Pallas kernels, factor(): pl.pallas_call(factor_kernel, out_shape=[jax.ShapeDtypeStruct((NB, NB), j...  10.8 us
    ppermute x3, starting transfers between devices, body(): lax.ppermute(hop, AXES, [(at(r, c), at((r + 2 * d) % rows_here, c)) for r...  9.86 us
    pallas_call x1, Pallas kernels, update(): pl.pallas_call(functools.partial(update_kernel, plan), out_shape=jax.Shap...  7.12 us
    ppermute x5, starting transfers between devices, body(): lax.ppermute(corner, AXES, [(at(r, c), at(r + dr, c + dc)) for r, c in ho...  5.19 us
    ppermute x1, starting transfers between devices, body(): last = lax.ppermute(near + far, AXES, relay)  3.81 us
  transfers between devices with their start and end apart: 13, of which 2 were waited for; matrix products, arithmetic and copies ran while one was open for 6% of the time, Pallas kernels for 16%

profile of v2, /device:TPU:18, one launch (start us, length us, event | category | flops | bytes accessed | tf_op | source)
XLA Modules:
  0.0 66.4 jit_solution(10403409865224269431)
XLA Ops:
  0.0 1.1 %slice.11 = f32[1024,128]{1,0:T(8,128)S(1)} slice(f32[1024,1024]{1,0:T(8,128)} %refs_2_.1), slice={[0:1024], [0:128]} | slice | bytes 1048576 | tf_op jit(solution)/shard_map/slice | solution.py:191
  1.1 0.7 %collective-permute-start.6 = (f32[1024,128]{1,0:T(8,128)S(1)}, f32[1024,128]{1,0:T(8,128)S(1)}, u32[]{:S(2)}, u32[]{:S(2)}) collective-permute-start(f32[1024,128]{1,0:T(8,128)S(1)} %slice.11), channel_id=1, source_target_pairs={{0,2},{4,6},{8,10},{12,14},{16,18},{20,22},{24,26},{28,30}} | collective-permute-start | bytes 1572872 | tf_op jit(solution)/shard_map/ppermute | solution.py:213
  1.8 1.3 %collective-permute-start.5 = (f32[1024,128]{1,0:T(8,128)S(1)}, f32[1024,128]{1,0:T(8,128)S(1)}, u32[]{:S(2)}, u32[]{:S(2)}) collective-permute-start(f32[1024,128]{1,0:T(8,128)S(1)} %slice.11), channel_id=1, source_target_pairs={{0,1},{4,5},{8,9},{12,13},{16,17},{20,21},{24,25},{28,29}} | collective-permute-start | bytes 1572872 | tf_op jit(solution)/shard_map/ppermute | solution.py:209
  3.1 0.8 %slice_select_fusion = f32[128,128]{1,0:T(8,128)S(1)} fusion(f32[1024,1024]{1,0:T(8,128)} %refs_2_.1, pred[]{:T(512)S(6)} %and.13), kind=kLoop, calls=%fused_computation.1 | loop fusion | flops 16384 | bytes 131073 | tf_op jit(solution)/shard_map/jit(_where)/select_n | solution.py:183
  3.9 0.7 collective-permute-start
  4.6 1.0 %slice.12 = f32[512,128]{1,0:T(8,128)S(1)} slice(f32[1024,1024]{1,0:T(8,128)} %refs_2_.1), slice={[0:512], [0:128]} | slice | bytes 524288 | tf_op jit(solution)/shard_map/slice | solution.py:192
  5.6 0.7 %collective-permute-start.9 = (f32[512,128]{1,0:T(8,128)S(1)}, f32[512,128]{1,0:T(8,128)S(1)}, u32[]{:S(2)}, u32[]{:S(2)}) collective-permute-start(f32[512,128]{1,0:T(8,128)S(1)} %slice.12), channel_id=1, source_target_pairs={{4,5},{8,10},{12,15},{20,21},{24,26},{28,31}} | collective-permute-start | bytes 786440 | tf_op jit(solution)/shard_map/ppermute | solution.py:195
  6.3 1.3 %collective-permute-start.8 = (f32[512,128]{1,0:T(8,128)S(1)}, f32[512,128]{1,0:T(8,128)S(1)}, u32[]{:S(2)}, u32[]{:S(2)}) collective-permute-start(f32[512,128]{1,0:T(8,128)S(1)} %slice.12), channel_id=1, source_target_pairs={{0,4},{4,1},{8,14},{12,11},{16,20},{20,17},{24,30},{28,27}} | collective-permute-start | bytes 786440 | tf_op jit(solution)/shard_map/ppermute | solution.py:194
  7.6 0.0 collective-permute-done
  7.6 0.9 %fusion = f32[128,128]{1,0:T(8,128)S(1)} fusion(f32[128,128]{1,0:T(8,128)S(1)} %collective-permute-done, f32[1024,1024]{1,0:T(8,128)} %refs_2_.1, pred[]{:T(512)S(6)} %and.13), kind=kLoop, calls=%fused_computation.2 | loop fusion | flops 32768 | bytes 196609 | tf_op jit(solution)/shard_map/add | solution.py:188
  8.4 0.7 collective-permute-start.1
  9.1 0.0 collective-permute-done.1
  9.1 1.3 %collective-permute-start.2 = (f32[128,128]{1,0:T(8,128)S(1)}, f32[128,128]{1,0:T(8,128)S(1)}, u32[]{:S(2)}, u32[]{:S(2)}) collective-permute-start(f32[128,128]{1,0:T(8,128)S(1)} %add.26), channel_id=1, source_target_pairs={{0,16},{1,17},{2,18},{3,19}} | collective-permute-start | bytes 196616 | tf_op jit(solution)/shard_map/ppermute | solution.py:188
  10.4 18.6 %collective-permute-done.2 = f32[128,128]{1,0:T(8,128)S(1)} collective-permute-done((f32[128,128]{1,0:T(8,128)S(1)}, f32[128,128]{1,0:T(8,128)S(1)}, u32[]{:S(2)}, u32[]{:S(2)}) %collective-permute-start.2) | collective-permute-done | bytes 65568 | tf_op jit(solution)/shard_map/ppermute | solution.py:188
  29.0 1.3 %collective-permute-start.3 = (f32[128,128]{1,0:T(8,128)S(1)}, f32[128,128]{1,0:T(8,128)S(1)}, u32[]{:S(2)}, u32[]{:S(2)}) collective-permute-start(f32[128,128]{1,0:T(8,128)S(1)} %add.27), channel_id=1, source_target_pairs={{0,8},{1,9},{2,10},{3,11},{16,24},{17,25},{18,26},{19,27}} | collective-permute-start | bytes 196616 | tf_op jit(solution)/shard_map/ppermute | solution.py:188
  30.4 1.9 %collective-permute-done.3 = f32[128,128]{1,0:T(8,128)S(1)} collective-permute-done((f32[128,128]{1,0:T(8,128)S(1)}, f32[128,128]{1,0:T(8,128)S(1)}, u32[]{:S(2)}, u32[]{:S(2)}) %collective-permute-start.3) | collective-permute-done | bytes 65568 | tf_op jit(solution)/shard_map/ppermute | solution.py:188
  32.2 1.3 %collective-permute-start.4 = (f32[128,128]{1,0:T(8,128)S(1)}, f32[128,128]{1,0:T(8,128)S(1)}, u32[]{:S(2)}, u32[]{:S(2)}) collective-permute-start(f32[128,128]{1,0:T(8,128)S(1)} %add.28), channel_id=1, source_target_pairs={{0,4},{1,5},{2,6},{3,7},{16,20},{17,21},{18,22},{19,23},{8,12},{9,... | collective-permute-start | bytes 196616 | tf_op jit(solution)/shard_map/ppermute | solution.py:188
  33.5 0.0 collective-permute-done.6.refs_4_
  33.6 0.0 collective-permute-done.5.refs_3_
  33.6 0.1 add.30
  33.6 3.8 %collective-permute-start.7 = (f32[1024,128]{1,0:T(8,128)S(1)}, f32[1024,128]{1,0:T(8,128)S(1)}, u32[]{:S(2)}, u32[]{:S(2)}) collective-permute-start(f32[1024,128]{1,0:T(8,128)S(1)} %add.30), channel_id=1, source_target_pairs={{1,3},{6,7},{9,11},{14,15},{17,19},{22,23},{25,27},{30,31}} | collective-permute-start | bytes 1572872 | tf_op jit(solution)/shard_map/ppermute | solution.py:216
  37.5 0.0 collective-permute-done.9
  37.5 0.0 collective-permute-done.8
  37.5 1.0 %add_select_fusion.refs_6_ = f32[512,128]{1,0:T(8,128)S(1)} fusion(f32[512,128]{1,0:T(8,128)S(1)} %collective-permute-done.8, f32[512,128]{1,0:T(8,128)S(1)} %collective-permute-done.9, pred[]{:T(512)S(6)} %and.15, f32[1024,1024]{1,0:T(8,128)} %refs_2_.1), kind=kLoop, calls=%fused_computation | loop fusion | flops 131072 | bytes 1048577 | tf_op jit(solution)/shard_map/jit(_where)/select_n | solution.py:196
  38.5 2.4 %collective-permute-start.12 = (f32[512,128]{1,0:T(8,128)S(1)}, f32[512,128]{1,0:T(8,128)S(1)}, u32[]{:S(2)}, u32[]{:S(2)}) collective-permute-start(f32[512,128]{1,0:T(8,128)S(1)} %add_select_fusion.refs_6_), channel_id=1, source_target_pairs={{0,24},{1,25},{4,28},{5,29},{10,2},{11,3},{14,6},{15,7},{16,8},{17... | collective-permute-start | bytes 786440 | tf_op jit(solution)/shard_map/ppermute | solution.py:200
  40.9 6.2 %collective-permute-start.11 = (f32[512,128]{1,0:T(8,128)S(1)}, f32[512,128]{1,0:T(8,128)S(1)}, u32[]{:S(2)}, u32[]{:S(2)}) collective-permute-start(f32[512,128]{1,0:T(8,128)S(1)} %add_select_fusion.refs_6_), channel_id=1, source_target_pairs={{0,16},{1,17},{4,20},{5,21},{10,26},{11,27},{14,30},{15,31},{16,0}... | collective-permute-start | bytes 786440 | tf_op jit(solution)/shard_map/ppermute | solution.py:200
  47.0 1.3 %collective-permute-start.10 = (f32[512,128]{1,0:T(8,128)S(1)}, f32[512,128]{1,0:T(8,128)S(1)}, u32[]{:S(2)}, u32[]{:S(2)}) collective-permute-start(f32[512,128]{1,0:T(8,128)S(1)} %add_select_fusion.refs_6_), channel_id=1, source_target_pairs={{0,8},{1,9},{4,12},{5,13},{10,18},{11,19},{14,22},{15,23},{16,24},... | collective-permute-start | bytes 786440 | tf_op jit(solution)/shard_map/ppermute | solution.py:200
  48.4 0.0 collective-permute-done.4
  48.4 0.0 copy-start
  48.4 10.8 %factor.1 = (f32[128,128]{1,0:T(8,128)S(1)}, f32[128,128]{1,0:T(8,128)S(1)}) custom-call(f32[128,128]{1,0:T(8,128)S(1)} %add.29.corner_ref), custom_call_target="tpu_custom_call" | custom-call | flops 4000000000 | bytes 40000000 | tf_op jit(solution)/shard_map/factor/pallas_call | solution.py:49
  59.2 0.0 collective-permute-done.12.refs_9_
  59.2 0.0 collective-permute-done.11.refs_8_
  59.3 0.0 collective-permute-done.10.refs_7_
  59.3 0.0 collective-permute-done.7.refs_5_
  59.3 0.0 copy-done
  59.3 7.1 %update.1 = f32[1024,1024]{1,0:T(8,128)} custom-call(f32[128,128]{1,0:T(8,128)S(1)} %get-tuple-element.7.refs_0_, f32[128,128]{1,0:T(8,128)S(1)} %get-tuple-element.8.refs_1_, f32[1024,1024]{1,0:T(8,128)S(1)} %copy-done, f32[1024,128]{1,0:T(8,128)S(1)} %collective-permute-done.5.refs_3_, f32[1024,128]{1,0:T(8,128)S(1)} %collective-permute-done.6.refs_4_, ...), custom_call_target="tpu_custom_call" | custom-call | flops 805306368 | bytes 8388608 | tf_op jit(solution)/shard_map/update/pallas_call | solution.py:148
  (4 shorter events, 0.0 us)
Async XLA Ops:
  1.1 32.5 %collective-permute-start.6 = (f32[1024,128]{1,0:T(8,128)S(1)}, f32[1024,128]{1,0:T(8,128)S(1)}, u32[]{:S(2)}, u32[]{:S(2)}) collective-permute-start(f32[1024,128]{1,0:T(8,128)S(1)} %slice.11), channel_id=1, source_target_pairs={{0,2},{4,6},{8,10},{12,14},{16,18},{20,22},{24,26},{28,30}} | collective-permute-start | bytes 1572872 | tf_op jit(solution)/shard_map/ppermute | solution.py:213
  1.8 31.8 %collective-permute-start.5 = (f32[1024,128]{1,0:T(8,128)S(1)}, f32[1024,128]{1,0:T(8,128)S(1)}, u32[]{:S(2)}, u32[]{:S(2)}) collective-permute-start(f32[1024,128]{1,0:T(8,128)S(1)} %slice.11), channel_id=1, source_target_pairs={{0,1},{4,5},{8,9},{12,13},{16,17},{20,21},{24,25},{28,29}} | collective-permute-start | bytes 1572872 | tf_op jit(solution)/shard_map/ppermute | solution.py:209
  3.9 3.6 %collective-permute-start = (f32[128,128]{1,0:T(8,128)S(1)}, f32[128,128]{1,0:T(8,128)S(1)}, u32[]{:S(2)}, u32[]{:S(2)}) collective-permute-start(f32[128,128]{1,0:T(8,128)S(1)} %slice_select_fusion), channel_id=1, source_target_pairs={{0,1}} | collective-permute-start | bytes 196616 | tf_op jit(solution)/shard_map/ppermute | solution.py:188
  5.6 31.9 %collective-permute-start.9 = (f32[512,128]{1,0:T(8,128)S(1)}, f32[512,128]{1,0:T(8,128)S(1)}, u32[]{:S(2)}, u32[]{:S(2)}) collective-permute-start(f32[512,128]{1,0:T(8,128)S(1)} %slice.12), channel_id=1, source_target_pairs={{4,5},{8,10},{12,15},{20,21},{24,26},{28,31}} | collective-permute-start | bytes 786440 | tf_op jit(solution)/shard_map/ppermute | solution.py:195
  6.3 31.2 %collective-permute-start.8 = (f32[512,128]{1,0:T(8,128)S(1)}, f32[512,128]{1,0:T(8,128)S(1)}, u32[]{:S(2)}, u32[]{:S(2)}) collective-permute-start(f32[512,128]{1,0:T(8,128)S(1)} %slice.12), channel_id=1, source_target_pairs={{0,4},{4,1},{8,14},{12,11},{16,20},{20,17},{24,30},{28,27}} | collective-permute-start | bytes 786440 | tf_op jit(solution)/shard_map/ppermute | solution.py:194
  8.4 0.7 %collective-permute-start.1 = (f32[128,128]{1,0:T(8,128)S(1)}, f32[128,128]{1,0:T(8,128)S(1)}, u32[]{:S(2)}, u32[]{:S(2)}) collective-permute-start(f32[128,128]{1,0:T(8,128)S(1)} %fusion), channel_id=1, source_target_pairs={{0,2},{1,3}} | collective-permute-start | bytes 196616 | tf_op jit(solution)/shard_map/ppermute | solution.py:188
  9.1 19.9 %collective-permute-start.2 = (f32[128,128]{1,0:T(8,128)S(1)}, f32[128,128]{1,0:T(8,128)S(1)}, u32[]{:S(2)}, u32[]{:S(2)}) collective-permute-start(f32[128,128]{1,0:T(8,128)S(1)} %add.26), channel_id=1, source_target_pairs={{0,16},{1,17},{2,18},{3,19}} | collective-permute-start | bytes 196616 | tf_op jit(solution)/shard_map/ppermute | solution.py:188
  29.0 3.2 %collective-permute-start.3 = (f32[128,128]{1,0:T(8,128)S(1)}, f32[128,128]{1,0:T(8,128)S(1)}, u32[]{:S(2)}, u32[]{:S(2)}) collective-permute-start(f32[128,128]{1,0:T(8,128)S(1)} %add.27), channel_id=1, source_target_pairs={{0,8},{1,9},{2,10},{3,11},{16,24},{17,25},{18,26},{19,27}} | collective-permute-start | bytes 196616 | tf_op jit(solution)/shard_map/ppermute | solution.py:188
  32.2 16.1 %collective-permute-start.4 = (f32[128,128]{1,0:T(8,128)S(1)}, f32[128,128]{1,0:T(8,128)S(1)}, u32[]{:S(2)}, u32[]{:S(2)}) collective-permute-start(f32[128,128]{1,0:T(8,128)S(1)} %add.28), channel_id=1, source_target_pairs={{0,4},{1,5},{2,6},{3,7},{16,20},{17,21},{18,22},{19,23},{8,12},{9,... | collective-permute-start | bytes 196616 | tf_op jit(solution)/shard_map/ppermute | solution.py:188
  33.6 25.6 %collective-permute-start.7 = (f32[1024,128]{1,0:T(8,128)S(1)}, f32[1024,128]{1,0:T(8,128)S(1)}, u32[]{:S(2)}, u32[]{:S(2)}) collective-permute-start(f32[1024,128]{1,0:T(8,128)S(1)} %add.30), channel_id=1, source_target_pairs={{1,3},{6,7},{9,11},{14,15},{17,19},{22,23},{25,27},{30,31}} | collective-permute-start | bytes 1572872 | tf_op jit(solution)/shard_map/ppermute | solution.py:216
  38.5 20.8 %collective-permute-start.12 = (f32[512,128]{1,0:T(8,128)S(1)}, f32[512,128]{1,0:T(8,128)S(1)}, u32[]{:S(2)}, u32[]{:S(2)}) collective-permute-start(f32[512,128]{1,0:T(8,128)S(1)} %add_select_fusion.refs_6_), channel_id=1, source_target_pairs={{0,24},{1,25},{4,28},{5,29},{10,2},{11,3},{14,6},{15,7},{16,8},{17... | collective-permute-start | bytes 786440 | tf_op jit(solution)/shard_map/ppermute | solution.py:200
  40.9 18.4 %collective-permute-start.11 = (f32[512,128]{1,0:T(8,128)S(1)}, f32[512,128]{1,0:T(8,128)S(1)}, u32[]{:S(2)}, u32[]{:S(2)}) collective-permute-start(f32[512,128]{1,0:T(8,128)S(1)} %add_select_fusion.refs_6_), channel_id=1, source_target_pairs={{0,16},{1,17},{4,20},{5,21},{10,26},{11,27},{14,30},{15,31},{16,0}... | collective-permute-start | bytes 786440 | tf_op jit(solution)/shard_map/ppermute | solution.py:200
  47.0 12.2 %collective-permute-start.10 = (f32[512,128]{1,0:T(8,128)S(1)}, f32[512,128]{1,0:T(8,128)S(1)}, u32[]{:S(2)}, u32[]{:S(2)}) collective-permute-start(f32[512,128]{1,0:T(8,128)S(1)} %add_select_fusion.refs_6_), channel_id=1, source_target_pairs={{0,8},{1,9},{4,12},{5,13},{10,18},{11,19},{14,22},{15,23},{16,24},... | collective-permute-start | bytes 786440 | tf_op jit(solution)/shard_map/ppermute | solution.py:200
  48.4 10.9 %copy-start = (f32[1024,1024]{1,0:T(8,128)S(1)}, f32[1024,1024]{1,0:T(8,128)}, u32[]{:S(2)}) copy-start(f32[1024,1024]{1,0:T(8,128)} %refs_2_.1) | copy-start | bytes 12582916

commit v3 on v2

--- a/solution.py
+++ b/solution.py
@@ -181,15 +181,16 @@
         return r * cols_here + c
 
     corner = jnp.where((row_index == 0) & (col_index == 0), matrix[:NB, :NB], 0.0)
+    column = matrix[:, :NB]
+    first = column[:NB * (col_blocks // sources)]
     holders = [(0, 0)]
     offsets = [(0, 1 << b) for b in range(cols_here.bit_length() - 1)]
     offsets += [(1 << b, 0) for b in reversed(range(rows_here.bit_length() - 1))]
     for dr, dc in offsets:
         corner = corner + lax.ppermute(corner, AXES, [(at(r, c), at(r + dr, c + dc)) for r, c in holders])
         holders = holders + [(r + dr, c + dc) for r, c in holders]
-
-    column = matrix[:, :NB]
-    first = column[:NB * (col_blocks // sources)]
+        if len(holders) == cols_here:
+            corner, column, first = lax.optimization_barrier((corner, column, first))
 
     hop = lax.ppermute(first, AXES, [(at(r, 0), at(r ^ 1, r % cols_here)) for r in every_row])
     hop += lax.ppermute(first, AXES, [(at(r, 0), at(r, r % cols_here)) for r in every_row if r % cols_here])

time: 66.9 us -> 60.9 us (0.910)
  the two profiles are of different devices: /device:TPU:18 before, /device:TPU:0 now
where the time goes in v3:
time: 60.9 us; the launch traced here: 60.4 us
  starting transfers between devices  28.9 us (47%)
  Pallas kernels  17.3 us (28%)
  waiting for transfers between devices  10.1 us (17%)
  local copies, waits for them, and re-layouts  2.05 us (3%)
  other arithmetic  1.83 us (3%)
    pallas_call x1, Pallas kernels, factor(): pl.pallas_call(factor_kernel, out_shape=[jax.ShapeDtypeStruct((NB, NB), j...  10.8 us
    ppermute x3, starting transfers between devices, body(): lax.ppermute(hop, AXES, [(at(r, c), at((r + 2 * d) % rows_here, c)) for r...  10.5 us
    ppermute x5, starting transfers between devices, body(): lax.ppermute(corner, AXES, [(at(r, c), at(r + dr, c + dc)) for r, c in ho...  10 us
    ppermute x5, waiting for transfers between devices, body(): lax.ppermute(corner, AXES, [(at(r, c), at(r + dr, c + dc)) for r, c in ho...  6.9 us
    pallas_call x1, Pallas kernels, update(): pl.pallas_call(functools.partial(update_kernel, plan), out_shape=jax.Shap...  6.48 us
    ppermute x1, starting transfers between devices, body(): far = lax.ppermute(merged, 'col', [(h, h + 2 * step) for h in base])  4.42 us
    ppermute x3, waiting for transfers between devices, body(): lax.ppermute(hop, AXES, [(at(r, c), at((r + 2 * d) % rows_here, c)) for r...  3.18 us
    ppermute x1, starting transfers between devices, body(): near = lax.ppermute(merged, 'col', [(h, h + step) for h in base])  1.32 us
  transfers between devices with their start and end apart: 13, of which 6 were waited for; matrix products, arithmetic and copies ran while one was open for 4% of the time, Pallas kernels for 18%

profile of v3, /device:TPU:0, one launch (start us, length us, event | category | flops | bytes accessed | tf_op | source)
XLA Modules:
  0.0 60.4 jit_solution(18174305413358402682)
XLA Ops:
  0.0 0.8 %slice_select_fusion = f32[128,128]{1,0:T(8,128)S(1)} fusion(f32[1024,1024]{1,0:T(8,128)} %refs_2_.1, pred[]{:T(512)S(6)} %and.13), kind=kLoop, calls=%fused_computation.1 | loop fusion | flops 16384 | bytes 131073 | tf_op jit(solution)/shard_map/jit(_where)/select_n | solution.py:183
  0.8 4.8 %collective-permute-start = (f32[128,128]{1,0:T(8,128)S(1)}, f32[128,128]{1,0:T(8,128)S(1)}, u32[]{:S(2)}, u32[]{:S(2)}) collective-permute-start(f32[128,128]{1,0:T(8,128)S(1)} %slice_select_fusion), channel_id=1, source_target_pairs={{0,1}} | collective-permute-start | bytes 196616 | tf_op jit(solution)/shard_map/ppermute | solution.py:190
  5.7 1.9 %collective-permute-done = f32[128,128]{1,0:T(8,128)S(1)} collective-permute-done((f32[128,128]{1,0:T(8,128)S(1)}, f32[128,128]{1,0:T(8,128)S(1)}, u32[]{:S(2)}, u32[]{:S(2)}) %collective-permute-start) | collective-permute-done | bytes 65568 | tf_op jit(solution)/shard_map/ppermute | solution.py:190
  7.6 0.9 %fusion = f32[128,128]{1,0:T(8,128)S(1)} fusion(f32[128,128]{1,0:T(8,128)S(1)} %collective-permute-done, f32[1024,1024]{1,0:T(8,128)} %refs_2_.1, pred[]{:T(512)S(6)} %and.13), kind=kLoop, calls=%fused_computation.2 | loop fusion | flops 32768 | bytes 196609 | tf_op jit(solution)/shard_map/add | solution.py:190
  8.4 1.3 %collective-permute-start.1 = (f32[128,128]{1,0:T(8,128)S(1)}, f32[128,128]{1,0:T(8,128)S(1)}, u32[]{:S(2)}, u32[]{:S(2)}) collective-permute-start(f32[128,128]{1,0:T(8,128)S(1)} %fusion), channel_id=1, source_target_pairs={{0,2},{1,3}} | collective-permute-start | bytes 196616 | tf_op jit(solution)/shard_map/ppermute | solution.py:190
  9.7 1.0 %slice.12 = f32[512,128]{1,0:T(8,128)S(1)} slice(f32[1024,1024]{1,0:T(8,128)} %refs_2_.1), slice={[0:512], [0:128]} | slice | bytes 524288 | tf_op jit(solution)/shard_map/slice | solution.py:185
  10.7 1.1 %slice.11 = f32[1024,128]{1,0:T(8,128)S(1)} slice(f32[1024,1024]{1,0:T(8,128)} %refs_2_.1), slice={[0:1024], [0:128]} | slice | bytes 1048576 | tf_op jit(solution)/shard_map/slice | solution.py:184
  11.8 0.4 collective-permute-done.1
  12.2 4.4 %collective-permute-start.6 = (f32[1024,128]{1,0:T(8,128)S(1)}, f32[1024,128]{1,0:T(8,128)S(1)}, u32[]{:S(2)}, u32[]{:S(2)}) collective-permute-start(f32[1024,128]{1,0:T(8,128)S(1)} %slice.11), channel_id=1, source_target_pairs={{0,2},{4,6},{8,10},{12,14},{16,18},{20,22},{24,26},{28,30}} | collective-permute-start | bytes 1572872 | tf_op jit(solution)/shard_map/ppermute | solution.py:214
  16.6 1.3 %collective-permute-start.5 = (f32[1024,128]{1,0:T(8,128)S(1)}, f32[1024,128]{1,0:T(8,128)S(1)}, u32[]{:S(2)}, u32[]{:S(2)}) collective-permute-start(f32[1024,128]{1,0:T(8,128)S(1)} %slice.11), channel_id=1, source_target_pairs={{0,1},{4,5},{8,9},{12,13},{16,17},{20,21},{24,25},{28,29}} | collective-permute-start | bytes 1572872 | tf_op jit(solution)/shard_map/ppermute | solution.py:210
  17.9 0.7 %collective-permute-start.9 = (f32[512,128]{1,0:T(8,128)S(1)}, f32[512,128]{1,0:T(8,128)S(1)}, u32[]{:S(2)}, u32[]{:S(2)}) collective-permute-start(f32[512,128]{1,0:T(8,128)S(1)} %slice.12), channel_id=1, source_target_pairs={{4,5},{8,10},{12,15},{20,21},{24,26},{28,31}} | collective-permute-start | bytes 786440 | tf_op jit(solution)/shard_map/ppermute | solution.py:196
  18.6 1.3 %collective-permute-start.8 = (f32[512,128]{1,0:T(8,128)S(1)}, f32[512,128]{1,0:T(8,128)S(1)}, u32[]{:S(2)}, u32[]{:S(2)}) collective-permute-start(f32[512,128]{1,0:T(8,128)S(1)} %slice.12), channel_id=1, source_target_pairs={{0,4},{4,1},{8,14},{12,11},{16,20},{20,17},{24,30},{28,27}} | collective-permute-start | bytes 786440 | tf_op jit(solution)/shard_map/ppermute | solution.py:195
  19.9 1.3 %collective-permute-start.2 = (f32[128,128]{1,0:T(8,128)S(1)}, f32[128,128]{1,0:T(8,128)S(1)}, u32[]{:S(2)}, u32[]{:S(2)}) collective-permute-start(f32[128,128]{1,0:T(8,128)S(1)} %add.26), channel_id=1, source_target_pairs={{0,16},{1,17},{2,18},{3,19}} | collective-permute-start | bytes 196616 | tf_op jit(solution)/shard_map/ppermute | solution.py:190
  21.2 1.9 %collective-permute-done.2 = f32[128,128]{1,0:T(8,128)S(1)} collective-permute-done((f32[128,128]{1,0:T(8,128)S(1)}, f32[128,128]{1,0:T(8,128)S(1)}, u32[]{:S(2)}, u32[]{:S(2)}) %collective-permute-start.2) | collective-permute-done | bytes 65568 | tf_op jit(solution)/shard_map/ppermute | solution.py:190
  23.1 1.3 %collective-permute-start.3 = (f32[128,128]{1,0:T(8,128)S(1)}, f32[128,128]{1,0:T(8,128)S(1)}, u32[]{:S(2)}, u32[]{:S(2)}) collective-permute-start(f32[128,128]{1,0:T(8,128)S(1)} %add.27), channel_id=1, source_target_pairs={{0,8},{1,9},{2,10},{3,11},{16,24},{17,25},{18,26},{19,27}} | collective-permute-start | bytes 196616 | tf_op jit(solution)/shard_map/ppermute | solution.py:190
  24.4 1.9 %collective-permute-done.3 = f32[128,128]{1,0:T(8,128)S(1)} collective-permute-done((f32[128,128]{1,0:T(8,128)S(1)}, f32[128,128]{1,0:T(8,128)S(1)}, u32[]{:S(2)}, u32[]{:S(2)}) %collective-permute-start.3) | collective-permute-done | bytes 65568 | tf_op jit(solution)/shard_map/ppermute | solution.py:190
  26.3 1.3 %collective-permute-start.4 = (f32[128,128]{1,0:T(8,128)S(1)}, f32[128,128]{1,0:T(8,128)S(1)}, u32[]{:S(2)}, u32[]{:S(2)}) collective-permute-start(f32[128,128]{1,0:T(8,128)S(1)} %add.28), channel_id=1, source_target_pairs={{0,4},{1,5},{2,6},{3,7},{16,20},{17,21},{18,22},{19,23},{8,12},{9,... | collective-permute-start | bytes 196616 | tf_op jit(solution)/shard_map/ppermute | solution.py:190
  27.6 0.9 %collective-permute-done.4 = f32[128,128]{1,0:T(8,128)S(1)} collective-permute-done((f32[128,128]{1,0:T(8,128)S(1)}, f32[128,128]{1,0:T(8,128)S(1)}, u32[]{:S(2)}, u32[]{:S(2)}) %collective-permute-start.4) | collective-permute-done | bytes 65568 | tf_op jit(solution)/shard_map/ppermute | solution.py:190
  28.5 0.0 collective-permute-done.6.refs_4_
  28.5 0.0 collective-permute-done.5.refs_3_
  28.5 0.1 add.30
  28.6 0.7 %collective-permute-start.7 = (f32[1024,128]{1,0:T(8,128)S(1)}, f32[1024,128]{1,0:T(8,128)S(1)}, u32[]{:S(2)}, u32[]{:S(2)}) collective-permute-start(f32[1024,128]{1,0:T(8,128)S(1)} %add.30), channel_id=1, source_target_pairs={{1,3},{6,7},{9,11},{14,15},{17,19},{22,23},{25,27},{30,31}} | collective-permute-start | bytes 1572872 | tf_op jit(solution)/shard_map/ppermute | solution.py:217
  29.3 0.0 collective-permute-done.9
  29.3 0.0 collective-permute-done.8
  29.4 0.0 copy-start
  29.4 7.2 %collective-permute-start.12 = (f32[512,128]{1,0:T(8,128)S(1)}, f32[512,128]{1,0:T(8,128)S(1)}, u32[]{:S(2)}, u32[]{:S(2)}) collective-permute-start(f32[512,128]{1,0:T(8,128)S(1)} %add_select_fusion.refs_6_), channel_id=1, source_target_pairs={{0,24},{1,25},{4,28},{5,29},{10,2},{11,3},{14,6},{15,7},{16,8},{17... | collective-permute-start | bytes 786440 | tf_op jit(solution)/shard_map/ppermute | solution.py:201
  36.6 1.9 %collective-permute-start.11 = (f32[512,128]{1,0:T(8,128)S(1)}, f32[512,128]{1,0:T(8,128)S(1)}, u32[]{:S(2)}, u32[]{:S(2)}) collective-permute-start(f32[512,128]{1,0:T(8,128)S(1)} %add_select_fusion.refs_6_), channel_id=1, source_target_pairs={{0,16},{1,17},{4,20},{5,21},{10,26},{11,27},{14,30},{15,31},{16,0}... | collective-permute-start | bytes 786440 | tf_op jit(solution)/shard_map/ppermute | solution.py:201
  38.6 1.3 %collective-permute-start.10 = (f32[512,128]{1,0:T(8,128)S(1)}, f32[512,128]{1,0:T(8,128)S(1)}, u32[]{:S(2)}, u32[]{:S(2)}) collective-permute-start(f32[512,128]{1,0:T(8,128)S(1)} %add_select_fusion.refs_6_), channel_id=1, source_target_pairs={{0,8},{1,9},{4,12},{5,13},{10,18},{11,19},{14,22},{15,23},{16,24},... | collective-permute-start | bytes 786440 | tf_op jit(solution)/shard_map/ppermute | solution.py:201
  39.9 10.8 %factor.1 = (f32[128,128]{1,0:T(8,128)S(1)}, f32[128,128]{1,0:T(8,128)S(1)}) custom-call(f32[128,128]{1,0:T(8,128)S(1)} %add.29.corner_ref), custom_call_target="tpu_custom_call" | custom-call | flops 4000000000 | bytes 40000000 | tf_op jit(solution)/shard_map/factor/pallas_call | solution.py:49
  50.7 0.0 collective-permute-done.12.refs_9_
  50.7 0.0 collective-permute-done.11.refs_8_
  50.7 3.2 %collective-permute-done.10.refs_7_ = f32[512,128]{1,0:T(8,128)S(1)} collective-permute-done((f32[512,128]{1,0:T(8,128)S(1)}, f32[512,128]{1,0:T(8,128)S(1)}, u32[]{:S(2)}, u32[]{:S(2)}) %collective-permute-start.10) | collective-permute-done | bytes 262176 | tf_op jit(solution)/shard_map/ppermute | solution.py:201
  53.9 0.0 collective-permute-done.7.refs_5_
  53.9 0.0 copy-done
  53.9 6.5 %update.1 = f32[1024,1024]{1,0:T(8,128)} custom-call(f32[128,128]{1,0:T(8,128)S(1)} %get-tuple-element.11.refs_0_, f32[128,128]{1,0:T(8,128)S(1)} %get-tuple-element.12.refs_1_, f32[1024,1024]{1,0:T(8,128)S(1)} %copy-done, f32[1024,128]{1,0:T(8,128)S(1)} %collective-permute-done.5.refs_3_, f32[1024,128]{1,0:T(8,128)S(1)} %collective-permute-done.6.refs_4_, ...), custom_call_target="tpu_custom_call" | custom-call | flops 805306368 | bytes 8388608 | tf_op jit(solution)/shard_map/update/pallas_call | solution.py:148
  (5 shorter events, 0.1 us)
Async XLA Ops:
  0.8 6.7 %collective-permute-start = (f32[128,128]{1,0:T(8,128)S(1)}, f32[128,128]{1,0:T(8,128)S(1)}, u32[]{:S(2)}, u32[]{:S(2)}) collective-permute-start(f32[128,128]{1,0:T(8,128)S(1)} %slice_select_fusion), channel_id=1, source_target_pairs={{0,1}} | collective-permute-start | bytes 196616 | tf_op jit(solution)/shard_map/ppermute | solution.py:190
  8.4 3.7 %collective-permute-start.1 = (f32[128,128]{1,0:T(8,128)S(1)}, f32[128,128]{1,0:T(8,128)S(1)}, u32[]{:S(2)}, u32[]{:S(2)}) collective-permute-start(f32[128,128]{1,0:T(8,128)S(1)} %fusion), channel_id=1, source_target_pairs={{0,2},{1,3}} | collective-permute-start | bytes 196616 | tf_op jit(solution)/shard_map/ppermute | solution.py:190
  12.2 16.4 %collective-permute-start.6 = (f32[1024,128]{1,0:T(8,128)S(1)}, f32[1024,128]{1,0:T(8,128)S(1)}, u32[]{:S(2)}, u32[]{:S(2)}) collective-permute-start(f32[1024,128]{1,0:T(8,128)S(1)} %slice.11), channel_id=1, source_target_pairs={{0,2},{4,6},{8,10},{12,14},{16,18},{20,22},{24,26},{28,30}} | collective-permute-start | bytes 1572872 | tf_op jit(solution)/shard_map/ppermute | solution.py:214
  16.6 11.9 %collective-permute-start.5 = (f32[1024,128]{1,0:T(8,128)S(1)}, f32[1024,128]{1,0:T(8,128)S(1)}, u32[]{:S(2)}, u32[]{:S(2)}) collective-permute-start(f32[1024,128]{1,0:T(8,128)S(1)} %slice.11), channel_id=1, source_target_pairs={{0,1},{4,5},{8,9},{12,13},{16,17},{20,21},{24,25},{28,29}} | collective-permute-start | bytes 1572872 | tf_op jit(solution)/shard_map/ppermute | solution.py:210
  17.9 11.4 %collective-permute-start.9 = (f32[512,128]{1,0:T(8,128)S(1)}, f32[512,128]{1,0:T(8,128)S(1)}, u32[]{:S(2)}, u32[]{:S(2)}) collective-permute-start(f32[512,128]{1,0:T(8,128)S(1)} %slice.12), channel_id=1, source_target_pairs={{4,5},{8,10},{12,15},{20,21},{24,26},{28,31}} | collective-permute-start | bytes 786440 | tf_op jit(solution)/shard_map/ppermute | solution.py:196
  18.6 10.7 %collective-permute-start.8 = (f32[512,128]{1,0:T(8,128)S(1)}, f32[512,128]{1,0:T(8,128)S(1)}, u32[]{:S(2)}, u32[]{:S(2)}) collective-permute-start(f32[512,128]{1,0:T(8,128)S(1)} %slice.12), channel_id=1, source_target_pairs={{0,4},{4,1},{8,14},{12,11},{16,20},{20,17},{24,30},{28,27}} | collective-permute-start | bytes 786440 | tf_op jit(solution)/shard_map/ppermute | solution.py:195
  19.9 3.2 %collective-permute-start.2 = (f32[128,128]{1,0:T(8,128)S(1)}, f32[128,128]{1,0:T(8,128)S(1)}, u32[]{:S(2)}, u32[]{:S(2)}) collective-permute-start(f32[128,128]{1,0:T(8,128)S(1)} %add.26), channel_id=1, source_target_pairs={{0,16},{1,17},{2,18},{3,19}} | collective-permute-start | bytes 196616 | tf_op jit(solution)/shard_map/ppermute | solution.py:190
  23.1 3.2 %collective-permute-start.3 = (f32[128,128]{1,0:T(8,128)S(1)}, f32[128,128]{1,0:T(8,128)S(1)}, u32[]{:S(2)}, u32[]{:S(2)}) collective-permute-start(f32[128,128]{1,0:T(8,128)S(1)} %add.27), channel_id=1, source_target_pairs={{0,8},{1,9},{2,10},{3,11},{16,24},{17,25},{18,26},{19,27}} | collective-permute-start | bytes 196616 | tf_op jit(solution)/shard_map/ppermute | solution.py:190
  26.3 2.2 %collective-permute-start.4 = (f32[128,128]{1,0:T(8,128)S(1)}, f32[128,128]{1,0:T(8,128)S(1)}, u32[]{:S(2)}, u32[]{:S(2)}) collective-permute-start(f32[128,128]{1,0:T(8,128)S(1)} %add.28), channel_id=1, source_target_pairs={{0,4},{1,5},{2,6},{3,7},{16,20},{17,21},{18,22},{19,23},{8,12},{9,... | collective-permute-start | bytes 196616 | tf_op jit(solution)/shard_map/ppermute | solution.py:190
  28.6 25.3 %collective-permute-start.7 = (f32[1024,128]{1,0:T(8,128)S(1)}, f32[1024,128]{1,0:T(8,128)S(1)}, u32[]{:S(2)}, u32[]{:S(2)}) collective-permute-start(f32[1024,128]{1,0:T(8,128)S(1)} %add.30), channel_id=1, source_target_pairs={{1,3},{6,7},{9,11},{14,15},{17,19},{22,23},{25,27},{30,31}} | collective-permute-start | bytes 1572872 | tf_op jit(solution)/shard_map/ppermute | solution.py:217
  29.4 24.5 %copy-start = (f32[1024,1024]{1,0:T(8,128)S(1)}, f32[1024,1024]{1,0:T(8,128)}, u32[]{:S(2)}) copy-start(f32[1024,1024]{1,0:T(8,128)} %refs_2_.1) | copy-start | bytes 12582916
  29.4 21.3 %collective-permute-start.12 = (f32[512,128]{1,0:T(8,128)S(1)}, f32[512,128]{1,0:T(8,128)S(1)}, u32[]{:S(2)}, u32[]{:S(2)}) collective-permute-start(f32[512,128]{1,0:T(8,128)S(1)} %add_select_fusion.refs_6_), channel_id=1, source_target_pairs={{0,24},{1,25},{4,28},{5,29},{10,2},{11,3},{14,6},{15,7},{16,8},{17... | collective-permute-start | bytes 786440 | tf_op jit(solution)/shard_map/ppermute | solution.py:201
  36.6 14.1 %collective-permute-start.11 = (f32[512,128]{1,0:T(8,128)S(1)}, f32[512,128]{1,0:T(8,128)S(1)}, u32[]{:S(2)}, u32[]{:S(2)}) collective-permute-start(f32[512,128]{1,0:T(8,128)S(1)} %add_select_fusion.refs_6_), channel_id=1, source_target_pairs={{0,16},{1,17},{4,20},{5,21},{10,26},{11,27},{14,30},{15,31},{16,0}... | collective-permute-start | bytes 786440 | tf_op jit(solution)/shard_map/ppermute | solution.py:201
  38.6 15.4 %collective-permute-start.10 = (f32[512,128]{1,0:T(8,128)S(1)}, f32[512,128]{1,0:T(8,128)S(1)}, u32[]{:S(2)}, u32[]{:S(2)}) collective-permute-start(f32[512,128]{1,0:T(8,128)S(1)} %add_select_fusion.refs_6_), channel_id=1, source_target_pairs={{0,8},{1,9},{4,12},{5,13},{10,18},{11,19},{14,22},{15,23},{16,24},... | collective-permute-start | bytes 786440 | tf_op jit(solution)/shard_map/ppermute | solution.py:201

commit v4 on v2

--- a/solution.py
+++ b/solution.py
@@ -64,12 +64,12 @@
 
 
 def update_kernel(plan, *refs):
-    rows_here, cols_here, sources, arrivals, hops = plan
-    n_panel, n_mirror = len(arrivals) + 1, hops
+    rows_here, cols_here, sources, arrivals = plan
+    n_panel = len(arrivals)
     lower_ref, inverse_ref, matrix_ref = refs[:3]
-    panel_refs = refs[3:3 + n_panel - 1]
-    mirror_refs = refs[3 + n_panel - 1:3 + n_panel - 1 + n_mirror]
-    out_ref, old, new, panel, mirror, rhs, in_sems, panel_sems, mirror_sems, out_sems = refs[3 + n_panel - 1 + n_mirror:]
+    panel_refs = refs[3:3 + n_panel]
+    mirror_refs = refs[3 + n_panel:3 + n_panel + sources]
+    out_ref, old, new, panel, mirror, rhs, in_sems, panel_sems, mirror_sems, out_sems = refs[3 + n_panel + sources:]
     row_index = lax.axis_index("row")
     col_index = lax.axis_index("col")
     height, width = old.shape
@@ -78,10 +78,9 @@
     tiles = height // TILE
     here = [pl.ds(i * TILE, TILE) for i in range(tiles)]
 
-    pairs = rows_here // 2
     for q in range(sources):
-        away = lax.rem(row_index // 2 - (col_index + q * cols_here) // 2 + pairs, pairs)
-        for d in range(hops):
+        away = lax.rem(q - row_index // cols_here + sources, sources)
+        for d in range(sources):
             @pl.when(away == d)
             def _(d=d, q=q):
                 pltpu.make_async_copy(mirror_refs[d], mirror.at[pl.ds(q * each, each)], mirror_sems.at[q]).start()
@@ -180,26 +179,31 @@
     def at(r, c):
         return r * cols_here + c
 
-    corner = jnp.where((row_index == 0) & (col_index == 0), matrix[:NB, :NB], 0.0)
-    holders = [(0, 0)]
-    offsets = [(0, 1 << b) for b in range(cols_here.bit_length() - 1)]
-    offsets += [(1 << b, 0) for b in reversed(range(rows_here.bit_length() - 1))]
-    for dr, dc in offsets:
-        corner = corner + lax.ppermute(corner, AXES, [(at(r, c), at(r + dr, c + dc)) for r, c in holders])
-        holders = holders + [(r + dr, c + dc) for r, c in holders]
-
     column = matrix[:, :NB]
     first = column[:NB * (col_blocks // sources)]
+    last = cols_here - 1
+    corner = jnp.where((row_index == 0) & (col_index == 0), matrix[:NB, :NB], 0.0)
+    corner = corner + lax.ppermute(corner, AXES, [(at(0, 0), at(0, last))])
+    corner, column, first = lax.optimization_barrier((corner, column, first))
+    holders = [(0, last)]
+    hops = [(1 << b, 0) for b in reversed(range(rows_here.bit_length() - 1))]
+    hops += [(0, 1 << b) for b in range(cols_here.bit_length() - 1)]
+    for dr, dc in hops:
+        pairs = [(at(r, c), at(r + dr, c - dc)) for r, c in holders if (r + dr, c - dc) != (0, 0)]
+        corner = corner + lax.ppermute(corner, AXES, pairs)
+        holders = holders + [(r + dr, c - dc) for r, c in holders]
 
     hop = lax.ppermute(first, AXES, [(at(r, 0), at(r ^ 1, r % cols_here)) for r in every_row])
     hop += lax.ppermute(first, AXES, [(at(r, 0), at(r, r % cols_here)) for r in every_row if r % cols_here])
     hop = jnp.where((col_index == 0) & (row_index % cols_here == 0), first, hop)
+    own = [(c + q * cols_here, c) for c in range(cols_here) for q in range(sources)]
+    own = own + [(r ^ 1, c) for r, c in own]
+    for bit in (1 << b for b in range(1, cols_here.bit_length() - 1)):
+        hop = hop + lax.ppermute(hop, AXES, [(at(r, c), at(r ^ bit, c)) for r, c in own])
+        own = own + [(r ^ bit, c) for r, c in own]
     mirrors = [hop]
-    pairs = rows_here // 2
-    for d in range(1, pairs):
-        mirrors.append(lax.ppermute(hop, AXES, [
-            (at(r, c), at((r + 2 * d) % rows_here, c))
-            for r in every_row for c in range(cols_here) if r // 2 in [(c + q * cols_here) // 2 for q in range(sources)]]))
+    for q in range(1, sources):
+        mirrors.append(lax.ppermute(hop, "row", [((r + q * cols_here) % rows_here, r) for r in every_row]))
 
     panels, arrivals = [], []
     merged = column
@@ -213,15 +217,14 @@
             far = lax.ppermute(merged, "col", [(h, h + 2 * step) for h in base])
             relay = [(at(r, h + (step if r % 2 == 0 else 2 * step)), at(r, h + 3 * step))
                      for r in every_row for h in base]
-            last = lax.ppermute(near + far, AXES, relay)
-            panels += [far, last]
+            panels += [far, lax.ppermute(near + far, AXES, relay)]
             arrivals += [[h + 2 * step for h in base], [h + 3 * step for h in base]]
         step *= 4
         if step < cols_here:
             merged = jnp.where(col_index == 0, column, 0.0) + sum(panels)
 
     lower, inverse = factor(corner)
-    return update(lower, inverse, matrix, panels, mirrors, (rows_here, cols_here, sources, arrivals, pairs))
+    return update(lower, inverse, matrix, panels, mirrors, (rows_here, cols_here, sources, arrivals))
 
 
 def solution(mesh):

time: 66.9 us -> 59.3 us (0.89)
  the two profiles are of different devices: /device:TPU:18 before, /device:TPU:8 now
where the time goes in v4:
time: 59.3 us; the launch traced here: 58.8 us
  waiting for transfers between devices  20.7 us (35%)
  Pallas kernels  17.3 us (29%)
  starting transfers between devices  16.6 us (28%)
  local copies, waits for them, and re-layouts  2.05 us (3%)
  other arithmetic  1.88 us (3%)
    pallas_call x1, Pallas kernels, factor(): pl.pallas_call(factor_kernel, out_shape=[jax.ShapeDtypeStruct((NB, NB), j...  10.8 us
    ppermute x5, waiting for transfers between devices, body(): corner = corner + lax.ppermute(corner, AXES, pairs)  10.2 us
    pallas_call x1, Pallas kernels, update(): pl.pallas_call(functools.partial(update_kernel, plan), out_shape=jax.Shap...  6.49 us
    ppermute x1, waiting for transfers between devices, body(): far = lax.ppermute(merged, 'col', [(h, h + 2 * step) for h in base])  6.06 us
    ppermute x1, waiting for transfers between devices, body(): lax.ppermute(first, AXES, [(at(r, 0), at(r ^ 1, r % cols_here)) for r in...  4.42 us
    ppermute x5, starting transfers between devices, body(): corner = corner + lax.ppermute(corner, AXES, pairs)  3.95 us
    ppermute x1, starting transfers between devices, body(): lax.ppermute(first, AXES, [(at(r, 0), at(r, r % cols_here)) for r in ever...  3.43 us
    ppermute x1, starting transfers between devices, body(): lax.ppermute(hop, 'row', [((r + q * cols_here) % rows_here, r) for r in e...  2.65 us
  transfers between devices with their start and end apart: 13, of which 3 were waited for; matrix products, arithmetic and copies ran while one was open for 4% of the time, Pallas kernels for 18%

profile of v4, /device:TPU:8, one launch (start us, length us, event | category | flops | bytes accessed | tf_op | source)
XLA Modules:
  0.0 58.8 jit_solution(9510474297768523883)
XLA Ops:
  0.0 0.8 %slice_select_fusion = f32[128,128]{1,0:T(8,128)S(1)} fusion(f32[1024,1024]{1,0:T(8,128)} %refs_2_.1, pred[]{:T(512)S(6)} %and.13), kind=kLoop, calls=%fused_computation.1 | loop fusion | flops 16384 | bytes 131073 | tf_op jit(solution)/shard_map/jit(_where)/select_n | solution.py:185
  0.8 0.7 %collective-permute-start = (f32[128,128]{1,0:T(8,128)S(1)}, f32[128,128]{1,0:T(8,128)S(1)}, u32[]{:S(2)}, u32[]{:S(2)}) collective-permute-start(f32[128,128]{1,0:T(8,128)S(1)} %slice_select_fusion), channel_id=1, source_target_pairs={{0,3}} | collective-permute-start | bytes 196616 | tf_op jit(solution)/shard_map/ppermute | solution.py:186
  1.5 1.0 %slice.12 = f32[512,128]{1,0:T(8,128)S(1)} slice(f32[1024,1024]{1,0:T(8,128)} %refs_2_.1), slice={[0:512], [0:128]} | slice | bytes 524288 | tf_op jit(solution)/shard_map/slice | solution.py:183
  2.5 1.1 %slice.11 = f32[1024,128]{1,0:T(8,128)S(1)} slice(f32[1024,1024]{1,0:T(8,128)} %refs_2_.1), slice={[0:1024], [0:128]} | slice | bytes 1048576 | tf_op jit(solution)/shard_map/slice | solution.py:182
  3.6 0.0 collective-permute-done
  3.6 0.9 %fusion = f32[128,128]{1,0:T(8,128)S(1)} fusion(f32[128,128]{1,0:T(8,128)S(1)} %collective-permute-done, f32[1024,1024]{1,0:T(8,128)} %refs_2_.1, pred[]{:T(512)S(6)} %and.13), kind=kLoop, calls=%fused_computation.2 | loop fusion | flops 32768 | bytes 196609 | tf_op jit(solution)/shard_map/add | solution.py:186
  4.4 3.4 %collective-permute-start.10 = (f32[512,128]{1,0:T(8,128)S(1)}, f32[512,128]{1,0:T(8,128)S(1)}, u32[]{:S(2)}, u32[]{:S(2)}) collective-permute-start(f32[512,128]{1,0:T(8,128)S(1)} %slice.12), channel_id=1, source_target_pairs={{4,5},{8,10},{12,15},{20,21},{24,26},{28,31}} | collective-permute-start | bytes 786440 | tf_op jit(solution)/shard_map/ppermute | solution.py:197
  7.9 1.3 %collective-permute-start.9 = (f32[512,128]{1,0:T(8,128)S(1)}, f32[512,128]{1,0:T(8,128)S(1)}, u32[]{:S(2)}, u32[]{:S(2)}) collective-permute-start(f32[512,128]{1,0:T(8,128)S(1)} %slice.12), channel_id=1, source_target_pairs={{0,4},{4,1},{8,14},{12,11},{16,20},{20,17},{24,30},{28,27}} | collective-permute-start | bytes 786440 | tf_op jit(solution)/shard_map/ppermute | solution.py:196
  9.2 1.3 %collective-permute-start.7 = (f32[1024,128]{1,0:T(8,128)S(1)}, f32[1024,128]{1,0:T(8,128)S(1)}, u32[]{:S(2)}, u32[]{:S(2)}) collective-permute-start(f32[1024,128]{1,0:T(8,128)S(1)} %slice.11), channel_id=1, source_target_pairs={{0,2},{4,6},{8,10},{12,14},{16,18},{20,22},{24,26},{28,30}} | collective-permute-start | bytes 1572872 | tf_op jit(solution)/shard_map/ppermute | solution.py:217
  10.5 1.3 %collective-permute-start.6 = (f32[1024,128]{1,0:T(8,128)S(1)}, f32[1024,128]{1,0:T(8,128)S(1)}, u32[]{:S(2)}, u32[]{:S(2)}) collective-permute-start(f32[1024,128]{1,0:T(8,128)S(1)} %slice.11), channel_id=1, source_target_pairs={{0,1},{4,5},{8,9},{12,13},{16,17},{20,21},{24,25},{28,29}} | collective-permute-start | bytes 1572872 | tf_op jit(solution)/shard_map/ppermute | solution.py:213
  11.8 0.7 %collective-permute-start.1 = (f32[128,128]{1,0:T(8,128)S(1)}, f32[128,128]{1,0:T(8,128)S(1)}, u32[]{:S(2)}, u32[]{:S(2)}) collective-permute-start(f32[128,128]{1,0:T(8,128)S(1)} %fusion), channel_id=1, source_target_pairs={{3,19}} | collective-permute-start | bytes 196616 | tf_op jit(solution)/shard_map/ppermute | solution.py:193
  12.5 0.0 collective-permute-done.1
  12.6 0.7 %collective-permute-start.2 = (f32[128,128]{1,0:T(8,128)S(1)}, f32[128,128]{1,0:T(8,128)S(1)}, u32[]{:S(2)}, u32[]{:S(2)}) collective-permute-start(f32[128,128]{1,0:T(8,128)S(1)} %add.32), channel_id=1, source_target_pairs={{3,11},{19,27}} | collective-permute-start | bytes 196616 | tf_op jit(solution)/shard_map/ppermute | solution.py:193
  13.2 0.0 collective-permute-done.10
  13.2 4.4 %collective-permute-done.9 = f32[512,128]{1,0:T(8,128)S(1)} collective-permute-done((f32[512,128]{1,0:T(8,128)S(1)}, f32[512,128]{1,0:T(8,128)S(1)}, u32[]{:S(2)}, u32[]{:S(2)}) %collective-permute-start.9) | collective-permute-done | bytes 262176 | tf_op jit(solution)/shard_map/ppermute | solution.py:196
  17.7 1.3 %collective-permute-start.11 = (f32[512,128]{1,0:T(8,128)S(1)}, f32[512,128]{1,0:T(8,128)S(1)}, u32[]{:S(2)}, u32[]{:S(2)}) collective-permute-start(f32[512,128]{1,0:T(8,128)S(1)} %add_select_fusion), channel_id=1, source_target_pairs={{0,8},{16,24},{5,13},{21,29},{10,2},{26,18},{15,7},{31,23},{4,12},... | collective-permute-start | bytes 786440 | tf_op jit(solution)/shard_map/ppermute | solution.py:202
  19.0 0.0 collective-permute-done.2
  19.0 0.7 %collective-permute-start.3 = (f32[128,128]{1,0:T(8,128)S(1)}, f32[128,128]{1,0:T(8,128)S(1)}, u32[]{:S(2)}, u32[]{:S(2)}) collective-permute-start(f32[128,128]{1,0:T(8,128)S(1)} %add.33), channel_id=1, source_target_pairs={{3,7},{19,23},{11,15},{27,31}} | collective-permute-start | bytes 196616 | tf_op jit(solution)/shard_map/ppermute | solution.py:193
  19.7 6.1 %collective-permute-done.7.refs_4_ = f32[1024,128]{1,0:T(8,128)S(1)} collective-permute-done((f32[1024,128]{1,0:T(8,128)S(1)}, f32[1024,128]{1,0:T(8,128)S(1)}, u32[]{:S(2)}, u32[]{:S(2)}) %collective-permute-start.7) | collective-permute-done | bytes 524320 | tf_op jit(solution)/shard_map/ppermute | solution.py:217
  25.8 0.0 collective-permute-done.6.refs_3_
  25.8 0.1 add.37
  25.8 0.7 %collective-permute-start.8 = (f32[1024,128]{1,0:T(8,128)S(1)}, f32[1024,128]{1,0:T(8,128)S(1)}, u32[]{:S(2)}, u32[]{:S(2)}) collective-permute-start(f32[1024,128]{1,0:T(8,128)S(1)} %add.37), channel_id=1, source_target_pairs={{1,3},{6,7},{9,11},{14,15},{17,19},{22,23},{25,27},{30,31}} | collective-permute-start | bytes 1572872 | tf_op jit(solution)/shard_map/ppermute | solution.py:220
  26.5 0.0 collective-permute-done.3
  26.6 0.7 %collective-permute-start.4 = (f32[128,128]{1,0:T(8,128)S(1)}, f32[128,128]{1,0:T(8,128)S(1)}, u32[]{:S(2)}, u32[]{:S(2)}) collective-permute-start(f32[128,128]{1,0:T(8,128)S(1)} %add.34), channel_id=1, source_target_pairs={{3,2},{19,18},{11,10},{27,26},{7,6},{23,22},{15,14},{31,30}} | collective-permute-start | bytes 196616 | tf_op jit(solution)/shard_map/ppermute | solution.py:193
  27.2 0.0 collective-permute-done.4
  27.3 1.3 %collective-permute-start.5 = (f32[128,128]{1,0:T(8,128)S(1)}, f32[128,128]{1,0:T(8,128)S(1)}, u32[]{:S(2)}, u32[]{:S(2)}) collective-permute-start(f32[128,128]{1,0:T(8,128)S(1)} %add.35), channel_id=1, source_target_pairs={{3,1},{19,17},{11,9},{27,25},{7,5},{23,21},{15,13},{31,29},{18,16}... | collective-permute-start | bytes 196616 | tf_op jit(solution)/shard_map/ppermute | solution.py:193
  28.6 10.2 %collective-permute-done.5 = f32[128,128]{1,0:T(8,128)S(1)} collective-permute-done((f32[128,128]{1,0:T(8,128)S(1)}, f32[128,128]{1,0:T(8,128)S(1)}, u32[]{:S(2)}, u32[]{:S(2)}) %collective-permute-start.5) | collective-permute-done | bytes 65568 | tf_op jit(solution)/shard_map/ppermute | solution.py:193
  38.8 0.0 collective-permute-done.11
  38.8 0.0 copy-start
  38.8 2.7 %collective-permute-start.12 = (f32[512,128]{1,0:T(8,128)S(1)}, f32[512,128]{1,0:T(8,128)S(1)}, u32[]{:S(2)}, u32[]{:S(2)}) collective-permute-start(f32[512,128]{1,0:T(8,128)S(1)} %add.40.refs_6_), channel_id=1, source_target_pairs={{16,0},{20,4},{24,8},{28,12},{0,16},{4,20},{8,24},{12,28},{17,1},{... | collective-permute-start | bytes 786440 | tf_op jit(solution)/shard_map/ppermute | solution.py:206
  41.5 10.8 %factor.1 = (f32[128,128]{1,0:T(8,128)S(1)}, f32[128,128]{1,0:T(8,128)S(1)}) custom-call(f32[128,128]{1,0:T(8,128)S(1)} %add.36.corner_ref), custom_call_target="tpu_custom_call" | custom-call | flops 4000000000 | bytes 40000000 | tf_op jit(solution)/shard_map/factor/pallas_call | solution.py:49
  52.3 0.0 collective-permute-done.12.refs_7_
  52.3 0.0 collective-permute-done.8.refs_5_
  52.3 0.0 copy-done
  52.3 6.5 %update.1 = f32[1024,1024]{1,0:T(8,128)} custom-call(f32[128,128]{1,0:T(8,128)S(1)} %get-tuple-element.11.refs_0_, f32[128,128]{1,0:T(8,128)S(1)} %get-tuple-element.12.refs_1_, f32[1024,1024]{1,0:T(8,128)S(1)} %copy-done, f32[1024,128]{1,0:T(8,128)S(1)} %collective-permute-done.6.refs_3_, f32[1024,128]{1,0:T(8,128)S(1)} %collective-permute-done.7.refs_4_, ...), custom_call_target="tpu_custom_call" | custom-call | flops 805306368 | bytes 8388608 | tf_op jit(solution)/shard_map/update/pallas_call | solution.py:147
  (7 shorter events, 0.1 us)
Async XLA Ops:
  0.8 2.7 %collective-permute-start = (f32[128,128]{1,0:T(8,128)S(1)}, f32[128,128]{1,0:T(8,128)S(1)}, u32[]{:S(2)}, u32[]{:S(2)}) collective-permute-start(f32[128,128]{1,0:T(8,128)S(1)} %slice_select_fusion), channel_id=1, source_target_pairs={{0,3}} | collective-permute-start | bytes 196616 | tf_op jit(solution)/shard_map/ppermute | solution.py:186
  4.4 8.8 %collective-permute-start.10 = (f32[512,128]{1,0:T(8,128)S(1)}, f32[512,128]{1,0:T(8,128)S(1)}, u32[]{:S(2)}, u32[]{:S(2)}) collective-permute-start(f32[512,128]{1,0:T(8,128)S(1)} %slice.12), channel_id=1, source_target_pairs={{4,5},{8,10},{12,15},{20,21},{24,26},{28,31}} | collective-permute-start | bytes 786440 | tf_op jit(solution)/shard_map/ppermute | solution.py:197
  7.9 9.8 %collective-permute-start.9 = (f32[512,128]{1,0:T(8,128)S(1)}, f32[512,128]{1,0:T(8,128)S(1)}, u32[]{:S(2)}, u32[]{:S(2)}) collective-permute-start(f32[512,128]{1,0:T(8,128)S(1)} %slice.12), channel_id=1, source_target_pairs={{0,4},{4,1},{8,14},{12,11},{16,20},{20,17},{24,30},{28,27}} | collective-permute-start | bytes 786440 | tf_op jit(solution)/shard_map/ppermute | solution.py:196
  9.2 16.6 %collective-permute-start.7 = (f32[1024,128]{1,0:T(8,128)S(1)}, f32[1024,128]{1,0:T(8,128)S(1)}, u32[]{:S(2)}, u32[]{:S(2)}) collective-permute-start(f32[1024,128]{1,0:T(8,128)S(1)} %slice.11), channel_id=1, source_target_pairs={{0,2},{4,6},{8,10},{12,14},{16,18},{20,22},{24,26},{28,30}} | collective-permute-start | bytes 1572872 | tf_op jit(solution)/shard_map/ppermute | solution.py:217
  10.5 15.3 %collective-permute-start.6 = (f32[1024,128]{1,0:T(8,128)S(1)}, f32[1024,128]{1,0:T(8,128)S(1)}, u32[]{:S(2)}, u32[]{:S(2)}) collective-permute-start(f32[1024,128]{1,0:T(8,128)S(1)} %slice.11), channel_id=1, source_target_pairs={{0,1},{4,5},{8,9},{12,13},{16,17},{20,21},{24,25},{28,29}} | collective-permute-start | bytes 1572872 | tf_op jit(solution)/shard_map/ppermute | solution.py:213
  11.8 0.7 %collective-permute-start.1 = (f32[128,128]{1,0:T(8,128)S(1)}, f32[128,128]{1,0:T(8,128)S(1)}, u32[]{:S(2)}, u32[]{:S(2)}) collective-permute-start(f32[128,128]{1,0:T(8,128)S(1)} %fusion), channel_id=1, source_target_pairs={{3,19}} | collective-permute-start | bytes 196616 | tf_op jit(solution)/shard_map/ppermute | solution.py:193
  12.6 6.4 %collective-permute-start.2 = (f32[128,128]{1,0:T(8,128)S(1)}, f32[128,128]{1,0:T(8,128)S(1)}, u32[]{:S(2)}, u32[]{:S(2)}) collective-permute-start(f32[128,128]{1,0:T(8,128)S(1)} %add.32), channel_id=1, source_target_pairs={{3,11},{19,27}} | collective-permute-start | bytes 196616 | tf_op jit(solution)/shard_map/ppermute | solution.py:193
  17.7 21.0 %collective-permute-start.11 = (f32[512,128]{1,0:T(8,128)S(1)}, f32[512,128]{1,0:T(8,128)S(1)}, u32[]{:S(2)}, u32[]{:S(2)}) collective-permute-start(f32[512,128]{1,0:T(8,128)S(1)} %add_select_fusion), channel_id=1, source_target_pairs={{0,8},{16,24},{5,13},{21,29},{10,2},{26,18},{15,7},{31,23},{4,12},... | collective-permute-start | bytes 786440 | tf_op jit(solution)/shard_map/ppermute | solution.py:202
  19.0 7.5 %collective-permute-start.3 = (f32[128,128]{1,0:T(8,128)S(1)}, f32[128,128]{1,0:T(8,128)S(1)}, u32[]{:S(2)}, u32[]{:S(2)}) collective-permute-start(f32[128,128]{1,0:T(8,128)S(1)} %add.33), channel_id=1, source_target_pairs={{3,7},{19,23},{11,15},{27,31}} | collective-permute-start | bytes 196616 | tf_op jit(solution)/shard_map/ppermute | solution.py:193
  25.8 26.5 %collective-permute-start.8 = (f32[1024,128]{1,0:T(8,128)S(1)}, f32[1024,128]{1,0:T(8,128)S(1)}, u32[]{:S(2)}, u32[]{:S(2)}) collective-permute-start(f32[1024,128]{1,0:T(8,128)S(1)} %add.37), channel_id=1, source_target_pairs={{1,3},{6,7},{9,11},{14,15},{17,19},{22,23},{25,27},{30,31}} | collective-permute-start | bytes 1572872 | tf_op jit(solution)/shard_map/ppermute | solution.py:220
  26.6 0.7 %collective-permute-start.4 = (f32[128,128]{1,0:T(8,128)S(1)}, f32[128,128]{1,0:T(8,128)S(1)}, u32[]{:S(2)}, u32[]{:S(2)}) collective-permute-start(f32[128,128]{1,0:T(8,128)S(1)} %add.34), channel_id=1, source_target_pairs={{3,2},{19,18},{11,10},{27,26},{7,6},{23,22},{15,14},{31,30}} | collective-permute-start | bytes 196616 | tf_op jit(solution)/shard_map/ppermute | solution.py:193
  27.3 11.5 %collective-permute-start.5 = (f32[128,128]{1,0:T(8,128)S(1)}, f32[128,128]{1,0:T(8,128)S(1)}, u32[]{:S(2)}, u32[]{:S(2)}) collective-permute-start(f32[128,128]{1,0:T(8,128)S(1)} %add.35), channel_id=1, source_target_pairs={{3,1},{19,17},{11,9},{27,25},{7,5},{23,21},{15,13},{31,29},{18,16}... | collective-permute-start | bytes 196616 | tf_op jit(solution)/shard_map/ppermute | solution.py:193
  38.8 13.5 %copy-start = (f32[1024,1024]{1,0:T(8,128)S(1)}, f32[1024,1024]{1,0:T(8,128)}, u32[]{:S(2)}) copy-start(f32[1024,1024]{1,0:T(8,128)} %refs_2_.1) | copy-start | bytes 12582916
  38.8 13.5 %collective-permute-start.12 = (f32[512,128]{1,0:T(8,128)S(1)}, f32[512,128]{1,0:T(8,128)S(1)}, u32[]{:S(2)}, u32[]{:S(2)}) collective-permute-start(f32[512,128]{1,0:T(8,128)S(1)} %add.40.refs_6_), channel_id=1, source_target_pairs={{16,0},{20,4},{24,8},{28,12},{0,16},{4,20},{8,24},{12,28},{17,1},{... | collective-permute-start | bytes 786440 | tf_op jit(solution)/shard_map/ppermute | solution.py:206

commit v5 on v4

v5 whole, which is shorter than its diff:
```python
import functools

import jax
import jax.numpy as jnp
from jax import lax
from jax.experimental import pallas as pl
from jax.experimental.pallas import tpu as pltpu
from jax.sharding import PartitionSpec as P

NB = 128
TILE = 256
AXES = ("row", "col")
HIGHEST = lax.Precision.HIGHEST
TRANS_B = (((1,), (1,)), ((), ()))


def factor_kernel(corner_ref, lower_ref, inverse_ref):
    works = lax.rem(lax.axis_index("row"), 2) == 0

    @pl.when(jnp.logical_not(works))
    def _():
        lower_ref[...] = jnp.zeros_like(lower_ref)
        inverse_ref[...] = jnp.zeros_like(inverse_ref)

    @pl.when(works)
    def _():
        eliminate(corner_ref, lower_ref, inverse_ref)


def eliminate(corner_ref, lower_ref, inverse_ref):
    blocks = NB // 8
    rows = lax.broadcasted_iota(jnp.int32, (NB, NB), 0)
    cols = lax.broadcasted_iota(jnp.int32, (NB, NB), 1)
    sub = lax.broadcasted_iota(jnp.int32, (8, NB), 0)
    corner = corner_ref[...]
    left = jnp.where(rows >= cols, corner, corner.T)
    right = jnp.where(rows == cols, 1.0, 0.0).astype(jnp.float32)
    lefts = [left[8 * b:8 * b + 8, :] for b in range(blocks)]
    rights = [right[8 * b:8 * b + 8, :] for b in range(blocks)]

    def whole(row):
        return jnp.broadcast_to(row, (8, NB))

    for b in range(blocks):
        def spread(i, b=b):
            return [jnp.broadcast_to(lefts[i][:, 8 * b + j:8 * b + j + 1], (8, NB)) for j in range(8)]

        here = spread(b)
        inverse_pivots, pivot_rows = [], []
        for k in range(8):
            inverse_pivots.append(1.0 / whole(here[k][k:k + 1, :]))
            pivot_rows.append([whole(column[k:k + 1, :]) for column in here])
            mult = jnp.where(sub > k, here[k] * inverse_pivots[k], 0.0)
            for j in range(k + 1, 8):
                here[j] = here[j] - mult * pivot_rows[k][j]
            lefts[b] = lefts[b] - mult * lefts[b][k:k + 1, :]
            rights[b] = rights[b] - mult * rights[b][k:k + 1, :]
        left_rows = [whole(lefts[b][k:k + 1, :]) for k in range(8)]
        right_rows = [whole(rights[b][k:k + 1, :]) for k in range(8)]
        for i in range(b + 1, blocks):
            there = spread(i)
            for k in range(8):
                mult = there[k] * inverse_pivots[k]
                for j in range(k + 1, 8):
                    there[j] = there[j] - mult * pivot_rows[k][j]
                lefts[i] = lefts[i] - mult * left_rows[k]
                rights[i] = rights[i] - mult * right_rows[k]
    upper = jnp.concatenate(lefts, axis=0)
    unit_inverse = jnp.concatenate(rights, axis=0)
    diagonal = jnp.sum(jnp.where(rows == cols, upper, 0.0), axis=1, keepdims=True)
    scale = 1.0 / jnp.sqrt(jnp.broadcast_to(diagonal, (NB, NB)))
    lower_ref[...] = jnp.where(rows >= cols, (upper * scale).T, 0.0)
    inverse_ref[...] = jnp.where(rows >= cols, unit_inverse * scale, 0.0)


def factor(corner):
    return pl.pallas_call(
        factor_kernel,
        out_shape=[jax.ShapeDtypeStruct((NB, NB), jnp.float32)] * 2,
        in_specs=[pl.BlockSpec(memory_space=pltpu.VMEM)],
        out_specs=[pl.BlockSpec(memory_space=pltpu.VMEM)] * 2,
        compiler_params=pltpu.CompilerParams(vmem_limit_bytes=4 * 1024 * 1024),
        cost_estimate=pl.CostEstimate(flops=4_000_000_000, bytes_accessed=40_000_000, transcendentals=0),
        name="factor",
    )(corner)


def split(value):
    high = value.astype(jnp.bfloat16)
    low = (value - high.astype(jnp.float32)).astype(jnp.bfloat16)
    return high, low


def update_kernel(plan, lower_ref, inverse_ref, inverse_from_ref, matrix_ref, panel_even_ref, panel_odd_ref,
                  mirror_even_ref, mirror_odd_ref, out_ref, old, new, panel, mirror, rhs, in_sems, panel_sems,
                  mirror_sems, out_sems):
    rows_here, cols_here, sources = plan
    row_index = lax.axis_index("row")
    col_index = lax.axis_index("col")
    height, width = old.shape
    col_blocks = width // NB
    each = mirror.shape[0] // sources
    tiles = height // TILE
    here = [pl.ds(i * TILE, TILE) for i in range(tiles)]
    odd = lax.rem(row_index, 2) == 1
    even = jnp.logical_not(odd)

    for q in range(sources):
        away = lax.rem(q - row_index // cols_here + sources, sources)
        for mirror_ref, here_if in [(mirror_odd_ref, odd), (mirror_even_ref, even)]:
            @pl.when(here_if)
            def _(q=q, away=away, mirror_ref=mirror_ref):
                source = mirror_ref.at[pl.ds(pl.multiple_of(away * each, each), each)]
                pltpu.make_async_copy(source, mirror.at[pl.ds(q * each, each)], mirror_sems.at[q]).start()

    first_column = matrix_ref.at[:, pl.ds(0, NB)]
    for i in range(tiles):
        for panel_ref, here_if in [(first_column, col_index == 0), (panel_odd_ref, odd & (col_index > 0)),
                                   (panel_even_ref, even & (col_index > 0))]:
            @pl.when(here_if)
            def _(i=i, panel_ref=panel_ref):
                pltpu.make_async_copy(panel_ref.at[here[i]], panel.at[here[i]], panel_sems.at[i]).start()
        pltpu.make_async_copy(matrix_ref.at[here[i]], old.at[here[i]], in_sems.at[i]).start()

    inverse = inverse_ref[...] + inverse_from_ref[...]
    for q in range(sources):
        half = pl.ds(q * each, each)
        pltpu.make_async_copy(mirror_odd_ref.at[half], mirror.at[half], mirror_sems.at[q]).wait()
    for t in range(col_blocks):
        block = (t % sources) * each + (t // sources) * NB
        part = lax.dot_general(inverse, mirror[pl.ds(block, NB), :], TRANS_B, precision=HIGHEST,
                               preferred_element_type=jnp.float32)
        high, low = split(part)
        at = pl.ds(t * NB, NB)
        rhs[pl.ds(0, NB), at] = high
        rhs[pl.ds(NB, NB), at] = high
        rhs[pl.ds(2 * NB, NB), at] = low

    for i in range(tiles):
        pltpu.make_async_copy(panel_odd_ref.at[here[i]], panel.at[here[i]], panel_sems.at[i]).wait()
        tall = lax.dot_general(panel[here[i], :], inverse, TRANS_B, precision=HIGHEST,
                               preferred_element_type=jnp.float32)
        high, low = split(tall)
        lhs = jnp.concatenate([high, low, high], axis=1)
        product = jnp.dot(lhs, rhs[...], preferred_element_type=jnp.float32)
        pltpu.make_async_copy(matrix_ref.at[here[i]], old.at[here[i]], in_sems.at[i]).wait()
        for s in range(TILE // NB):
            row = (i * (TILE // NB) + s) * rows_here + row_index
            down = pl.ds(i * TILE + s * NB, NB)
            for t in range(col_blocks):
                across = pl.ds(t * NB, NB)
                col = t * cols_here + col_index
                before = old[down, across]
                after = before - product[s * NB:(s + 1) * NB, t * NB:(t + 1) * NB]
                value = jnp.where((row >= col) & (col >= 1), after, before)
                if t == 0:
                    block = jnp.where(row == 0, lower_ref[...], tall[s * NB:(s + 1) * NB, :])
                    value = jnp.where(col == 0, block, value)
                new[down, across] = value
        pltpu.make_async_copy(new.at[here[i]], out_ref.at[here[i]], out_sems.at[i]).start()
    for i in range(tiles):
        pltpu.make_async_copy(new.at[here[i]], out_ref.at[here[i]], out_sems.at[i]).wait()


def update(lower, inverses, matrix, panels, mirrors, plan):
    height, width = matrix.shape
    sources = plan[2]
    tiles = height // TILE
    vmem = pl.BlockSpec(memory_space=pltpu.VMEM)
    anywhere = pl.BlockSpec(memory_space=pl.ANY)
    return pl.pallas_call(
        functools.partial(update_kernel, plan),
        out_shape=jax.ShapeDtypeStruct(matrix.shape, jnp.float32),
        in_specs=[vmem] * 3 + [pl.BlockSpec(memory_space=pltpu.HBM)] + [anywhere] * 4,
        out_specs=anywhere,
        scratch_shapes=[
            pltpu.VMEM((height, width), jnp.float32),
            pltpu.VMEM((height, width), jnp.float32),
            pltpu.VMEM((height, NB), jnp.float32),
            pltpu.VMEM((width, NB), jnp.float32),
            pltpu.VMEM((3 * NB, width), jnp.bfloat16),
            pltpu.SemaphoreType.DMA((tiles,)),
            pltpu.SemaphoreType.DMA((tiles,)),
            pltpu.SemaphoreType.DMA((sources,)),
            pltpu.SemaphoreType.DMA((tiles,)),
        ],
        compiler_params=pltpu.CompilerParams(vmem_limit_bytes=16 * 1024 * 1024),
        cost_estimate=pl.CostEstimate(flops=2 * height * width * NB * 3,
                                      bytes_accessed=8 * height * width, transcendentals=0),
        name="update",
    )(lower, *inverses, matrix, *panels, *mirrors)


def body(matrix):
    rows_here = lax.axis_size("row")
    cols_here = lax.axis_size("col")
    row_index = lax.axis_index("row")
    col_index = lax.axis_index("col")
    col_blocks = matrix.shape[1] // NB
    sources = rows_here // cols_here
    last = cols_here - 1
    even_rows = range(0, rows_here, 2)
    odd_rows = range(1, rows_here, 2)

    def send(value, pairs):
        return lax.ppermute(value, AXES, [(a * cols_here + b, c * cols_here + d) for (a, b), (c, d) in pairs])

    def after(value, *others):
        return lax.optimization_barrier((value, *others))[0]

    corner = jnp.where((row_index == 0) & (col_index == 0), matrix[:NB, :NB], 0.0)
    corner = corner + send(corner, [((0, 0), (0, last))])
    crossed = corner
    holders = [(0, last)]
    hops = [(1 << b, 0) for b in reversed(range(1, rows_here.bit_length() - 1))]
    hops += [(0, 1 << b) for b in range(cols_here.bit_length() - 1)]
    for dr, dc in hops:
        moved = [(r + dr, c - dc) for r, c in holders]
        corner = corner + send(corner, [(h, m) for h, m in zip(holders, moved) if m != (0, 0)])
        holders = holders + moved

    column = after(matrix[:, :NB], crossed)
    even_panel = send(column, [((r, 0), (r + 1, 0)) for r in even_rows])
    odd_panel = jnp.where(col_index == 0, after(column, even_panel), 0.0)

    half = NB * (col_blocks // sources)
    of_odd = send(odd_panel[:half], [((r, 0), (r, r % cols_here)) for r in odd_rows])
    of_even = send(even_panel[:half], [((r, 0), (r, (r - 1) % cols_here)) for r in odd_rows if (r - 1) % cols_here])
    keeps = (col_index == 0) & (row_index % cols_here == 1)
    mirror = of_odd + of_even + jnp.where(keeps, even_panel[:half], 0.0)
    holders = [((c + q * cols_here) | 1, c) for c in range(cols_here) for q in range(sources)]
    for bit in (1 << b for b in range(1, cols_here.bit_length() - 1)):
        moved = [(r ^ bit, c) for r, c in holders]
        mirror = mirror + send(mirror, list(zip(holders, moved)))
        holders = holders + moved
    mirror = jnp.concatenate([mirror] + [
        send(mirror, [(((r + q * cols_here) % rows_here, c), (r, c)) for r, c in holders])
        for q in range(1, sources)], axis=0)

    step = 1
    while step < cols_here:
        base = [(r, c) for r in odd_rows for c in range(step)]
        near = [((r, c), (r, c + step)) for r, c in base]
        far = [((r, c), (r, c + 2 * step)) for r, c in base]
        near_last = [((r, c + step), (r, c + 3 * step)) for r, c in base]
        far_last = [((r, c + 2 * step), (r, c + 3 * step)) for r, c in base]
        odd_first = odd_panel + send(odd_panel, near)
        even_first = even_panel + send(even_panel, far)
        odd_second = send(odd_first, far + near_last)
        even_second = send(even_first, near + far_last)
        odd_panel = odd_first + odd_second
        even_panel = even_first + even_second
        step *= 4

    lower, inverse = factor(corner)

    down = [((r, c), (r - 1, c)) for r in odd_rows for c in range(cols_here)]
    panel = send(even_panel, down)
    mirrors = [send(mirror, down), mirror]
    inverses = [inverse, send(inverse, [(b, a) for a, b in down])]
    return update(lower, inverses, matrix, [panel, odd_panel], mirrors, (rows_here, cols_here, sources))


def solution(mesh):
    return jax.shard_map(
        body,
        mesh=mesh,
        in_specs=(P("row", "col"),),
        out_specs=P("row", "col"),
        check_vma=False,
    )
```

time: 59.3 us -> 49.7 us (0.84)
  the two profiles are of different devices: /device:TPU:8 before, /device:TPU:0 now
where the time goes in v5:
time: 49.7 us; the launch traced here: 49.2 us
  starting transfers between devices  30.8 us (62%)
  Pallas kernels  10.7 us (22%)
  waiting for transfers between devices  3.13 us (6%)
  other arithmetic  3.06 us (6%)
  local copies, waits for them, and re-layouts  1.12 us (2%)
    ppermute x17, starting transfers between devices, send(): lax.ppermute(value, AXES, [(a * cols_here + b, c * cols_here + d) for (a,...  30.8 us
    pallas_call x1, Pallas kernels, update(): pl.pallas_call(functools.partial(update_kernel, plan), out_shape=jax.Shap...  6.44 us
    pallas_call x1, Pallas kernels, factor(): pl.pallas_call(factor_kernel, out_shape=[jax.ShapeDtypeStruct((NB, NB), j...  4.27 us
    ppermute x17, waiting for transfers between devices, send(): lax.ppermute(value, AXES, [(a * cols_here + b, c * cols_here + d) for (a,...  3.13 us
    slice x1, local copies, waits for them, and re-layouts, body(): column = after(matrix[:, :NB], crossed)  1.08 us
    add x1, other arithmetic, body(): mirror = of_odd + of_even + jnp.where(keeps, even_panel[:half], 0.0)  1 us
  transfers between devices with their start and end apart: 17, of which 3 were waited for; matrix products, arithmetic and copies ran while one was open for 5% of the time, Pallas kernels for 9%

profile of v5, /device:TPU:0, one launch (start us, length us, event | category | flops | bytes accessed | tf_op | source)
XLA Modules:
  0.0 49.2 jit_solution(16398679237553490750)
XLA Ops:
  0.0 0.8 %slice_select_fusion = f32[128,128]{1,0:T(8,128)S(1)} fusion(f32[1024,1024]{1,0:T(8,128)} %matrix_ref.1, pred[]{:T(512)S(6)} %and.13), kind=kLoop, calls=%fused_computation.3 | loop fusion | flops 16384 | bytes 131073 | tf_op jit(solution)/shard_map/jit(_where)/select_n | solution.py:211
  0.8 5.8 %collective-permute-start = (f32[128,128]{1,0:T(8,128)S(1)}, f32[128,128]{1,0:T(8,128)S(1)}, u32[]{:S(2)}, u32[]{:S(2)}) collective-permute-start(f32[128,128]{1,0:T(8,128)S(1)} %slice_select_fusion), channel_id=1, source_target_pairs={{0,3}} | collective-permute-start | bytes 196616 | tf_op jit(solution)/shard_map/ppermute | solution.py:206
  6.6 1.1 %slice.14 = f32[1024,128]{1,0:T(8,128)S(1)} slice(f32[1024,1024]{1,0:T(8,128)} %matrix_ref.1), slice={[0:1024], [0:128]} | slice | bytes 1048576 | tf_op jit(solution)/shard_map/slice | solution.py:222
  7.7 0.8 %collective-permute-done = f32[128,128]{1,0:T(8,128)S(1)} collective-permute-done((f32[128,128]{1,0:T(8,128)S(1)}, f32[128,128]{1,0:T(8,128)S(1)}, u32[]{:S(2)}, u32[]{:S(2)}) %collective-permute-start) | collective-permute-done | bytes 65568 | tf_op jit(solution)/shard_map/ppermute | solution.py:206
  8.5 0.8 %fusion.1 = f32[128,128]{1,0:T(8,128)S(1)} fusion(f32[128,128]{1,0:T(8,128)S(1)} %collective-permute-done, f32[1024,1024]{1,0:T(8,128)} %matrix_ref.1, pred[]{:T(512)S(6)} %and.13), kind=kLoop, calls=%fused_computation.5 | loop fusion | flops 32768 | bytes 196609 | tf_op jit(solution)/shard_map/add | solution.py:212
  9.4 1.3 %collective-permute-start.6 = (f32[1024,128]{1,0:T(8,128)S(1)}, f32[1024,128]{1,0:T(8,128)S(1)}, u32[]{:S(2)}, u32[]{:S(2)}) collective-permute-start(f32[1024,128]{1,0:T(8,128)S(1)} %slice.14), channel_id=1, source_target_pairs={{0,4},{8,12},{16,20},{24,28}} | collective-permute-start | bytes 1572872 | tf_op jit(solution)/shard_map/ppermute | solution.py:206
  10.7 1.5 %collective-permute-done.6 = f32[1024,128]{1,0:T(8,128)S(1)} collective-permute-done((f32[1024,128]{1,0:T(8,128)S(1)}, f32[1024,128]{1,0:T(8,128)S(1)}, u32[]{:S(2)}, u32[]{:S(2)}) %collective-permute-start.6) | collective-permute-done | bytes 524320 | tf_op jit(solution)/shard_map/ppermute | solution.py:206
  12.2 0.7 %collective-permute-start.13 = (f32[512,128]{1,0:T(8,128)S(1)}, f32[512,128]{1,0:T(8,128)S(1)}, u32[]{:S(2)}, u32[]{:S(2)}) collective-permute-start(f32[512,128]{1,0:T(8,128)S(1)} %slice.18), channel_id=1, source_target_pairs={{12,14},{28,30}} | collective-permute-start | bytes 786440 | tf_op jit(solution)/shard_map/ppermute | solution.py:206
  13.0 1.4 %collective-permute-start.12 = (f32[512,128]{1,0:T(8,128)S(1)}, f32[512,128]{1,0:T(8,128)}, u32[]{:S(2)}, u32[]{:S(2)}) collective-permute-start(f32[512,128]{1,0:T(8,128)S(1)} %slice.17), channel_id=1, source_target_pairs={{4,5},{12,15},{20,21},{28,31}} | collective-permute-start | bytes 786440 | tf_op jit(solution)/shard_map/ppermute | solution.py:206
  14.3 0.7 %collective-permute-start.7 = (f32[1024,128]{1,0:T(8,128)S(1)}, f32[1024,128]{1,0:T(8,128)S(1)}, u32[]{:S(2)}, u32[]{:S(2)}) collective-permute-start(f32[1024,128]{1,0:T(8,128)S(1)} %collective-permute-done.6), channel_id=1, source_target_pairs={{4,6},{12,14},{20,22},{28,30}} | collective-permute-start | bytes 1572872 | tf_op jit(solution)/shard_map/ppermute | solution.py:206
  15.0 0.7 %collective-permute-start.10 = (f32[1024,128]{1,0:T(8,128)S(1)}, f32[1024,128]{1,0:T(8,128)S(1)}, u32[]{:S(2)}, u32[]{:S(2)}) collective-permute-start(f32[1024,128]{1,0:T(8,128)S(1)} %broadcast_select_fusion), channel_id=1, source_target_pairs={{4,5},{12,13},{20,21},{28,29}} | collective-permute-start | bytes 1572872 | tf_op jit(solution)/shard_map/ppermute | solution.py:206
  15.8 0.0 collective-permute-done.13
  15.8 0.0 collective-permute-done.12
  15.8 1.0 %select_add_fusion = f32[512,128]{1,0:T(8,128)S(1)} fusion(f32[512,128]{1,0:T(8,128)} %collective-permute-done.12, f32[512,128]{1,0:T(8,128)S(1)} %collective-permute-done.13, pred[]{:T(512)S(6)} %and.15, f32[1024,128]{1,0:T(8,128)S(1)} %collective-permute-done.6), kind=kLoop, calls=%fused_computation.1 | loop fusion | flops 196608 | bytes 1048577 | tf_op jit(solution)/shard_map/add | solution.py:230
  16.8 0.7 %collective-permute-start.14 = (f32[512,128]{1,0:T(8,128)S(1)}, f32[512,128]{1,0:T(8,128)S(1)}, u32[]{:S(2)}, u32[]{:S(2)}) collective-permute-start(f32[512,128]{1,0:T(8,128)S(1)} %select_add_fusion), channel_id=1, source_target_pairs={{4,12},{20,28},{5,13},{21,29},{14,6},{30,22},{15,7},{31,23}} | collective-permute-start | bytes 786440 | tf_op jit(solution)/shard_map/ppermute | solution.py:206
  17.5 0.0 collective-permute-done.7
  17.5 0.1 add.45
  17.5 0.7 %collective-permute-start.8 = (f32[1024,128]{1,0:T(8,128)S(1)}, f32[1024,128]{1,0:T(8,128)S(1)}, u32[]{:S(2)}, u32[]{:S(2)}) collective-permute-start(f32[1024,128]{1,0:T(8,128)S(1)} %add.45), channel_id=1, source_target_pairs={{4,5},{12,13},{20,21},{28,29},{6,7},{14,15},{22,23},{30,31}} | collective-permute-start | bytes 1572872 | tf_op jit(solution)/shard_map/ppermute | solution.py:206
  18.2 0.7 %collective-permute-start.1 = (f32[128,128]{1,0:T(8,128)S(1)}, f32[128,128]{1,0:T(8,128)S(1)}, u32[]{:S(2)}, u32[]{:S(2)}) collective-permute-start(f32[128,128]{1,0:T(8,128)S(1)} %fusion.1), channel_id=1, source_target_pairs={{3,19}} | collective-permute-start | bytes 196616 | tf_op jit(solution)/shard_map/ppermute | solution.py:206
  18.9 0.0 collective-permute-done.1
  18.9 0.7 %collective-permute-start.2 = (f32[128,128]{1,0:T(8,128)S(1)}, f32[128,128]{1,0:T(8,128)S(1)}, u32[]{:S(2)}, u32[]{:S(2)}) collective-permute-start(f32[128,128]{1,0:T(8,128)S(1)} %add.41), channel_id=1, source_target_pairs={{3,11},{19,27}} | collective-permute-start | bytes 196616 | tf_op jit(solution)/shard_map/ppermute | solution.py:206
  19.6 0.0 collective-permute-done.2
  19.6 0.7 %collective-permute-start.3 = (f32[128,128]{1,0:T(8,128)S(1)}, f32[128,128]{1,0:T(8,128)S(1)}, u32[]{:S(2)}, u32[]{:S(2)}) collective-permute-start(f32[128,128]{1,0:T(8,128)S(1)} %add.42), channel_id=1, source_target_pairs={{3,2},{19,18},{11,10},{27,26}} | collective-permute-start | bytes 196616 | tf_op jit(solution)/shard_map/ppermute | solution.py:206
  20.3 0.0 collective-permute-done.14
  20.4 0.7 %collective-permute-start.15 = (f32[512,128]{1,0:T(8,128)S(1)}, f32[512,128]{1,0:T(8,128)S(1)}, u32[]{:S(2)}, u32[]{:S(2)}) collective-permute-start(f32[512,128]{1,0:T(8,128)S(1)} %add.52), channel_id=1, source_target_pairs={{20,4},{4,20},{21,5},{5,21},{30,14},{14,30},{31,15},{15,31},{28,12... | collective-permute-start | bytes 786440 | tf_op jit(solution)/shard_map/ppermute | solution.py:206
  21.0 0.0 collective-permute-done.10
  21.1 0.1 fusion
  21.1 0.7 %collective-permute-start.11 = (f32[1024,128]{1,0:T(8,128)S(1)}, f32[1024,128]{1,0:T(8,128)S(1)}, u32[]{:S(2)}, u32[]{:S(2)}) collective-permute-start(f32[1024,128]{1,0:T(8,128)S(1)} %fusion), channel_id=1, source_target_pairs={{4,6},{12,14},{20,22},{28,30},{5,7},{13,15},{21,23},{29,31}} | collective-permute-start | bytes 1572872 | tf_op jit(solution)/shard_map/ppermute | solution.py:206
  21.8 0.0 collective-permute-done.15
  21.9 1.3 %collective-permute-start.16 = (f32[1024,128]{1,0:T(8,128)S(1)}, f32[1024,128]{1,0:T(8,128)S(1)}, u32[]{:S(2)}, u32[]{:S(2)}) collective-permute-start(f32[1024,128]{1,0:T(8,128)S(1)} %pad_maximum_fusion.mirror_odd_ref), channel_id=1, source_target_pairs={{4,0},{5,1},{6,2},{7,3},{12,8},{13,9},{14,10},{15,11},{20,16},{21,... | collective-permute-start | bytes 1572872 | tf_op jit(solution)/shard_map/ppermute | solution.py:206
  23.2 0.0 collective-permute-done.8
  23.2 0.1 add.46
  23.3 1.3 %collective-permute-start.9 = (f32[1024,128]{1,0:T(8,128)S(1)}, f32[1024,128]{1,0:T(8,128)S(1)}, u32[]{:S(2)}, u32[]{:S(2)}) collective-permute-start(f32[1024,128]{1,0:T(8,128)S(1)} %add.46), channel_id=1, source_target_pairs={{4,0},{5,1},{6,2},{7,3},{12,8},{13,9},{14,10},{15,11},{20,16},{21,... | collective-permute-start | bytes 1572872 | tf_op jit(solution)/shard_map/ppermute | solution.py:206
  24.6 0.0 collective-permute-done.3
  24.6 0.7 %collective-permute-start.4 = (f32[128,128]{1,0:T(8,128)S(1)}, f32[128,128]{1,0:T(8,128)S(1)}, u32[]{:S(2)}, u32[]{:S(2)}) collective-permute-start(f32[128,128]{1,0:T(8,128)S(1)} %add.43), channel_id=1, source_target_pairs={{3,1},{19,17},{11,9},{27,25},{18,16},{10,8},{26,24}} | collective-permute-start | bytes 196616 | tf_op jit(solution)/shard_map/ppermute | solution.py:206
  25.3 0.0 collective-permute-done.4
  25.3 0.0 copy-start
  25.3 4.3 %factor.1 = (f32[128,128]{1,0:T(8,128)S(1)}, f32[128,128]{1,0:T(8,128)S(1)}) custom-call(f32[128,128]{1,0:T(8,128)S(1)} %add.44.corner_ref), custom_call_target="tpu_custom_call" | custom-call | flops 4000000000 | bytes 40000000 | tf_op jit(solution)/shard_map/factor/pallas_call | solution.py:77
  29.6 12.3 %collective-permute-start.5 = (f32[128,128]{1,0:T(8,128)S(1)}, f32[128,128]{1,0:T(8,128)S(1)}, u32[]{:S(2)}, u32[]{:S(2)}) collective-permute-start(f32[128,128]{1,0:T(8,128)S(1)} %get-tuple-element.10.inverse_ref), channel_id=1, source_target_pairs={{0,4},{1,5},{2,6},{3,7},{8,12},{9,13},{10,14},{11,15},{16,20},{17,... | collective-permute-start | bytes 196616 | tf_op jit(solution)/shard_map/ppermute | solution.py:206
  41.8 0.0 collective-permute-done.11
  41.9 0.1 add.48.panel_odd_ref
  41.9 0.8 %collective-permute-done.5.inverse_from_ref = f32[128,128]{1,0:T(8,128)S(1)} collective-permute-done((f32[128,128]{1,0:T(8,128)S(1)}, f32[128,128]{1,0:T(8,128)S(1)}, u32[]{:S(2)}, u32[]{:S(2)}) %collective-permute-start.5) | collective-permute-done | bytes 65568 | tf_op jit(solution)/shard_map/ppermute | solution.py:206
  42.7 0.0 collective-permute-done.16.mirror_even_ref
  42.7 0.0 collective-permute-done.9.panel_even_ref
  42.7 0.0 copy-done
  42.7 6.4 %update.1 = f32[1024,1024]{1,0:T(8,128)} custom-call(f32[128,128]{1,0:T(8,128)S(1)} %get-tuple-element.9.lower_ref, f32[128,128]{1,0:T(8,128)S(1)} %get-tuple-element.10.inverse_ref, f32[128,128]{1,0:T(8,128)S(1)} %collective-permute-done.5.inverse_from_ref, f32[1024,1024]{1,0:T(8,128)S(1)} %copy-done, ...), custom_call_target="tpu_custom_call" | custom-call | flops 805306368 | bytes 8388608 | tf_op jit(solution)/shard_map/update/pallas_call | solution.py:171
  (9 shorter events, 0.2 us)
Async XLA Ops:
  0.8 7.7 %collective-permute-start = (f32[128,128]{1,0:T(8,128)S(1)}, f32[128,128]{1,0:T(8,128)S(1)}, u32[]{:S(2)}, u32[]{:S(2)}) collective-permute-start(f32[128,128]{1,0:T(8,128)S(1)} %slice_select_fusion), channel_id=1, source_target_pairs={{0,3}} | collective-permute-start | bytes 196616 | tf_op jit(solution)/shard_map/ppermute | solution.py:206
  9.4 2.8 %collective-permute-start.6 = (f32[1024,128]{1,0:T(8,128)S(1)}, f32[1024,128]{1,0:T(8,128)S(1)}, u32[]{:S(2)}, u32[]{:S(2)}) collective-permute-start(f32[1024,128]{1,0:T(8,128)S(1)} %slice.14), channel_id=1, source_target_pairs={{0,4},{8,12},{16,20},{24,28}} | collective-permute-start | bytes 1572872 | tf_op jit(solution)/shard_map/ppermute | solution.py:206
  12.2 3.5 %collective-permute-start.13 = (f32[512,128]{1,0:T(8,128)S(1)}, f32[512,128]{1,0:T(8,128)S(1)}, u32[]{:S(2)}, u32[]{:S(2)}) collective-permute-start(f32[512,128]{1,0:T(8,128)S(1)} %slice.18), channel_id=1, source_target_pairs={{12,14},{28,30}} | collective-permute-start | bytes 786440 | tf_op jit(solution)/shard_map/ppermute | solution.py:206
  13.0 2.8 %collective-permute-start.12 = (f32[512,128]{1,0:T(8,128)S(1)}, f32[512,128]{1,0:T(8,128)}, u32[]{:S(2)}, u32[]{:S(2)}) collective-permute-start(f32[512,128]{1,0:T(8,128)S(1)} %slice.17), channel_id=1, source_target_pairs={{4,5},{12,15},{20,21},{28,31}} | collective-permute-start | bytes 786440 | tf_op jit(solution)/shard_map/ppermute | solution.py:206
  14.3 3.1 %collective-permute-start.7 = (f32[1024,128]{1,0:T(8,128)S(1)}, f32[1024,128]{1,0:T(8,128)S(1)}, u32[]{:S(2)}, u32[]{:S(2)}) collective-permute-start(f32[1024,128]{1,0:T(8,128)S(1)} %collective-permute-done.6), channel_id=1, source_target_pairs={{4,6},{12,14},{20,22},{28,30}} | collective-permute-start | bytes 1572872 | tf_op jit(solution)/shard_map/ppermute | solution.py:206
  15.0 6.0 %collective-permute-start.10 = (f32[1024,128]{1,0:T(8,128)S(1)}, f32[1024,128]{1,0:T(8,128)S(1)}, u32[]{:S(2)}, u32[]{:S(2)}) collective-permute-start(f32[1024,128]{1,0:T(8,128)S(1)} %broadcast_select_fusion), channel_id=1, source_target_pairs={{4,5},{12,13},{20,21},{28,29}} | collective-permute-start | bytes 1572872 | tf_op jit(solution)/shard_map/ppermute | solution.py:206
  16.8 3.5 %collective-permute-start.14 = (f32[512,128]{1,0:T(8,128)S(1)}, f32[512,128]{1,0:T(8,128)S(1)}, u32[]{:S(2)}, u32[]{:S(2)}) collective-permute-start(f32[512,128]{1,0:T(8,128)S(1)} %select_add_fusion), channel_id=1, source_target_pairs={{4,12},{20,28},{5,13},{21,29},{14,6},{30,22},{15,7},{31,23}} | collective-permute-start | bytes 786440 | tf_op jit(solution)/shard_map/ppermute | solution.py:206
  17.5 5.6 %collective-permute-start.8 = (f32[1024,128]{1,0:T(8,128)S(1)}, f32[1024,128]{1,0:T(8,128)S(1)}, u32[]{:S(2)}, u32[]{:S(2)}) collective-permute-start(f32[1024,128]{1,0:T(8,128)S(1)} %add.45), channel_id=1, source_target_pairs={{4,5},{12,13},{20,21},{28,29},{6,7},{14,15},{22,23},{30,31}} | collective-permute-start | bytes 1572872 | tf_op jit(solution)/shard_map/ppermute | solution.py:206
  18.2 0.7 %collective-permute-start.1 = (f32[128,128]{1,0:T(8,128)S(1)}, f32[128,128]{1,0:T(8,128)S(1)}, u32[]{:S(2)}, u32[]{:S(2)}) collective-permute-start(f32[128,128]{1,0:T(8,128)S(1)} %fusion.1), channel_id=1, source_target_pairs={{3,19}} | collective-permute-start | bytes 196616 | tf_op jit(solution)/shard_map/ppermute | solution.py:206
  18.9 0.7 %collective-permute-start.2 = (f32[128,128]{1,0:T(8,128)S(1)}, f32[128,128]{1,0:T(8,128)S(1)}, u32[]{:S(2)}, u32[]{:S(2)}) collective-permute-start(f32[128,128]{1,0:T(8,128)S(1)} %add.41), channel_id=1, source_target_pairs={{3,11},{19,27}} | collective-permute-start | bytes 196616 | tf_op jit(solution)/shard_map/ppermute | solution.py:206
  19.6 4.9 %collective-permute-start.3 = (f32[128,128]{1,0:T(8,128)S(1)}, f32[128,128]{1,0:T(8,128)S(1)}, u32[]{:S(2)}, u32[]{:S(2)}) collective-permute-start(f32[128,128]{1,0:T(8,128)S(1)} %add.42), channel_id=1, source_target_pairs={{3,2},{19,18},{11,10},{27,26}} | collective-permute-start | bytes 196616 | tf_op jit(solution)/shard_map/ppermute | solution.py:206
  20.4 1.5 %collective-permute-start.15 = (f32[512,128]{1,0:T(8,128)S(1)}, f32[512,128]{1,0:T(8,128)S(1)}, u32[]{:S(2)}, u32[]{:S(2)}) collective-permute-start(f32[512,128]{1,0:T(8,128)S(1)} %add.52), channel_id=1, source_target_pairs={{20,4},{4,20},{21,5},{5,21},{30,14},{14,30},{31,15},{15,31},{28,12... | collective-permute-start | bytes 786440 | tf_op jit(solution)/shard_map/ppermute | solution.py:206
  21.1 20.7 %collective-permute-start.11 = (f32[1024,128]{1,0:T(8,128)S(1)}, f32[1024,128]{1,0:T(8,128)S(1)}, u32[]{:S(2)}, u32[]{:S(2)}) collective-permute-start(f32[1024,128]{1,0:T(8,128)S(1)} %fusion), channel_id=1, source_target_pairs={{4,6},{12,14},{20,22},{28,30},{5,7},{13,15},{21,23},{29,31}} | collective-permute-start | bytes 1572872 | tf_op jit(solution)/shard_map/ppermute | solution.py:206
  21.9 20.8 %collective-permute-start.16 = (f32[1024,128]{1,0:T(8,128)S(1)}, f32[1024,128]{1,0:T(8,128)S(1)}, u32[]{:S(2)}, u32[]{:S(2)}) collective-permute-start(f32[1024,128]{1,0:T(8,128)S(1)} %pad_maximum_fusion.mirror_odd_ref), channel_id=1, source_target_pairs={{4,0},{5,1},{6,2},{7,3},{12,8},{13,9},{14,10},{15,11},{20,16},{21,... | collective-permute-start | bytes 1572872 | tf_op jit(solution)/shard_map/ppermute | solution.py:206
  23.3 19.5 %collective-permute-start.9 = (f32[1024,128]{1,0:T(8,128)S(1)}, f32[1024,128]{1,0:T(8,128)S(1)}, u32[]{:S(2)}, u32[]{:S(2)}) collective-permute-start(f32[1024,128]{1,0:T(8,128)S(1)} %add.46), channel_id=1, source_target_pairs={{4,0},{5,1},{6,2},{7,3},{12,8},{13,9},{14,10},{15,11},{20,16},{21,... | collective-permute-start | bytes 1572872 | tf_op jit(solution)/shard_map/ppermute | solution.py:206
  24.6 0.7 %collective-permute-start.4 = (f32[128,128]{1,0:T(8,128)S(1)}, f32[128,128]{1,0:T(8,128)S(1)}, u32[]{:S(2)}, u32[]{:S(2)}) collective-permute-start(f32[128,128]{1,0:T(8,128)S(1)} %add.43), channel_id=1, source_target_pairs={{3,1},{19,17},{11,9},{27,25},{18,16},{10,8},{26,24}} | collective-permute-start | bytes 196616 | tf_op jit(solution)/shard_map/ppermute | solution.py:206
  25.3 17.4 %copy-start = (f32[1024,1024]{1,0:T(8,128)S(1)}, f32[1024,1024]{1,0:T(8,128)}, u32[]{:S(2)}) copy-start(f32[1024,1024]{1,0:T(8,128)} %matrix_ref.1) | copy-start | bytes 12582916
  29.6 13.1 %collective-permute-start.5 = (f32[128,128]{1,0:T(8,128)S(1)}, f32[128,128]{1,0:T(8,128)S(1)}, u32[]{:S(2)}, u32[]{:S(2)}) collective-permute-start(f32[128,128]{1,0:T(8,128)S(1)} %get-tuple-element.10.inverse_ref), channel_id=1, source_target_pairs={{0,4},{1,5},{2,6},{3,7},{8,12},{9,13},{10,14},{11,15},{16,20},{17,... | collective-permute-start | bytes 196616 | tf_op jit(solution)/shard_map/ppermute | solution.py:206

commit v6 on v5

v6 whole, which is shorter than its diff:
```python
import functools

import jax
import jax.numpy as jnp
from jax import lax
from jax.experimental import pallas as pl
from jax.experimental.pallas import tpu as pltpu
from jax.sharding import PartitionSpec as P

NB = 128
TILE = 256
AXES = ("row", "col")
HIGHEST = lax.Precision.HIGHEST
TRANS_B = (((1,), (1,)), ((), ()))


def factor_kernel(matrix_ref, lower_ref, inverse_ref, corner_ref, sem):
    works = (lax.axis_index("row") == 0) & (lax.axis_index("col") == 0)

    @pl.when(jnp.logical_not(works))
    def _():
        lower_ref[...] = jnp.zeros_like(lower_ref)
        inverse_ref[...] = jnp.zeros_like(inverse_ref)

    @pl.when(works)
    def _():
        copy = pltpu.make_async_copy(matrix_ref.at[pl.ds(0, NB), pl.ds(0, NB)], corner_ref, sem)
        copy.start()
        copy.wait()
        eliminate(corner_ref, lower_ref, inverse_ref)


def eliminate(corner_ref, lower_ref, inverse_ref):
    blocks = NB // 8
    rows = lax.broadcasted_iota(jnp.int32, (NB, NB), 0)
    cols = lax.broadcasted_iota(jnp.int32, (NB, NB), 1)
    sub = lax.broadcasted_iota(jnp.int32, (8, NB), 0)
    corner = corner_ref[...]
    left = jnp.where(rows >= cols, corner, corner.T)
    right = jnp.where(rows == cols, 1.0, 0.0).astype(jnp.float32)
    lefts = [left[8 * b:8 * b + 8, :] for b in range(blocks)]
    rights = [right[8 * b:8 * b + 8, :] for b in range(blocks)]

    def whole(row):
        return jnp.broadcast_to(row, (8, NB))

    for b in range(blocks):
        def spread(i, b=b):
            return [jnp.broadcast_to(lefts[i][:, 8 * b + j:8 * b + j + 1], (8, NB)) for j in range(8)]

        here = spread(b)
        inverse_pivots, pivot_rows = [], []
        for k in range(8):
            inverse_pivots.append(1.0 / whole(here[k][k:k + 1, :]))
            pivot_rows.append([whole(column[k:k + 1, :]) for column in here])
            mult = jnp.where(sub > k, here[k] * inverse_pivots[k], 0.0)
            for j in range(k + 1, 8):
                here[j] = here[j] - mult * pivot_rows[k][j]
            lefts[b] = lefts[b] - mult * lefts[b][k:k + 1, :]
            rights[b] = rights[b] - mult * rights[b][k:k + 1, :]
        left_rows = [whole(lefts[b][k:k + 1, :]) for k in range(8)]
        right_rows = [whole(rights[b][k:k + 1, :]) for k in range(8)]
        for i in range(b + 1, blocks):
            there = spread(i)
            for k in range(8):
                mult = there[k] * inverse_pivots[k]
                for j in range(k + 1, 8):
                    there[j] = there[j] - mult * pivot_rows[k][j]
                lefts[i] = lefts[i] - mult * left_rows[k]
                rights[i] = rights[i] - mult * right_rows[k]
    upper = jnp.concatenate(lefts, axis=0)
    unit_inverse = jnp.concatenate(rights, axis=0)
    diagonal = jnp.sum(jnp.where(rows == cols, upper, 0.0), axis=1, keepdims=True)
    scale = 1.0 / jnp.sqrt(jnp.broadcast_to(diagonal, (NB, NB)))
    lower_ref[...] = jnp.where(rows >= cols, (upper * scale).T, 0.0)
    inverse_ref[...] = jnp.where(rows >= cols, unit_inverse * scale, 0.0)


def factor(matrix):
    return pl.pallas_call(
        factor_kernel,
        out_shape=[jax.ShapeDtypeStruct((NB, NB), jnp.float32)] * 2,
        in_specs=[pl.BlockSpec(memory_space=pltpu.HBM)],
        out_specs=[pl.BlockSpec(memory_space=pltpu.VMEM)] * 2,
        scratch_shapes=[pltpu.VMEM((NB, NB), jnp.float32), pltpu.SemaphoreType.DMA],
        compiler_params=pltpu.CompilerParams(vmem_limit_bytes=62 * 1024 * 1024),
        cost_estimate=pl.CostEstimate(flops=4_000_000, bytes_accessed=200_000, transcendentals=0),
        name="factor",
    )(matrix)


def split(value):
    high = value.astype(jnp.bfloat16)
    low = (value - high.astype(jnp.float32)).astype(jnp.bfloat16)
    return high, low


def update_kernel(plan, lower_ref, inverse_ref, inverse_from_ref, matrix_ref, mirror_even_ref, mirror_odd_ref, *refs):
    rows_here, cols_here, sources = plan
    panel_refs = refs[:cols_here - 1]
    out_ref, new, panel, mirror, rhs, out_sems = refs[cols_here - 1:]
    row_index = lax.axis_index("row")
    col_index = lax.axis_index("col")
    height, width = matrix_ref.shape
    col_blocks = width // NB
    each = mirror.shape[0] // sources
    tiles = height // TILE
    here = [pl.ds(i * TILE, TILE) for i in range(tiles)]
    odd = lax.rem(row_index, 2) == 1

    for q in range(sources):
        away = lax.rem(q - row_index // cols_here + sources, sources)
        for mirror_ref, here_if in [(mirror_odd_ref, odd), (mirror_even_ref, jnp.logical_not(odd))]:
            @pl.when(here_if)
            def _(q=q, away=away, mirror_ref=mirror_ref):
                mirror[pl.ds(q * each, each), :] = mirror_ref[pl.ds(pl.multiple_of(away * each, each), each), :]

    @pl.when(col_index == 0)
    def _():
        panel[...] = matrix_ref[:, pl.ds(0, NB)]

    for c in range(1, cols_here):
        @pl.when(col_index == c)
        def _(c=c):
            panel[...] = panel_refs[c - 1][...]

    inverse = inverse_ref[...] + inverse_from_ref[...]
    for t in range(col_blocks):
        block = (t % sources) * each + (t // sources) * NB
        part = lax.dot_general(inverse, mirror[pl.ds(block, NB), :], TRANS_B, precision=HIGHEST,
                               preferred_element_type=jnp.float32)
        high, low = split(part)
        at = pl.ds(t * NB, NB)
        rhs[pl.ds(0, NB), at] = high
        rhs[pl.ds(NB, NB), at] = high
        rhs[pl.ds(2 * NB, NB), at] = low

    for i in range(tiles):
        tall = lax.dot_general(panel[here[i], :], inverse, TRANS_B, precision=HIGHEST,
                               preferred_element_type=jnp.float32)
        high, low = split(tall)
        lhs = jnp.concatenate([high, low, high], axis=1)
        product = jnp.dot(lhs, rhs[...], preferred_element_type=jnp.float32)
        for s in range(TILE // NB):
            row = (i * (TILE // NB) + s) * rows_here + row_index
            down = pl.ds(i * TILE + s * NB, NB)
            for t in range(col_blocks):
                across = pl.ds(t * NB, NB)
                col = t * cols_here + col_index
                before = matrix_ref[down, across]
                after = before - product[s * NB:(s + 1) * NB, t * NB:(t + 1) * NB]
                value = jnp.where((row >= col) & (col >= 1), after, before)
                if t == 0:
                    block = tall[s * NB:(s + 1) * NB, :]
                    if i == 0 and s == 0:
                        block = jnp.where(row == 0, lower_ref[...], block)
                    value = jnp.where(col == 0, block, value)
                new[down, across] = value
        pltpu.make_async_copy(new.at[here[i]], out_ref.at[here[i]], out_sems.at[i]).start()
    for i in range(tiles):
        pltpu.make_async_copy(new.at[here[i]], out_ref.at[here[i]], out_sems.at[i]).wait()


def update(lower, inverses, matrix, panels, mirrors, plan):
    height, width = matrix.shape
    tiles = height // TILE
    vmem = pl.BlockSpec(memory_space=pltpu.VMEM)
    return pl.pallas_call(
        functools.partial(update_kernel, plan),
        out_shape=jax.ShapeDtypeStruct(matrix.shape, jnp.float32),
        in_specs=[vmem] * (4 + len(mirrors) + len(panels)),
        out_specs=pl.BlockSpec(memory_space=pl.ANY),
        scratch_shapes=[
            pltpu.VMEM((height, width), jnp.float32),
            pltpu.VMEM((height, NB), jnp.float32),
            pltpu.VMEM((width, NB), jnp.float32),
            pltpu.VMEM((3 * NB, width), jnp.bfloat16),
            pltpu.SemaphoreType.DMA((tiles,)),
        ],
        compiler_params=pltpu.CompilerParams(vmem_limit_bytes=28 * 1024 * 1024),
        cost_estimate=pl.CostEstimate(flops=2 * height * width * NB * 3,
                                      bytes_accessed=8 * height * width, transcendentals=0),
        name="update",
    )(lower, *inverses, matrix, *mirrors, *panels)


TIES = {'mode': 'Y', 'A': 0, 'E1': 0, 'E2': 0, 'E3': None, 'M1': 1, 'M2': 3, 'X1': 4, 'need': {4: [1, 2]}, 'X1need': False}


def body(matrix):
    rows_here = lax.axis_size("row")
    cols_here = lax.axis_size("col")
    row_index = lax.axis_index("row")
    col_index = lax.axis_index("col")
    col_blocks = matrix.shape[1] // NB
    sources = rows_here // cols_here
    last = cols_here - 1
    every_row = range(rows_here)
    even_rows = range(0, rows_here, 2)
    odd_rows = range(1, rows_here, 2)
    T = TIES

    def send(value, pairs):
        return lax.ppermute(value, AXES, [(a * cols_here + b, c * cols_here + d) for (a, b), (c, d) in pairs])

    def after(value, *others):
        return lax.optimization_barrier((value, *others))[0]

    column = matrix[:, :NB]
    half = NB * (col_blocks // sources)
    first = column[:half]
    if T["mode"] == "Y":
        lower, inverse = factor(matrix)
    else:
        inverse = jnp.where((row_index == 0) & (col_index == 0), matrix[:NB, :NB], 0.0)
    inverse = inverse + send(inverse, [((0, 0), (0, last))])
    along = [inverse]
    bulk = {}

    def tie(value, name):
        t = T[name]
        return value if t is None or t >= len(along) else after(value, along[t])

    def try_bulk():
        if "A" not in bulk and T["A"] < len(along):
            bulk["A"] = send(tie(first, "A"), [((r, 0), (r | 1, r % cols_here)) for r in every_row])
        if 1 not in bulk and T["E1"] < len(along):
            merged = tie(column, "E1")
            step = 1
            while step < cols_here:
                base = [(r, c) for r in every_row for c in range(step)]
                near = send(merged, [((r, c), (r, c + step)) for r, c in base])
                far = send(merged, [((r, c), (r, c + 2 * step)) for r, c in base])
                both = near + far
                if T["E3"] is not None and T["E3"] < len(along): both = after(both, along[T["E3"]])
                relay = send(both, [((r, c + step * (1 + r % 2)), (r, c + 3 * step)) for r, c in base])
                for c in range(step):
                    bulk[c + step], bulk[c + 2 * step], bulk[c + 3 * step] = near, far, relay
                step *= 4
                if step < cols_here:
                    merged = jnp.where(col_index == 0, column, 0.0) + sum({id(v): v for k, v in bulk.items() if k != "A"}.values())

    holders = [(0, last)]
    hops = [(1 << b, 0) for b in reversed(range(1, rows_here.bit_length() - 1))]
    hops += [(0, 1 << b) for b in range(cols_here.bit_length() - 1)]
    for n, (dr, dc) in enumerate(hops):
        try_bulk()
        need = [bulk[k] for k in T["need"].get(n + 1, []) if k in bulk]
        if need:
            inverse, *got = lax.optimization_barrier((inverse, *need))
            for k, v in zip([k for k in T["need"][n + 1] if k in bulk], got): bulk[k] = v
        moved = [(r + dr, c - dc) for r, c in holders]
        inverse = inverse + send(inverse, [(h, m) for h, m in zip(holders, moved) if m != (0, 0)])
        holders = holders + moved
        along.append(inverse)
    try_bulk()
    panels = [bulk[c] for c in range(1, cols_here)]

    mirror = bulk["A"]
    holders = [((c + q * cols_here) | 1, c) for c in range(cols_here) for q in range(sources)]
    mirror = tie(mirror, "M1")
    for bit in (1 << b for b in range(1, cols_here.bit_length() - 1)):
        moved = [(r ^ bit, c) for r, c in holders]
        mirror = mirror + send(mirror, list(zip(holders, moved)))
        holders = holders + moved
    mirror = tie(mirror, "M2")
    mirror = jnp.concatenate([mirror] + [
        send(mirror, [(((r + q * cols_here) % rows_here, c), (r, c)) for r, c in holders])
        for q in range(1, sources)], axis=0)
    need = T["need"].get(5, [])
    if need:
        inverse, *got = lax.optimization_barrier((inverse, *[panels[k - 1] for k in need]))
        for k, v in zip(need, got): panels[k - 1] = v
    if T.get("X1need"):
        mirror, *panels = lax.optimization_barrier((mirror, *panels))
    mirror = tie(mirror, "X1")
    if T["mode"] == "X":
        lower, inverse = factor(inverse)
    down = [((r, c), (r - 1, c)) for r in odd_rows for c in range(cols_here)]
    mirrors = [send(mirror, down), mirror]
    inverses = [inverse, send(inverse, [(b, a) for a, b in down])]
    return update(lower, inverses, matrix, panels, mirrors, (rows_here, cols_here, sources))


def solution(mesh):
    return jax.shard_map(
        body,
        mesh=mesh,
        in_specs=(P("row", "col"),),
        out_specs=P("row", "col"),
        check_vma=False,
    )
```

time: 49.7 us -> 42.6 us (0.86)
  the two profiles are of different devices: /device:TPU:0 before, /device:TPU:6 now
where the time goes in v6:
time: 42.6 us; the launch traced here: 41.8 us
  starting transfers between devices  17.9 us (42%)
  waiting for transfers between devices  15.4 us (36%)
  Pallas kernels  5.25 us (12%)
  local copies, waits for them, and re-layouts  2.06 us (5%)
  other arithmetic  1.01 us (2%)
    ppermute x13, starting transfers between devices, send(): lax.ppermute(value, AXES, [(a * cols_here + b, c * cols_here + d) for (a,...  17.9 us
    ppermute x13, waiting for transfers between devices, send(): lax.ppermute(value, AXES, [(a * cols_here + b, c * cols_here + d) for (a,...  15.4 us
    pallas_call x1, Pallas kernels, update(): pl.pallas_call(functools.partial(update_kernel, plan), out_shape=jax.Shap...  4.59 us
    slice x1, local copies, waits for them, and re-layouts, body(): column = matrix[:, :NB]  1.08 us
    slice x1, local copies, waits for them, and re-layouts, body(): first = column[:half]  0.97 us
  transfers between devices with their start and end apart: 13, of which 6 were waited for; matrix products, arithmetic and copies ran while one was open for 5% of the time, Pallas kernels for 0%

profile of v6, /device:TPU:6, one launch (start us, length us, event | category | flops | bytes accessed | tf_op | source)
XLA Modules:
  0.0 41.8 jit_solution(16917921691392752079)
XLA Ops:
  0.0 0.7 %factor.1 = (f32[128,128]{1,0:T(8,128)}, f32[128,128]{1,0:T(8,128)}) custom-call(f32[1024,1024]{1,0:T(8,128)} %matrix_ref.3), custom_call_target="tpu_custom_call" | custom-call | flops 4000000 | bytes 200000 | tf_op jit(solution)/shard_map/factor/pallas_call | solution.py:80
  0.7 0.0 copy-start
  0.7 0.0 copy-start.1
  0.7 1.6 %collective-permute-start = (f32[128,128]{1,0:T(8,128)}, f32[128,128]{1,0:T(8,128)S(1)}, u32[]{:S(2)}, u32[]{:S(2)}) collective-permute-start(f32[128,128]{1,0:T(8,128)} %get-tuple-element.16), channel_id=1, source_target_pairs={{0,3}} | collective-permute-start | bytes 196616 | tf_op jit(solution)/shard_map/ppermute | solution.py:204
  2.3 1.0 %slice.8 = f32[512,128]{1,0:T(8,128)S(1)} slice(f32[1024,1024]{1,0:T(8,128)} %matrix_ref.3), slice={[0:512], [0:128]} | slice | bytes 524288 | tf_op jit(solution)/shard_map/slice | solution.py:211
  3.2 6.3 %collective-permute-done = f32[128,128]{1,0:T(8,128)S(1)} collective-permute-done((f32[128,128]{1,0:T(8,128)}, f32[128,128]{1,0:T(8,128)S(1)}, u32[]{:S(2)}, u32[]{:S(2)}) %collective-permute-start) | collective-permute-done | bytes 65568 | tf_op jit(solution)/shard_map/ppermute | solution.py:204
  9.5 0.8 %add.21 = f32[128,128]{1,0:T(8,128)S(1)} add(f32[128,128]{1,0:T(8,128)} %get-tuple-element.16, f32[128,128]{1,0:T(8,128)S(1)} %collective-permute-done) | non-fusion elementwise | flops 16384 | bytes 196608 | tf_op jit(solution)/shard_map/add | solution.py:216
  10.3 0.7 %collective-permute-start.8 = (f32[512,128]{1,0:T(8,128)S(1)}, f32[512,128]{1,0:T(8,128)S(1)}, u32[]{:S(2)}, u32[]{:S(2)}) collective-permute-start(f32[512,128]{1,0:T(8,128)S(1)} %slice.8), channel_id=1, source_target_pairs={{0,4},{4,5},{8,14},{12,15},{16,20},{20,21},{24,30},{28,31}} | collective-permute-start | bytes 786440 | tf_op jit(solution)/shard_map/ppermute | solution.py:204
  11.0 1.3 %collective-permute-start.1 = (f32[128,128]{1,0:T(8,128)S(1)}, f32[128,128]{1,0:T(8,128)S(1)}, u32[]{:S(2)}, u32[]{:S(2)}) collective-permute-start(f32[128,128]{1,0:T(8,128)S(1)} %add.21), channel_id=1, source_target_pairs={{3,19}} | collective-permute-start | bytes 196616 | tf_op jit(solution)/shard_map/ppermute | solution.py:204
  12.3 1.1 %slice.7 = f32[1024,128]{1,0:T(8,128)S(1)} slice(f32[1024,1024]{1,0:T(8,128)} %matrix_ref.3), slice={[0:1024], [0:128]} | slice | bytes 1048576 | tf_op jit(solution)/shard_map/slice | solution.py:209
  13.4 0.7 %collective-permute-start.5 = (f32[1024,128]{1,0:T(8,128)S(1)}, f32[1024,128]{1,0:T(8,128)S(1)}, u32[]{:S(2)}, u32[]{:S(2)}) collective-permute-start(f32[1024,128]{1,0:T(8,128)S(1)} %slice.7), channel_id=1, source_target_pairs={{0,2},{4,6},{8,10},{12,14},{16,18},{20,22},{24,26},{28,30}} | collective-permute-start | bytes 1572872 | tf_op jit(solution)/shard_map/ppermute | solution.py:204
  14.1 0.7 %collective-permute-start.4 = (f32[1024,128]{1,0:T(8,128)S(1)}, f32[1024,128]{1,0:T(8,128)S(1)}, u32[]{:S(2)}, u32[]{:S(2)}) collective-permute-start(f32[1024,128]{1,0:T(8,128)S(1)} %slice.7), channel_id=1, source_target_pairs={{0,1},{4,5},{8,9},{12,13},{16,17},{20,21},{24,25},{28,29}} | collective-permute-start | bytes 1572872 | tf_op jit(solution)/shard_map/ppermute | solution.py:204
  14.8 0.0 collective-permute-done.1
  14.8 0.0 collective-permute-done.8
  14.9 0.7 %collective-permute-start.9 = (f32[512,128]{1,0:T(8,128)S(1)}, f32[512,128]{1,0:T(8,128)S(1)}, u32[]{:S(2)}, u32[]{:S(2)}) collective-permute-start(f32[512,128]{1,0:T(8,128)S(1)} %collective-permute-done.8), channel_id=1, source_target_pairs={{4,12},{20,28},{5,13},{21,29},{14,6},{30,22},{15,7},{31,23}} | collective-permute-start | bytes 786440 | tf_op jit(solution)/shard_map/ppermute | solution.py:204
  15.5 1.3 %collective-permute-start.2 = (f32[128,128]{1,0:T(8,128)S(1)}, f32[128,128]{1,0:T(8,128)S(1)}, u32[]{:S(2)}, u32[]{:S(2)}) collective-permute-start(f32[128,128]{1,0:T(8,128)S(1)} %add.22), channel_id=1, source_target_pairs={{3,11},{19,27}} | collective-permute-start | bytes 196616 | tf_op jit(solution)/shard_map/ppermute | solution.py:204
  16.8 1.9 %collective-permute-done.2 = f32[128,128]{1,0:T(8,128)S(1)} collective-permute-done((f32[128,128]{1,0:T(8,128)S(1)}, f32[128,128]{1,0:T(8,128)S(1)}, u32[]{:S(2)}, u32[]{:S(2)}) %collective-permute-start.2) | collective-permute-done | bytes 65568 | tf_op jit(solution)/shard_map/ppermute | solution.py:204
  18.7 1.3 %collective-permute-start.3 = (f32[128,128]{1,0:T(8,128)S(1)}, f32[128,128]{1,0:T(8,128)S(1)}, u32[]{:S(2)}, u32[]{:S(2)}) collective-permute-start(f32[128,128]{1,0:T(8,128)S(1)} %add.23), channel_id=1, source_target_pairs={{3,2},{19,18},{11,10},{27,26}} | collective-permute-start | bytes 196616 | tf_op jit(solution)/shard_map/ppermute | solution.py:204
  20.0 1.9 %collective-permute-done.3 = f32[128,128]{1,0:T(8,128)S(1)} collective-permute-done((f32[128,128]{1,0:T(8,128)S(1)}, f32[128,128]{1,0:T(8,128)S(1)}, u32[]{:S(2)}, u32[]{:S(2)}) %collective-permute-start.3) | collective-permute-done | bytes 65568 | tf_op jit(solution)/shard_map/ppermute | solution.py:204
  21.9 0.0 collective-permute-done.9
  22.0 0.7 %collective-permute-start.10 = (f32[512,128]{1,0:T(8,128)S(1)}, f32[512,128]{1,0:T(8,128)S(1)}, u32[]{:S(2)}, u32[]{:S(2)}) collective-permute-start(f32[512,128]{1,0:T(8,128)S(1)} %add.26), channel_id=1, source_target_pairs={{20,4},{4,20},{21,5},{5,21},{30,14},{14,30},{31,15},{15,31},{28,12... | collective-permute-start | bytes 786440 | tf_op jit(solution)/shard_map/ppermute | solution.py:204
  22.7 0.0 collective-permute-done.5.refs_1_
  22.7 0.0 collective-permute-done.4.refs_0_
  22.7 3.4 %collective-permute-start.6 = (f32[128,128]{1,0:T(8,128)S(1)}, f32[128,128]{1,0:T(8,128)S(1)}, u32[]{:S(2)}, u32[]{:S(2)}) collective-permute-start(f32[128,128]{1,0:T(8,128)S(1)} %add.24), channel_id=1, source_target_pairs={{3,1},{19,17},{11,9},{27,25},{18,16},{10,8},{26,24}} | collective-permute-start | bytes 196616 | tf_op jit(solution)/shard_map/ppermute | solution.py:204
  26.1 0.1 add.27
  26.1 1.3 %collective-permute-start.12 = (f32[1024,128]{1,0:T(8,128)S(1)}, f32[1024,128]{1,0:T(8,128)S(1)}, u32[]{:S(2)}, u32[]{:S(2)}) collective-permute-start(f32[1024,128]{1,0:T(8,128)S(1)} %add.27), channel_id=1, source_target_pairs={{1,3},{6,7},{9,11},{14,15},{17,19},{22,23},{25,27},{30,31}} | collective-permute-start | bytes 1572872 | tf_op jit(solution)/shard_map/ppermute | solution.py:204
  27.4 0.5 %collective-permute-done.6 = f32[128,128]{1,0:T(8,128)S(1)} collective-permute-done((f32[128,128]{1,0:T(8,128)S(1)}, f32[128,128]{1,0:T(8,128)S(1)}, u32[]{:S(2)}, u32[]{:S(2)}) %collective-permute-start.6) | collective-permute-done | bytes 65568 | tf_op jit(solution)/shard_map/ppermute | solution.py:204
  28.0 0.0 collective-permute-done.10
  28.0 1.3 %collective-permute-start.11 = (f32[1024,128]{1,0:T(8,128)S(1)}, f32[1024,128]{1,0:T(8,128)S(1)}, u32[]{:S(2)}, u32[]{:S(2)}) collective-permute-start(f32[1024,128]{1,0:T(8,128)S(1)} %pad_maximum_fusion.mirror_odd_ref), channel_id=1, source_target_pairs={{4,0},{5,1},{6,2},{7,3},{12,8},{13,9},{14,10},{15,11},{20,16},{21,... | collective-permute-start | bytes 1572872 | tf_op jit(solution)/shard_map/ppermute | solution.py:204
  29.3 3.1 %collective-permute-start.7 = (f32[128,128]{1,0:T(8,128)S(1)}, f32[128,128]{1,0:T(8,128)S(1)}, u32[]{:S(2)}, u32[]{:S(2)}) collective-permute-start(f32[128,128]{1,0:T(8,128)S(1)} %add.25.inverse_ref), channel_id=1, source_target_pairs={{0,4},{1,5},{2,6},{3,7},{8,12},{9,13},{10,14},{11,15},{16,20},{17,... | collective-permute-start | bytes 196616 | tf_op jit(solution)/shard_map/ppermute | solution.py:204
  32.4 0.9 %collective-permute-done.7.inverse_from_ref = f32[128,128]{1,0:T(8,128)S(1)} collective-permute-done((f32[128,128]{1,0:T(8,128)S(1)}, f32[128,128]{1,0:T(8,128)S(1)}, u32[]{:S(2)}, u32[]{:S(2)}) %collective-permute-start.7) | collective-permute-done | bytes 65568 | tf_op jit(solution)/shard_map/ppermute | solution.py:204
  33.3 3.9 %collective-permute-done.12.refs_2_ = f32[1024,128]{1,0:T(8,128)S(1)} collective-permute-done((f32[1024,128]{1,0:T(8,128)S(1)}, f32[1024,128]{1,0:T(8,128)S(1)}, u32[]{:S(2)}, u32[]{:S(2)}) %collective-permute-start.12) | collective-permute-done | bytes 524320 | tf_op jit(solution)/shard_map/ppermute | solution.py:204
  37.2 0.0 collective-permute-done.11.mirror_even_ref
  37.2 0.0 copy-done
  37.2 0.0 copy-done.1
  37.2 4.6 %update.1 = f32[1024,1024]{1,0:T(8,128)} custom-call(f32[128,128]{1,0:T(8,128)S(1)} %copy-done.1, f32[128,128]{1,0:T(8,128)S(1)} %add.25.inverse_ref, f32[128,128]{1,0:T(8,128)S(1)} %collective-permute-done.7.inverse_from_ref, f32[1024,1024]{1,0:T(8,128)S(1)} %copy-done, f32[1024,128]{1,0:T(8,128)S(1)} %collective-permute-done.11.mirror_even_ref, ...), custom_call_target="tpu_custom_call" | custom-call | flops 805306368 | bytes 8388608 | tf_op jit(solution)/shard_map/update/pallas_call | solution.py:168
  (6 shorter events, 0.1 us)
Async XLA Ops:
  0.7 36.6 %copy-start = (f32[1024,1024]{1,0:T(8,128)S(1)}, f32[1024,1024]{1,0:T(8,128)}, u32[]{:S(2)}) copy-start(f32[1024,1024]{1,0:T(8,128)} %matrix_ref.3) | copy-start | bytes 12582916
  0.7 36.5 %copy-start.1 = (f32[128,128]{1,0:T(8,128)S(1)}, f32[128,128]{1,0:T(8,128)}, u32[]{:S(2)}) copy-start(f32[128,128]{1,0:T(8,128)} %get-tuple-element.15.lower_ref) | copy-start | bytes 196612
  0.7 8.8 %collective-permute-start = (f32[128,128]{1,0:T(8,128)}, f32[128,128]{1,0:T(8,128)S(1)}, u32[]{:S(2)}, u32[]{:S(2)}) collective-permute-start(f32[128,128]{1,0:T(8,128)} %get-tuple-element.16), channel_id=1, source_target_pairs={{0,3}} | collective-permute-start | bytes 196616 | tf_op jit(solution)/shard_map/ppermute | solution.py:204
  10.3 4.5 %collective-permute-start.8 = (f32[512,128]{1,0:T(8,128)S(1)}, f32[512,128]{1,0:T(8,128)S(1)}, u32[]{:S(2)}, u32[]{:S(2)}) collective-permute-start(f32[512,128]{1,0:T(8,128)S(1)} %slice.8), channel_id=1, source_target_pairs={{0,4},{4,5},{8,14},{12,15},{16,20},{20,21},{24,30},{28,31}} | collective-permute-start | bytes 786440 | tf_op jit(solution)/shard_map/ppermute | solution.py:204
  11.0 3.8 %collective-permute-start.1 = (f32[128,128]{1,0:T(8,128)S(1)}, f32[128,128]{1,0:T(8,128)S(1)}, u32[]{:S(2)}, u32[]{:S(2)}) collective-permute-start(f32[128,128]{1,0:T(8,128)S(1)} %add.21), channel_id=1, source_target_pairs={{3,19}} | collective-permute-start | bytes 196616 | tf_op jit(solution)/shard_map/ppermute | solution.py:204
  13.4 9.3 %collective-permute-start.5 = (f32[1024,128]{1,0:T(8,128)S(1)}, f32[1024,128]{1,0:T(8,128)S(1)}, u32[]{:S(2)}, u32[]{:S(2)}) collective-permute-start(f32[1024,128]{1,0:T(8,128)S(1)} %slice.7), channel_id=1, source_target_pairs={{0,2},{4,6},{8,10},{12,14},{16,18},{20,22},{24,26},{28,30}} | collective-permute-start | bytes 1572872 | tf_op jit(solution)/shard_map/ppermute | solution.py:204
  14.1 8.6 %collective-permute-start.4 = (f32[1024,128]{1,0:T(8,128)S(1)}, f32[1024,128]{1,0:T(8,128)S(1)}, u32[]{:S(2)}, u32[]{:S(2)}) collective-permute-start(f32[1024,128]{1,0:T(8,128)S(1)} %slice.7), channel_id=1, source_target_pairs={{0,1},{4,5},{8,9},{12,13},{16,17},{20,21},{24,25},{28,29}} | collective-permute-start | bytes 1572872 | tf_op jit(solution)/shard_map/ppermute | solution.py:204
  14.9 7.1 %collective-permute-start.9 = (f32[512,128]{1,0:T(8,128)S(1)}, f32[512,128]{1,0:T(8,128)S(1)}, u32[]{:S(2)}, u32[]{:S(2)}) collective-permute-start(f32[512,128]{1,0:T(8,128)S(1)} %collective-permute-done.8), channel_id=1, source_target_pairs={{4,12},{20,28},{5,13},{21,29},{14,6},{30,22},{15,7},{31,23}} | collective-permute-start | bytes 786440 | tf_op jit(solution)/shard_map/ppermute | solution.py:204
  15.5 3.2 %collective-permute-start.2 = (f32[128,128]{1,0:T(8,128)S(1)}, f32[128,128]{1,0:T(8,128)S(1)}, u32[]{:S(2)}, u32[]{:S(2)}) collective-permute-start(f32[128,128]{1,0:T(8,128)S(1)} %add.22), channel_id=1, source_target_pairs={{3,11},{19,27}} | collective-permute-start | bytes 196616 | tf_op jit(solution)/shard_map/ppermute | solution.py:204
  18.7 3.2 %collective-permute-start.3 = (f32[128,128]{1,0:T(8,128)S(1)}, f32[128,128]{1,0:T(8,128)S(1)}, u32[]{:S(2)}, u32[]{:S(2)}) collective-permute-start(f32[128,128]{1,0:T(8,128)S(1)} %add.23), channel_id=1, source_target_pairs={{3,2},{19,18},{11,10},{27,26}} | collective-permute-start | bytes 196616 | tf_op jit(solution)/shard_map/ppermute | solution.py:204
  22.0 6.0 %collective-permute-start.10 = (f32[512,128]{1,0:T(8,128)S(1)}, f32[512,128]{1,0:T(8,128)S(1)}, u32[]{:S(2)}, u32[]{:S(2)}) collective-permute-start(f32[512,128]{1,0:T(8,128)S(1)} %add.26), channel_id=1, source_target_pairs={{20,4},{4,20},{21,5},{5,21},{30,14},{14,30},{31,15},{15,31},{28,12... | collective-permute-start | bytes 786440 | tf_op jit(solution)/shard_map/ppermute | solution.py:204
  22.7 5.3 %collective-permute-start.6 = (f32[128,128]{1,0:T(8,128)S(1)}, f32[128,128]{1,0:T(8,128)S(1)}, u32[]{:S(2)}, u32[]{:S(2)}) collective-permute-start(f32[128,128]{1,0:T(8,128)S(1)} %add.24), channel_id=1, source_target_pairs={{3,1},{19,17},{11,9},{27,25},{18,16},{10,8},{26,24}} | collective-permute-start | bytes 196616 | tf_op jit(solution)/shard_map/ppermute | solution.py:204
  26.1 11.1 %collective-permute-start.12 = (f32[1024,128]{1,0:T(8,128)S(1)}, f32[1024,128]{1,0:T(8,128)S(1)}, u32[]{:S(2)}, u32[]{:S(2)}) collective-permute-start(f32[1024,128]{1,0:T(8,128)S(1)} %add.27), channel_id=1, source_target_pairs={{1,3},{6,7},{9,11},{14,15},{17,19},{22,23},{25,27},{30,31}} | collective-permute-start | bytes 1572872 | tf_op jit(solution)/shard_map/ppermute | solution.py:204
  28.0 9.2 %collective-permute-start.11 = (f32[1024,128]{1,0:T(8,128)S(1)}, f32[1024,128]{1,0:T(8,128)S(1)}, u32[]{:S(2)}, u32[]{:S(2)}) collective-permute-start(f32[1024,128]{1,0:T(8,128)S(1)} %pad_maximum_fusion.mirror_odd_ref), channel_id=1, source_target_pairs={{4,0},{5,1},{6,2},{7,3},{12,8},{13,9},{14,10},{15,11},{20,16},{21,... | collective-permute-start | bytes 1572872 | tf_op jit(solution)/shard_map/ppermute | solution.py:204
  29.3 4.0 %collective-permute-start.7 = (f32[128,128]{1,0:T(8,128)S(1)}, f32[128,128]{1,0:T(8,128)S(1)}, u32[]{:S(2)}, u32[]{:S(2)}) collective-permute-start(f32[128,128]{1,0:T(8,128)S(1)} %add.25.inverse_ref), channel_id=1, source_target_pairs={{0,4},{1,5},{2,6},{3,7},{8,12},{9,13},{10,14},{11,15},{16,20},{17,... | collective-permute-start | bytes 196616 | tf_op jit(solution)/shard_map/ppermute | solution.py:204

commit v7 on v6

--- a/solution.py
+++ b/solution.py
@@ -14,20 +14,24 @@
 TRANS_B = (((1,), (1,)), ((), ()))
 
 
-def factor_kernel(matrix_ref, lower_ref, inverse_ref, corner_ref, sem):
+def factor_kernel(matrix_ref, lower_ref, inverse_ref, column_ref, half_ref, corner_ref, sems):
     works = (lax.axis_index("row") == 0) & (lax.axis_index("col") == 0)
-
-    @pl.when(jnp.logical_not(works))
-    def _():
-        lower_ref[...] = jnp.zeros_like(lower_ref)
-        inverse_ref[...] = jnp.zeros_like(inverse_ref)
+    first = pl.ds(0, NB)
+    copies = [
+        pltpu.make_async_copy(matrix_ref.at[first, first], corner_ref, sems.at[0]),
+        pltpu.make_async_copy(matrix_ref.at[pl.ds(0, half_ref.shape[0]), first], half_ref, sems.at[1]),
+        pltpu.make_async_copy(matrix_ref.at[:, first], column_ref, sems.at[2]),
+    ]
+    for copy in copies:
+        copy.start()
+    copies[0].wait()
 
     @pl.when(works)
     def _():
-        copy = pltpu.make_async_copy(matrix_ref.at[pl.ds(0, NB), pl.ds(0, NB)], corner_ref, sem)
-        copy.start()
+        eliminate(corner_ref, lower_ref, inverse_ref)
+
+    for copy in copies[1:]:
         copy.wait()
-        eliminate(corner_ref, lower_ref, inverse_ref)
 
 
 def eliminate(corner_ref, lower_ref, inverse_ref):
@@ -76,13 +80,15 @@
     inverse_ref[...] = jnp.where(rows >= cols, unit_inverse * scale, 0.0)
 
 
-def factor(matrix):
+def factor(matrix, half):
+    square = jax.ShapeDtypeStruct((NB, NB), jnp.float32)
+    tall = [jax.ShapeDtypeStruct((rows, NB), jnp.float32) for rows in (matrix.shape[0], half)]
     return pl.pallas_call(
         factor_kernel,
-        out_shape=[jax.ShapeDtypeStruct((NB, NB), jnp.float32)] * 2,
+        out_shape=[square, square, *tall],
         in_specs=[pl.BlockSpec(memory_space=pltpu.HBM)],
-        out_specs=[pl.BlockSpec(memory_space=pltpu.VMEM)] * 2,
-        scratch_shapes=[pltpu.VMEM((NB, NB), jnp.float32), pltpu.SemaphoreType.DMA],
+        out_specs=[pl.BlockSpec(memory_space=pltpu.VMEM)] * 2 + [pl.BlockSpec(memory_space=pltpu.VMEM)] * 2,
+        scratch_shapes=[pltpu.VMEM((NB, NB), jnp.float32), pltpu.SemaphoreType.DMA((3,))],
         compiler_params=pltpu.CompilerParams(vmem_limit_bytes=62 * 1024 * 1024),
         cost_estimate=pl.CostEstimate(flops=4_000_000, bytes_accessed=200_000, transcendentals=0),
         name="factor",
@@ -183,99 +189,65 @@
         name="update",
     )(lower, *inverses, matrix, *mirrors, *panels)
 
-
-TIES = {'mode': 'Y', 'A': 0, 'E1': 0, 'E2': 0, 'E3': None, 'M1': 1, 'M2': 3, 'X1': 4, 'need': {4: [1, 2]}, 'X1need': False}
-
-
 def body(matrix):
     rows_here = lax.axis_size("row")
     cols_here = lax.axis_size("col")
     row_index = lax.axis_index("row")
     col_index = lax.axis_index("col")
-    col_blocks = matrix.shape[1] // NB
     sources = rows_here // cols_here
+    every_row = range(rows_here)
+    odd_rows = range(1, rows_here, 2)
     last = cols_here - 1
-    every_row = range(rows_here)
-    even_rows = range(0, rows_here, 2)
-    odd_rows = range(1, rows_here, 2)
-    T = TIES
 
     def send(value, pairs):
         return lax.ppermute(value, AXES, [(a * cols_here + b, c * cols_here + d) for (a, b), (c, d) in pairs])
 
-    def after(value, *others):
-        return lax.optimization_barrier((value, *others))[0]
-
-    column = matrix[:, :NB]
-    half = NB * (col_blocks // sources)
-    first = column[:half]
-    if T["mode"] == "Y":
-        lower, inverse = factor(matrix)
-    else:
-        inverse = jnp.where((row_index == 0) & (col_index == 0), matrix[:NB, :NB], 0.0)
-    inverse = inverse + send(inverse, [((0, 0), (0, last))])
-    along = [inverse]
-    bulk = {}
-
-    def tie(value, name):
-        t = T[name]
-        return value if t is None or t >= len(along) else after(value, along[t])
-
-    def try_bulk():
-        if "A" not in bulk and T["A"] < len(along):
-            bulk["A"] = send(tie(first, "A"), [((r, 0), (r | 1, r % cols_here)) for r in every_row])
-        if 1 not in bulk and T["E1"] < len(along):
-            merged = tie(column, "E1")
-            step = 1
-            while step < cols_here:
-                base = [(r, c) for r in every_row for c in range(step)]
-                near = send(merged, [((r, c), (r, c + step)) for r, c in base])
-                far = send(merged, [((r, c), (r, c + 2 * step)) for r, c in base])
-                both = near + far
-                if T["E3"] is not None and T["E3"] < len(along): both = after(both, along[T["E3"]])
-                relay = send(both, [((r, c + step * (1 + r % 2)), (r, c + 3 * step)) for r, c in base])
-                for c in range(step):
-                    bulk[c + step], bulk[c + 2 * step], bulk[c + 3 * step] = near, far, relay
-                step *= 4
-                if step < cols_here:
-                    merged = jnp.where(col_index == 0, column, 0.0) + sum({id(v): v for k, v in bulk.items() if k != "A"}.values())
-
+    lower, inverse, column, first = factor(matrix, matrix.shape[1] // sources)
+    lower = jnp.where((row_index == 0) & (col_index == 0), lower, 0.0)
+
+    mirror = send(first, [((r, 0), (r | 1, r % cols_here)) for r in every_row])
+
+    panels = [None] * last
+    straight = []
+    merged = column
+    step = 1
+    while step < cols_here:
+        base = [(r, c) for r in every_row for c in range(step)]
+        near = send(merged, [((r, c), (r, c + step)) for r, c in base])
+        far = send(merged, [((r, c), (r, c + 2 * step)) for r, c in base])
+        relayed = send(near + far, [((r, c + step * (1 + r % 2)), (r, c + 3 * step)) for r, c in base])
+        straight += [near, far]
+        for c in range(step):
+            panels[c + step - 1], panels[c + 2 * step - 1], panels[c + 3 * step - 1] = near, far, relayed
+        merged = merged + near + far + relayed if step > 1 else (
+            jnp.where(col_index == 0, column, 0.0) + near + far + relayed)
+        step *= 4
+
+    inverse = send(inverse, [((0, 0), (0, last))])
     holders = [(0, last)]
     hops = [(1 << b, 0) for b in reversed(range(1, rows_here.bit_length() - 1))]
     hops += [(0, 1 << b) for b in range(cols_here.bit_length() - 1)]
-    for n, (dr, dc) in enumerate(hops):
-        try_bulk()
-        need = [bulk[k] for k in T["need"].get(n + 1, []) if k in bulk]
-        if need:
-            inverse, *got = lax.optimization_barrier((inverse, *need))
-            for k, v in zip([k for k in T["need"][n + 1] if k in bulk], got): bulk[k] = v
+    along = [inverse]
+    for dr, dc in hops:
+        if len(along) == len(hops):
+            inverse = lax.optimization_barrier((inverse, *straight))[0]
         moved = [(r + dr, c - dc) for r, c in holders]
-        inverse = inverse + send(inverse, [(h, m) for h, m in zip(holders, moved) if m != (0, 0)])
+        inverse = inverse + send(inverse, list(zip(holders, moved)))
         holders = holders + moved
         along.append(inverse)
-    try_bulk()
-    panels = [bulk[c] for c in range(1, cols_here)]
-
-    mirror = bulk["A"]
+
+    mirror, lower = lax.optimization_barrier((mirror, lower, along[1]))[:2]
     holders = [((c + q * cols_here) | 1, c) for c in range(cols_here) for q in range(sources)]
-    mirror = tie(mirror, "M1")
     for bit in (1 << b for b in range(1, cols_here.bit_length() - 1)):
         moved = [(r ^ bit, c) for r, c in holders]
         mirror = mirror + send(mirror, list(zip(holders, moved)))
         holders = holders + moved
-    mirror = tie(mirror, "M2")
+    mirror = lax.optimization_barrier((mirror, along[-2]))[0]
     mirror = jnp.concatenate([mirror] + [
         send(mirror, [(((r + q * cols_here) % rows_here, c), (r, c)) for r, c in holders])
         for q in range(1, sources)], axis=0)
-    need = T["need"].get(5, [])
-    if need:
-        inverse, *got = lax.optimization_barrier((inverse, *[panels[k - 1] for k in need]))
-        for k, v in zip(need, got): panels[k - 1] = v
-    if T.get("X1need"):
-        mirror, *panels = lax.optimization_barrier((mirror, *panels))
-    mirror = tie(mirror, "X1")
-    if T["mode"] == "X":
-        lower, inverse = factor(inverse)
+    mirror = lax.optimization_barrier((mirror, inverse))[0]
+
     down = [((r, c), (r - 1, c)) for r in odd_rows for c in range(cols_here)]
     mirrors = [send(mirror, down), mirror]
     inverses = [inverse, send(inverse, [(b, a) for a, b in down])]

time: 42.6 us -> 40.5 us (0.951); the launches traced: 41.8 us -> 40.2 us
  local copies, waits for them, and re-layouts: 2.06 us -> 0.01 us
  Pallas kernels: 5.25 us -> 6.71 us
  other arithmetic: 1.01 us -> 0.19 us
    slice x2 -> x0, local copies, waits for them, and re-layouts: 2.05 us -> none  [the longest x1 1.08 us: body(): column = matrix[:, :NB]]
    pallas_call x1, Pallas kernels: 0.66 us -> 2.14 us  [factor(): pl.pallas_call(factor_kernel, out_shape=[square, square, *tall], in_specs...]
    add x6 -> x5, other arithmetic: 0.94 us -> 0.09 us  [the longest x1 0.06 us: body(): near + far]
  transfers between devices with their start and end apart: 13 -> 13, of which waited for: 6 -> 7; matrix products, arithmetic and copies ran while one was open for 5% -> 0% of each run, Pallas kernels for 0% -> 0%
where the time goes in v7:
time: 40.5 us; the launch traced here: 40.2 us
  starting transfers between devices  17.8 us (44%)
  waiting for transfers between devices  15.3 us (38%)
  Pallas kernels  6.71 us (17%)
    ppermute x13, starting transfers between devices, send(): lax.ppermute(value, AXES, [(a * cols_here + b, c * cols_here + d) for (a,...  17.8 us
    ppermute x13, waiting for transfers between devices, send(): lax.ppermute(value, AXES, [(a * cols_here + b, c * cols_here + d) for (a,...  15.3 us
    pallas_call x1, Pallas kernels, update(): pl.pallas_call(functools.partial(update_kernel, plan), out_shape=jax.Shap...  4.57 us
    pallas_call x1, Pallas kernels, factor(): pl.pallas_call(factor_kernel, out_shape=[square, square, *tall], in_specs...  2.14 us
  transfers between devices with their start and end apart: 13, of which 7 were waited for; matrix products, arithmetic and copies ran while one was open for 0% of the time, Pallas kernels for 0%

profile of v7, /device:TPU:6, one launch (start us, length us, event | category | flops | bytes accessed | tf_op | source)
XLA Modules:
  0.0 40.2 jit_solution(12351520725272996909)
XLA Ops:
  0.0 2.1 %factor.1 = (f32[128,128]{1,0:T(8,128)}, f32[128,128]{1,0:T(8,128)}, f32[1024,128]{1,0:T(8,128)}, f32[512,128]{1,0:T(8,128)}) custom-call(f32[1024,1024]{1,0:T(8,128)} %matrix_ref.3), custom_call_target="tpu_custom_call" | custom-call | flops 4000000 | bytes 200000 | tf_op jit(solution)/shard_map/factor/pallas_call | solution.py:86
  2.2 1.3 %collective-permute-start.1 = (f32[128,128]{1,0:T(8,128)}, f32[128,128]{1,0:T(8,128)S(1)}, u32[]{:S(2)}, u32[]{:S(2)}) collective-permute-start(f32[128,128]{1,0:T(8,128)} %get-tuple-element.16), channel_id=1, source_target_pairs={{0,3}} | collective-permute-start | bytes 196616 | tf_op jit(solution)/shard_map/ppermute | solution.py:203
  3.5 0.7 %collective-permute-start = (f32[512,128]{1,0:T(8,128)}, f32[512,128]{1,0:T(8,128)S(1)}, u32[]{:S(2)}, u32[]{:S(2)}) collective-permute-start(f32[512,128]{1,0:T(8,128)} %get-tuple-element.14), channel_id=1, source_target_pairs={{0,4},{4,5},{8,14},{12,15},{16,20},{20,21},{24,30},{28,31}} | collective-permute-start | bytes 786440 | tf_op jit(solution)/shard_map/ppermute | solution.py:203
  4.1 0.7 %collective-permute-start.6 = (f32[1024,128]{1,0:T(8,128)}, f32[1024,128]{1,0:T(8,128)S(1)}, u32[]{:S(2)}, u32[]{:S(2)}) collective-permute-start(f32[1024,128]{1,0:T(8,128)} %get-tuple-element.18), channel_id=1, source_target_pairs={{0,2},{4,6},{8,10},{12,14},{16,18},{20,22},{24,26},{28,30}} | collective-permute-start | bytes 1572872 | tf_op jit(solution)/shard_map/ppermute | solution.py:203
  4.8 0.7 %collective-permute-start.5 = (f32[1024,128]{1,0:T(8,128)}, f32[1024,128]{1,0:T(8,128)S(1)}, u32[]{:S(2)}, u32[]{:S(2)}) collective-permute-start(f32[1024,128]{1,0:T(8,128)} %get-tuple-element.18), channel_id=1, source_target_pairs={{0,1},{4,5},{8,9},{12,13},{16,17},{20,21},{24,25},{28,29}} | collective-permute-start | bytes 1572872 | tf_op jit(solution)/shard_map/ppermute | solution.py:203
  5.6 0.0 copy-start
  5.6 4.6 %collective-permute-done.1 = f32[128,128]{1,0:T(8,128)S(1)} collective-permute-done((f32[128,128]{1,0:T(8,128)}, f32[128,128]{1,0:T(8,128)S(1)}, u32[]{:S(2)}, u32[]{:S(2)}) %collective-permute-start.1) | collective-permute-done | bytes 65568 | tf_op jit(solution)/shard_map/ppermute | solution.py:203
  10.2 1.3 %collective-permute-start.2 = (f32[128,128]{1,0:T(8,128)S(1)}, f32[128,128]{1,0:T(8,128)S(1)}, u32[]{:S(2)}, u32[]{:S(2)}) collective-permute-start(f32[128,128]{1,0:T(8,128)S(1)} %collective-permute-done.1), channel_id=1, source_target_pairs={{3,19}} | collective-permute-start | bytes 196616 | tf_op jit(solution)/shard_map/ppermute | solution.py:203
  11.5 1.9 %collective-permute-done.2 = f32[128,128]{1,0:T(8,128)S(1)} collective-permute-done((f32[128,128]{1,0:T(8,128)S(1)}, f32[128,128]{1,0:T(8,128)S(1)}, u32[]{:S(2)}, u32[]{:S(2)}) %collective-permute-start.2) | collective-permute-done | bytes 65568 | tf_op jit(solution)/shard_map/ppermute | solution.py:203
  13.4 0.0 collective-permute-done
  13.4 0.7 %collective-permute-start.9 = (f32[512,128]{1,0:T(8,128)S(1)}, f32[512,128]{1,0:T(8,128)S(1)}, u32[]{:S(2)}, u32[]{:S(2)}) collective-permute-start(f32[512,128]{1,0:T(8,128)S(1)} %collective-permute-done), channel_id=1, source_target_pairs={{4,12},{20,28},{5,13},{21,29},{14,6},{30,22},{15,7},{31,23}} | collective-permute-start | bytes 786440 | tf_op jit(solution)/shard_map/ppermute | solution.py:203
  14.1 1.3 %collective-permute-start.3 = (f32[128,128]{1,0:T(8,128)S(1)}, f32[128,128]{1,0:T(8,128)S(1)}, u32[]{:S(2)}, u32[]{:S(2)}) collective-permute-start(f32[128,128]{1,0:T(8,128)S(1)} %add.18), channel_id=1, source_target_pairs={{3,11},{19,27}} | collective-permute-start | bytes 196616 | tf_op jit(solution)/shard_map/ppermute | solution.py:203
  15.4 1.9 %collective-permute-done.3 = f32[128,128]{1,0:T(8,128)S(1)} collective-permute-done((f32[128,128]{1,0:T(8,128)S(1)}, f32[128,128]{1,0:T(8,128)S(1)}, u32[]{:S(2)}, u32[]{:S(2)}) %collective-permute-start.3) | collective-permute-done | bytes 65568 | tf_op jit(solution)/shard_map/ppermute | solution.py:203
  17.3 1.3 %collective-permute-start.4 = (f32[128,128]{1,0:T(8,128)S(1)}, f32[128,128]{1,0:T(8,128)S(1)}, u32[]{:S(2)}, u32[]{:S(2)}) collective-permute-start(f32[128,128]{1,0:T(8,128)S(1)} %add.19), channel_id=1, source_target_pairs={{3,2},{19,18},{11,10},{27,26}} | collective-permute-start | bytes 196616 | tf_op jit(solution)/shard_map/ppermute | solution.py:203
  18.6 1.9 %collective-permute-done.4 = f32[128,128]{1,0:T(8,128)S(1)} collective-permute-done((f32[128,128]{1,0:T(8,128)S(1)}, f32[128,128]{1,0:T(8,128)S(1)}, u32[]{:S(2)}, u32[]{:S(2)}) %collective-permute-start.4) | collective-permute-done | bytes 65568 | tf_op jit(solution)/shard_map/ppermute | solution.py:203
  20.5 0.0 collective-permute-done.9
  20.5 0.7 %collective-permute-start.10 = (f32[512,128]{1,0:T(8,128)S(1)}, f32[512,128]{1,0:T(8,128)S(1)}, u32[]{:S(2)}, u32[]{:S(2)}) collective-permute-start(f32[512,128]{1,0:T(8,128)S(1)} %add.22), channel_id=1, source_target_pairs={{20,4},{4,20},{21,5},{5,21},{30,14},{14,30},{31,15},{15,31},{28,12... | collective-permute-start | bytes 786440 | tf_op jit(solution)/shard_map/ppermute | solution.py:203
  21.2 0.0 collective-permute-done.6.refs_1_
  21.2 0.0 collective-permute-done.5.refs_0_
  21.2 3.3 %collective-permute-start.7 = (f32[128,128]{1,0:T(8,128)S(1)}, f32[128,128]{1,0:T(8,128)S(1)}, u32[]{:S(2)}, u32[]{:S(2)}) collective-permute-start(f32[128,128]{1,0:T(8,128)S(1)} %add.20), channel_id=1, source_target_pairs={{3,1},{19,17},{11,9},{27,25},{2,0},{18,16},{10,8},{26,24}} | collective-permute-start | bytes 196616 | tf_op jit(solution)/shard_map/ppermute | solution.py:203
  24.5 0.1 add.23
  24.6 1.3 %collective-permute-start.12 = (f32[1024,128]{1,0:T(8,128)S(1)}, f32[1024,128]{1,0:T(8,128)S(1)}, u32[]{:S(2)}, u32[]{:S(2)}) collective-permute-start(f32[1024,128]{1,0:T(8,128)S(1)} %add.23), channel_id=1, source_target_pairs={{1,3},{6,7},{9,11},{14,15},{17,19},{22,23},{25,27},{30,31}} | collective-permute-start | bytes 1572872 | tf_op jit(solution)/shard_map/ppermute | solution.py:203
  25.9 0.5 %collective-permute-done.7 = f32[128,128]{1,0:T(8,128)S(1)} collective-permute-done((f32[128,128]{1,0:T(8,128)S(1)}, f32[128,128]{1,0:T(8,128)S(1)}, u32[]{:S(2)}, u32[]{:S(2)}) %collective-permute-start.7) | collective-permute-done | bytes 65568 | tf_op jit(solution)/shard_map/ppermute | solution.py:203
  26.4 0.0 collective-permute-done.10
  26.5 1.3 %collective-permute-start.11 = (f32[1024,128]{1,0:T(8,128)S(1)}, f32[1024,128]{1,0:T(8,128)S(1)}, u32[]{:S(2)}, u32[]{:S(2)}) collective-permute-start(f32[1024,128]{1,0:T(8,128)S(1)} %pad_maximum_fusion.mirror_odd_ref), channel_id=1, source_target_pairs={{4,0},{5,1},{6,2},{7,3},{12,8},{13,9},{14,10},{15,11},{20,16},{21,... | collective-permute-start | bytes 1572872 | tf_op jit(solution)/shard_map/ppermute | solution.py:203
  27.8 3.3 %collective-permute-start.8 = (f32[128,128]{1,0:T(8,128)S(1)}, f32[128,128]{1,0:T(8,128)S(1)}, u32[]{:S(2)}, u32[]{:S(2)}) collective-permute-start(f32[128,128]{1,0:T(8,128)S(1)} %add.21.inverse_ref), channel_id=1, source_target_pairs={{0,4},{1,5},{2,6},{3,7},{8,12},{9,13},{10,14},{11,15},{16,20},{17,... | collective-permute-start | bytes 196616 | tf_op jit(solution)/shard_map/ppermute | solution.py:203
  31.1 0.9 %collective-permute-done.8.inverse_from_ref = f32[128,128]{1,0:T(8,128)S(1)} collective-permute-done((f32[128,128]{1,0:T(8,128)S(1)}, f32[128,128]{1,0:T(8,128)S(1)}, u32[]{:S(2)}, u32[]{:S(2)}) %collective-permute-start.8) | collective-permute-done | bytes 65568 | tf_op jit(solution)/shard_map/ppermute | solution.py:203
  32.0 3.7 %collective-permute-done.12.refs_2_ = f32[1024,128]{1,0:T(8,128)S(1)} collective-permute-done((f32[1024,128]{1,0:T(8,128)S(1)}, f32[1024,128]{1,0:T(8,128)S(1)}, u32[]{:S(2)}, u32[]{:S(2)}) %collective-permute-start.12) | collective-permute-done | bytes 524320 | tf_op jit(solution)/shard_map/ppermute | solution.py:203
  35.7 0.0 collective-permute-done.11.mirror_even_ref
  35.7 0.0 copy-done
  35.7 4.6 %update.1 = f32[1024,1024]{1,0:T(8,128)} custom-call(f32[128,128]{1,0:T(8,128)S(1)} %broadcast_select_fusion.lower_ref, f32[128,128]{1,0:T(8,128)S(1)} %add.21.inverse_ref, f32[128,128]{1,0:T(8,128)S(1)} %collective-permute-done.8.inverse_from_ref, f32[1024,1024]{1,0:T(8,128)S(1)} %copy-done, f32[1024,128]{1,0:T(8,128)S(1)} %collective-permute-done.11.mirror_even_ref, ...), custom_call_target="tpu_custom_call" | custom-call | flops 805306368 | bytes 8388608 | tf_op jit(solution)/shard_map/update/pallas_call | solution.py:174
  (7 shorter events, 0.1 us)
Async XLA Ops:
  2.2 8.0 %collective-permute-start.1 = (f32[128,128]{1,0:T(8,128)}, f32[128,128]{1,0:T(8,128)S(1)}, u32[]{:S(2)}, u32[]{:S(2)}) collective-permute-start(f32[128,128]{1,0:T(8,128)} %get-tuple-element.16), channel_id=1, source_target_pairs={{0,3}} | collective-permute-start | bytes 196616 | tf_op jit(solution)/shard_map/ppermute | solution.py:203
  3.5 9.9 %collective-permute-start = (f32[512,128]{1,0:T(8,128)}, f32[512,128]{1,0:T(8,128)S(1)}, u32[]{:S(2)}, u32[]{:S(2)}) collective-permute-start(f32[512,128]{1,0:T(8,128)} %get-tuple-element.14), channel_id=1, source_target_pairs={{0,4},{4,5},{8,14},{12,15},{16,20},{20,21},{24,30},{28,31}} | collective-permute-start | bytes 786440 | tf_op jit(solution)/shard_map/ppermute | solution.py:203
  4.1 17.1 %collective-permute-start.6 = (f32[1024,128]{1,0:T(8,128)}, f32[1024,128]{1,0:T(8,128)S(1)}, u32[]{:S(2)}, u32[]{:S(2)}) collective-permute-start(f32[1024,128]{1,0:T(8,128)} %get-tuple-element.18), channel_id=1, source_target_pairs={{0,2},{4,6},{8,10},{12,14},{16,18},{20,22},{24,26},{28,30}} | collective-permute-start | bytes 1572872 | tf_op jit(solution)/shard_map/ppermute | solution.py:203
  4.8 16.4 %collective-permute-start.5 = (f32[1024,128]{1,0:T(8,128)}, f32[1024,128]{1,0:T(8,128)S(1)}, u32[]{:S(2)}, u32[]{:S(2)}) collective-permute-start(f32[1024,128]{1,0:T(8,128)} %get-tuple-element.18), channel_id=1, source_target_pairs={{0,1},{4,5},{8,9},{12,13},{16,17},{20,21},{24,25},{28,29}} | collective-permute-start | bytes 1572872 | tf_op jit(solution)/shard_map/ppermute | solution.py:203
  5.6 30.1 %copy-start = (f32[1024,1024]{1,0:T(8,128)S(1)}, f32[1024,1024]{1,0:T(8,128)}, u32[]{:S(2)}) copy-start(f32[1024,1024]{1,0:T(8,128)} %matrix_ref.3) | copy-start | bytes 12582916
  10.2 3.2 %collective-permute-start.2 = (f32[128,128]{1,0:T(8,128)S(1)}, f32[128,128]{1,0:T(8,128)S(1)}, u32[]{:S(2)}, u32[]{:S(2)}) collective-permute-start(f32[128,128]{1,0:T(8,128)S(1)} %collective-permute-done.1), channel_id=1, source_target_pairs={{3,19}} | collective-permute-start | bytes 196616 | tf_op jit(solution)/shard_map/ppermute | solution.py:203
  13.4 7.1 %collective-permute-start.9 = (f32[512,128]{1,0:T(8,128)S(1)}, f32[512,128]{1,0:T(8,128)S(1)}, u32[]{:S(2)}, u32[]{:S(2)}) collective-permute-start(f32[512,128]{1,0:T(8,128)S(1)} %collective-permute-done), channel_id=1, source_target_pairs={{4,12},{20,28},{5,13},{21,29},{14,6},{30,22},{15,7},{31,23}} | collective-permute-start | bytes 786440 | tf_op jit(solution)/shard_map/ppermute | solution.py:203
  14.1 3.2 %collective-permute-start.3 = (f32[128,128]{1,0:T(8,128)S(1)}, f32[128,128]{1,0:T(8,128)S(1)}, u32[]{:S(2)}, u32[]{:S(2)}) collective-permute-start(f32[128,128]{1,0:T(8,128)S(1)} %add.18), channel_id=1, source_target_pairs={{3,11},{19,27}} | collective-permute-start | bytes 196616 | tf_op jit(solution)/shard_map/ppermute | solution.py:203
  17.3 3.2 %collective-permute-start.4 = (f32[128,128]{1,0:T(8,128)S(1)}, f32[128,128]{1,0:T(8,128)S(1)}, u32[]{:S(2)}, u32[]{:S(2)}) collective-permute-start(f32[128,128]{1,0:T(8,128)S(1)} %add.19), channel_id=1, source_target_pairs={{3,2},{19,18},{11,10},{27,26}} | collective-permute-start | bytes 196616 | tf_op jit(solution)/shard_map/ppermute | solution.py:203
  20.5 5.9 %collective-permute-start.10 = (f32[512,128]{1,0:T(8,128)S(1)}, f32[512,128]{1,0:T(8,128)S(1)}, u32[]{:S(2)}, u32[]{:S(2)}) collective-permute-start(f32[512,128]{1,0:T(8,128)S(1)} %add.22), channel_id=1, source_target_pairs={{20,4},{4,20},{21,5},{5,21},{30,14},{14,30},{31,15},{15,31},{28,12... | collective-permute-start | bytes 786440 | tf_op jit(solution)/shard_map/ppermute | solution.py:203
  21.2 5.2 %collective-permute-start.7 = (f32[128,128]{1,0:T(8,128)S(1)}, f32[128,128]{1,0:T(8,128)S(1)}, u32[]{:S(2)}, u32[]{:S(2)}) collective-permute-start(f32[128,128]{1,0:T(8,128)S(1)} %add.20), channel_id=1, source_target_pairs={{3,1},{19,17},{11,9},{27,25},{2,0},{18,16},{10,8},{26,24}} | collective-permute-start | bytes 196616 | tf_op jit(solution)/shard_map/ppermute | solution.py:203
  24.6 11.1 %collective-permute-start.12 = (f32[1024,128]{1,0:T(8,128)S(1)}, f32[1024,128]{1,0:T(8,128)S(1)}, u32[]{:S(2)}, u32[]{:S(2)}) collective-permute-start(f32[1024,128]{1,0:T(8,128)S(1)} %add.23), channel_id=1, source_target_pairs={{1,3},{6,7},{9,11},{14,15},{17,19},{22,23},{25,27},{30,31}} | collective-permute-start | bytes 1572872 | tf_op jit(solution)/shard_map/ppermute | solution.py:203
  26.5 9.2 %collective-permute-start.11 = (f32[1024,128]{1,0:T(8,128)S(1)}, f32[1024,128]{1,0:T(8,128)S(1)}, u32[]{:S(2)}, u32[]{:S(2)}) collective-permute-start(f32[1024,128]{1,0:T(8,128)S(1)} %pad_maximum_fusion.mirror_odd_ref), channel_id=1, source_target_pairs={{4,0},{5,1},{6,2},{7,3},{12,8},{13,9},{14,10},{15,11},{20,16},{21,... | collective-permute-start | bytes 1572872 | tf_op jit(solution)/shard_map/ppermute | solution.py:203
  27.8 4.2 %collective-permute-start.8 = (f32[128,128]{1,0:T(8,128)S(1)}, f32[128,128]{1,0:T(8,128)S(1)}, u32[]{:S(2)}, u32[]{:S(2)}) collective-permute-start(f32[128,128]{1,0:T(8,128)S(1)} %add.21.inverse_ref), channel_id=1, source_target_pairs={{0,4},{1,5},{2,6},{3,7},{8,12},{9,13},{10,14},{11,15},{16,20},{17,... | collective-permute-start | bytes 196616 | tf_op jit(solution)/shard_map/ppermute | solution.py:203

commit v8 on v7

--- a/solution.py
+++ b/solution.py
@@ -133,20 +133,20 @@
     inverse = inverse_ref[...] + inverse_from_ref[...]
     for t in range(col_blocks):
         block = (t % sources) * each + (t // sources) * NB
-        part = lax.dot_general(inverse, mirror[pl.ds(block, NB), :], TRANS_B, precision=HIGHEST,
+        part = lax.dot_general(mirror[pl.ds(block, NB), :], inverse, TRANS_B, precision=HIGHEST,
                                preferred_element_type=jnp.float32)
         high, low = split(part)
         at = pl.ds(t * NB, NB)
-        rhs[pl.ds(0, NB), at] = high
-        rhs[pl.ds(NB, NB), at] = high
-        rhs[pl.ds(2 * NB, NB), at] = low
+        rhs[at, pl.ds(0, NB)] = high
+        rhs[at, pl.ds(NB, NB)] = high
+        rhs[at, pl.ds(2 * NB, NB)] = low
 
     for i in range(tiles):
         tall = lax.dot_general(panel[here[i], :], inverse, TRANS_B, precision=HIGHEST,
                                preferred_element_type=jnp.float32)
         high, low = split(tall)
         lhs = jnp.concatenate([high, low, high], axis=1)
-        product = jnp.dot(lhs, rhs[...], preferred_element_type=jnp.float32)
+        product = lax.dot_general(lhs, rhs[...], TRANS_B, preferred_element_type=jnp.float32)
         for s in range(TILE // NB):
             row = (i * (TILE // NB) + s) * rows_here + row_index
             down = pl.ds(i * TILE + s * NB, NB)
@@ -180,7 +180,7 @@
             pltpu.VMEM((height, width), jnp.float32),
             pltpu.VMEM((height, NB), jnp.float32),
             pltpu.VMEM((width, NB), jnp.float32),
-            pltpu.VMEM((3 * NB, width), jnp.bfloat16),
+            pltpu.VMEM((width, 3 * NB), jnp.bfloat16),
             pltpu.SemaphoreType.DMA((tiles,)),
         ],
         compiler_params=pltpu.CompilerParams(vmem_limit_bytes=28 * 1024 * 1024),
@@ -215,8 +215,10 @@
         base = [(r, c) for r in every_row for c in range(step)]
         near = send(merged, [((r, c), (r, c + step)) for r, c in base])
         far = send(merged, [((r, c), (r, c + 2 * step)) for r, c in base])
-        relayed = send(near + far, [((r, c + step * (1 + r % 2)), (r, c + 3 * step)) for r, c in base])
-        straight += [near, far]
+        both = near + far
+        straight += [both]
+        relayed = send(both, [((r, c + step * (1 + r % 2)), (r, c + 3 * step)) for r, c in base])
+        straight += []
         for c in range(step):
             panels[c + step - 1], panels[c + 2 * step - 1], panels[c + 3 * step - 1] = near, far, relayed
         merged = merged + near + far + relayed if step > 1 else (
@@ -242,7 +244,6 @@
         moved = [(r ^ bit, c) for r, c in holders]
         mirror = mirror + send(mirror, list(zip(holders, moved)))
         holders = holders + moved
-    mirror = lax.optimization_barrier((mirror, along[-2]))[0]
     mirror = jnp.concatenate([mirror] + [
         send(mirror, [(((r + q * cols_here) % rows_here, c), (r, c)) for r, c in holders])
         for q in range(1, sources)], axis=0)

time: 40.5 us -> 40.4 us (level)
  no operation moved by 1% of the time
where the time goes in v8:
time: 40.4 us; the launch traced here: 40.1 us
  starting transfers between devices  17.7 us (44%)
  waiting for transfers between devices  15.4 us (38%)
  Pallas kernels  6.57 us (16%)
    ppermute x13, starting transfers between devices, send(): lax.ppermute(value, AXES, [(a * cols_here + b, c * cols_here + d) for (a,...  17.7 us
    ppermute x13, waiting for transfers between devices, send(): lax.ppermute(value, AXES, [(a * cols_here + b, c * cols_here + d) for (a,...  15.4 us
    pallas_call x1, Pallas kernels, update(): pl.pallas_call(functools.partial(update_kernel, plan), out_shape=jax.Shap...  4.42 us
    pallas_call x1, Pallas kernels, factor(): pl.pallas_call(factor_kernel, out_shape=[square, square, *tall], in_specs...  2.14 us
  transfers between devices with their start and end apart: 13, of which 7 were waited for; matrix products, arithmetic and copies ran while one was open for 0% of the time, Pallas kernels for 0%

profile of v8, /device:TPU:6, one launch (start us, length us, event | category | flops | bytes accessed | tf_op | source)
XLA Modules:
  0.0 40.1 jit_solution(14016683156395295995)
XLA Ops:
  0.0 2.1 %factor.1 = (f32[128,128]{1,0:T(8,128)}, f32[128,128]{1,0:T(8,128)}, f32[1024,128]{1,0:T(8,128)}, f32[512,128]{1,0:T(8,128)}) custom-call(f32[1024,1024]{1,0:T(8,128)} %matrix_ref.3), custom_call_target="tpu_custom_call" | custom-call | flops 4000000 | bytes 200000 | tf_op jit(solution)/shard_map/factor/pallas_call | solution.py:86
  2.2 1.3 %collective-permute-start.1 = (f32[128,128]{1,0:T(8,128)}, f32[128,128]{1,0:T(8,128)S(1)}, u32[]{:S(2)}, u32[]{:S(2)}) collective-permute-start(f32[128,128]{1,0:T(8,128)} %get-tuple-element.15), channel_id=1, source_target_pairs={{0,3}} | collective-permute-start | bytes 196616 | tf_op jit(solution)/shard_map/ppermute | solution.py:203
  3.5 0.7 %collective-permute-start = (f32[512,128]{1,0:T(8,128)}, f32[512,128]{1,0:T(8,128)S(1)}, u32[]{:S(2)}, u32[]{:S(2)}) collective-permute-start(f32[512,128]{1,0:T(8,128)} %get-tuple-element.13), channel_id=1, source_target_pairs={{0,4},{4,5},{8,14},{12,15},{16,20},{20,21},{24,30},{28,31}} | collective-permute-start | bytes 786440 | tf_op jit(solution)/shard_map/ppermute | solution.py:203
  4.1 0.7 %collective-permute-start.6 = (f32[1024,128]{1,0:T(8,128)}, f32[1024,128]{1,0:T(8,128)S(1)}, u32[]{:S(2)}, u32[]{:S(2)}) collective-permute-start(f32[1024,128]{1,0:T(8,128)} %get-tuple-element.17), channel_id=1, source_target_pairs={{0,2},{4,6},{8,10},{12,14},{16,18},{20,22},{24,26},{28,30}} | collective-permute-start | bytes 1572872 | tf_op jit(solution)/shard_map/ppermute | solution.py:203
  4.8 0.7 %collective-permute-start.5 = (f32[1024,128]{1,0:T(8,128)}, f32[1024,128]{1,0:T(8,128)S(1)}, u32[]{:S(2)}, u32[]{:S(2)}) collective-permute-start(f32[1024,128]{1,0:T(8,128)} %get-tuple-element.17), channel_id=1, source_target_pairs={{0,1},{4,5},{8,9},{12,13},{16,17},{20,21},{24,25},{28,29}} | collective-permute-start | bytes 1572872 | tf_op jit(solution)/shard_map/ppermute | solution.py:203
  5.6 0.0 copy-start
  5.6 4.6 %collective-permute-done.1 = f32[128,128]{1,0:T(8,128)S(1)} collective-permute-done((f32[128,128]{1,0:T(8,128)}, f32[128,128]{1,0:T(8,128)S(1)}, u32[]{:S(2)}, u32[]{:S(2)}) %collective-permute-start.1) | collective-permute-done | bytes 65568 | tf_op jit(solution)/shard_map/ppermute | solution.py:203
  10.2 1.3 %collective-permute-start.2 = (f32[128,128]{1,0:T(8,128)S(1)}, f32[128,128]{1,0:T(8,128)S(1)}, u32[]{:S(2)}, u32[]{:S(2)}) collective-permute-start(f32[128,128]{1,0:T(8,128)S(1)} %collective-permute-done.1), channel_id=1, source_target_pairs={{3,19}} | collective-permute-start | bytes 196616 | tf_op jit(solution)/shard_map/ppermute | solution.py:203
  11.5 1.9 %collective-permute-done.2 = f32[128,128]{1,0:T(8,128)S(1)} collective-permute-done((f32[128,128]{1,0:T(8,128)S(1)}, f32[128,128]{1,0:T(8,128)S(1)}, u32[]{:S(2)}, u32[]{:S(2)}) %collective-permute-start.2) | collective-permute-done | bytes 65568 | tf_op jit(solution)/shard_map/ppermute | solution.py:203
  13.4 0.0 collective-permute-done
  13.4 0.7 %collective-permute-start.9 = (f32[512,128]{1,0:T(8,128)S(1)}, f32[512,128]{1,0:T(8,128)S(1)}, u32[]{:S(2)}, u32[]{:S(2)}) collective-permute-start(f32[512,128]{1,0:T(8,128)S(1)} %collective-permute-done), channel_id=1, source_target_pairs={{4,12},{20,28},{5,13},{21,29},{14,6},{30,22},{15,7},{31,23}} | collective-permute-start | bytes 786440 | tf_op jit(solution)/shard_map/ppermute | solution.py:203
  14.1 0.0 collective-permute-done.9
  14.1 0.7 %collective-permute-start.10 = (f32[512,128]{1,0:T(8,128)S(1)}, f32[512,128]{1,0:T(8,128)S(1)}, u32[]{:S(2)}, u32[]{:S(2)}) collective-permute-start(f32[512,128]{1,0:T(8,128)S(1)} %add.23), channel_id=1, source_target_pairs={{20,4},{4,20},{21,5},{5,21},{30,14},{14,30},{31,15},{15,31},{28,12... | collective-permute-start | bytes 786440 | tf_op jit(solution)/shard_map/ppermute | solution.py:203
  14.8 1.3 %collective-permute-start.3 = (f32[128,128]{1,0:T(8,128)S(1)}, f32[128,128]{1,0:T(8,128)S(1)}, u32[]{:S(2)}, u32[]{:S(2)}) collective-permute-start(f32[128,128]{1,0:T(8,128)S(1)} %add.18), channel_id=1, source_target_pairs={{3,11},{19,27}} | collective-permute-start | bytes 196616 | tf_op jit(solution)/shard_map/ppermute | solution.py:203
  16.1 1.9 %collective-permute-done.3 = f32[128,128]{1,0:T(8,128)S(1)} collective-permute-done((f32[128,128]{1,0:T(8,128)S(1)}, f32[128,128]{1,0:T(8,128)S(1)}, u32[]{:S(2)}, u32[]{:S(2)}) %collective-permute-start.3) | collective-permute-done | bytes 65568 | tf_op jit(solution)/shard_map/ppermute | solution.py:203
  18.0 1.3 %collective-permute-start.4 = (f32[128,128]{1,0:T(8,128)S(1)}, f32[128,128]{1,0:T(8,128)S(1)}, u32[]{:S(2)}, u32[]{:S(2)}) collective-permute-start(f32[128,128]{1,0:T(8,128)S(1)} %add.19), channel_id=1, source_target_pairs={{3,2},{19,18},{11,10},{27,26}} | collective-permute-start | bytes 196616 | tf_op jit(solution)/shard_map/ppermute | solution.py:203
  19.3 1.9 %collective-permute-done.4 = f32[128,128]{1,0:T(8,128)S(1)} collective-permute-done((f32[128,128]{1,0:T(8,128)S(1)}, f32[128,128]{1,0:T(8,128)S(1)}, u32[]{:S(2)}, u32[]{:S(2)}) %collective-permute-start.4) | collective-permute-done | bytes 65568 | tf_op jit(solution)/shard_map/ppermute | solution.py:203
  21.2 0.0 collective-permute-done.6.refs_1_
  21.2 0.0 collective-permute-done.5.refs_0_
  21.2 0.1 add.21
  21.3 3.3 %collective-permute-start.7 = (f32[128,128]{1,0:T(8,128)S(1)}, f32[128,128]{1,0:T(8,128)S(1)}, u32[]{:S(2)}, u32[]{:S(2)}) collective-permute-start(f32[128,128]{1,0:T(8,128)S(1)} %add.20), channel_id=1, source_target_pairs={{3,1},{19,17},{11,9},{27,25},{2,0},{18,16},{10,8},{26,24}} | collective-permute-start | bytes 196616 | tf_op jit(solution)/shard_map/ppermute | solution.py:203
  24.6 1.3 %collective-permute-start.12 = (f32[1024,128]{1,0:T(8,128)S(1)}, f32[1024,128]{1,0:T(8,128)S(1)}, u32[]{:S(2)}, u32[]{:S(2)}) collective-permute-start(f32[1024,128]{1,0:T(8,128)S(1)} %add.21), channel_id=1, source_target_pairs={{1,3},{6,7},{9,11},{14,15},{17,19},{22,23},{25,27},{30,31}} | collective-permute-start | bytes 1572872 | tf_op jit(solution)/shard_map/ppermute | solution.py:203
  25.9 0.6 %collective-permute-done.7 = f32[128,128]{1,0:T(8,128)S(1)} collective-permute-done((f32[128,128]{1,0:T(8,128)S(1)}, f32[128,128]{1,0:T(8,128)S(1)}, u32[]{:S(2)}, u32[]{:S(2)}) %collective-permute-start.7) | collective-permute-done | bytes 65568 | tf_op jit(solution)/shard_map/ppermute | solution.py:203
  26.5 0.0 collective-permute-done.10
  26.5 1.3 %collective-permute-start.11 = (f32[1024,128]{1,0:T(8,128)S(1)}, f32[1024,128]{1,0:T(8,128)S(1)}, u32[]{:S(2)}, u32[]{:S(2)}) collective-permute-start(f32[1024,128]{1,0:T(8,128)S(1)} %pad_maximum_fusion.mirror_odd_ref), channel_id=1, source_target_pairs={{4,0},{5,1},{6,2},{7,3},{12,8},{13,9},{14,10},{15,11},{20,16},{21,... | collective-permute-start | bytes 1572872 | tf_op jit(solution)/shard_map/ppermute | solution.py:203
  27.8 3.2 %collective-permute-start.8 = (f32[128,128]{1,0:T(8,128)S(1)}, f32[128,128]{1,0:T(8,128)S(1)}, u32[]{:S(2)}, u32[]{:S(2)}) collective-permute-start(f32[128,128]{1,0:T(8,128)S(1)} %add.22.inverse_ref), channel_id=1, source_target_pairs={{0,4},{1,5},{2,6},{3,7},{8,12},{9,13},{10,14},{11,15},{16,20},{17,... | collective-permute-start | bytes 196616 | tf_op jit(solution)/shard_map/ppermute | solution.py:203
  31.1 0.9 %collective-permute-done.8.inverse_from_ref = f32[128,128]{1,0:T(8,128)S(1)} collective-permute-done((f32[128,128]{1,0:T(8,128)S(1)}, f32[128,128]{1,0:T(8,128)S(1)}, u32[]{:S(2)}, u32[]{:S(2)}) %collective-permute-start.8) | collective-permute-done | bytes 65568 | tf_op jit(solution)/shard_map/ppermute | solution.py:203
  32.0 3.7 %collective-permute-done.12.refs_2_ = f32[1024,128]{1,0:T(8,128)S(1)} collective-permute-done((f32[1024,128]{1,0:T(8,128)S(1)}, f32[1024,128]{1,0:T(8,128)S(1)}, u32[]{:S(2)}, u32[]{:S(2)}) %collective-permute-start.12) | collective-permute-done | bytes 524320 | tf_op jit(solution)/shard_map/ppermute | solution.py:203
  35.7 0.0 collective-permute-done.11.mirror_even_ref
  35.7 0.0 copy-done
  35.7 4.4 %update.1 = f32[1024,1024]{1,0:T(8,128)} custom-call(f32[128,128]{1,0:T(8,128)S(1)} %broadcast_select_fusion.lower_ref, f32[128,128]{1,0:T(8,128)S(1)} %add.22.inverse_ref, f32[128,128]{1,0:T(8,128)S(1)} %collective-permute-done.8.inverse_from_ref, f32[1024,1024]{1,0:T(8,128)S(1)} %copy-done, f32[1024,128]{1,0:T(8,128)S(1)} %collective-permute-done.11.mirror_even_ref, ...), custom_call_target="tpu_custom_call" | custom-call | flops 805306368 | bytes 8388608 | tf_op jit(solution)/shard_map/update/pallas_call | solution.py:174
  (7 shorter events, 0.1 us)
Async XLA Ops:
  2.2 8.0 %collective-permute-start.1 = (f32[128,128]{1,0:T(8,128)}, f32[128,128]{1,0:T(8,128)S(1)}, u32[]{:S(2)}, u32[]{:S(2)}) collective-permute-start(f32[128,128]{1,0:T(8,128)} %get-tuple-element.15), channel_id=1, source_target_pairs={{0,3}} | collective-permute-start | bytes 196616 | tf_op jit(solution)/shard_map/ppermute | solution.py:203
  3.5 9.9 %collective-permute-start = (f32[512,128]{1,0:T(8,128)}, f32[512,128]{1,0:T(8,128)S(1)}, u32[]{:S(2)}, u32[]{:S(2)}) collective-permute-start(f32[512,128]{1,0:T(8,128)} %get-tuple-element.13), channel_id=1, source_target_pairs={{0,4},{4,5},{8,14},{12,15},{16,20},{20,21},{24,30},{28,31}} | collective-permute-start | bytes 786440 | tf_op jit(solution)/shard_map/ppermute | solution.py:203
  4.1 17.1 %collective-permute-start.6 = (f32[1024,128]{1,0:T(8,128)}, f32[1024,128]{1,0:T(8,128)S(1)}, u32[]{:S(2)}, u32[]{:S(2)}) collective-permute-start(f32[1024,128]{1,0:T(8,128)} %get-tuple-element.17), channel_id=1, source_target_pairs={{0,2},{4,6},{8,10},{12,14},{16,18},{20,22},{24,26},{28,30}} | collective-permute-start | bytes 1572872 | tf_op jit(solution)/shard_map/ppermute | solution.py:203
  4.8 16.4 %collective-permute-start.5 = (f32[1024,128]{1,0:T(8,128)}, f32[1024,128]{1,0:T(8,128)S(1)}, u32[]{:S(2)}, u32[]{:S(2)}) collective-permute-start(f32[1024,128]{1,0:T(8,128)} %get-tuple-element.17), channel_id=1, source_target_pairs={{0,1},{4,5},{8,9},{12,13},{16,17},{20,21},{24,25},{28,29}} | collective-permute-start | bytes 1572872 | tf_op jit(solution)/shard_map/ppermute | solution.py:203
  5.6 30.1 %copy-start = (f32[1024,1024]{1,0:T(8,128)S(1)}, f32[1024,1024]{1,0:T(8,128)}, u32[]{:S(2)}) copy-start(f32[1024,1024]{1,0:T(8,128)} %matrix_ref.3) | copy-start | bytes 12582916
  10.2 3.2 %collective-permute-start.2 = (f32[128,128]{1,0:T(8,128)S(1)}, f32[128,128]{1,0:T(8,128)S(1)}, u32[]{:S(2)}, u32[]{:S(2)}) collective-permute-start(f32[128,128]{1,0:T(8,128)S(1)} %collective-permute-done.1), channel_id=1, source_target_pairs={{3,19}} | collective-permute-start | bytes 196616 | tf_op jit(solution)/shard_map/ppermute | solution.py:203
  13.4 0.7 %collective-permute-start.9 = (f32[512,128]{1,0:T(8,128)S(1)}, f32[512,128]{1,0:T(8,128)S(1)}, u32[]{:S(2)}, u32[]{:S(2)}) collective-permute-start(f32[512,128]{1,0:T(8,128)S(1)} %collective-permute-done), channel_id=1, source_target_pairs={{4,12},{20,28},{5,13},{21,29},{14,6},{30,22},{15,7},{31,23}} | collective-permute-start | bytes 786440 | tf_op jit(solution)/shard_map/ppermute | solution.py:203
  14.1 12.4 %collective-permute-start.10 = (f32[512,128]{1,0:T(8,128)S(1)}, f32[512,128]{1,0:T(8,128)S(1)}, u32[]{:S(2)}, u32[]{:S(2)}) collective-permute-start(f32[512,128]{1,0:T(8,128)S(1)} %add.23), channel_id=1, source_target_pairs={{20,4},{4,20},{21,5},{5,21},{30,14},{14,30},{31,15},{15,31},{28,12... | collective-permute-start | bytes 786440 | tf_op jit(solution)/shard_map/ppermute | solution.py:203
  14.8 3.2 %collective-permute-start.3 = (f32[128,128]{1,0:T(8,128)S(1)}, f32[128,128]{1,0:T(8,128)S(1)}, u32[]{:S(2)}, u32[]{:S(2)}) collective-permute-start(f32[128,128]{1,0:T(8,128)S(1)} %add.18), channel_id=1, source_target_pairs={{3,11},{19,27}} | collective-permute-start | bytes 196616 | tf_op jit(solution)/shard_map/ppermute | solution.py:203
  18.0 3.2 %collective-permute-start.4 = (f32[128,128]{1,0:T(8,128)S(1)}, f32[128,128]{1,0:T(8,128)S(1)}, u32[]{:S(2)}, u32[]{:S(2)}) collective-permute-start(f32[128,128]{1,0:T(8,128)S(1)} %add.19), channel_id=1, source_target_pairs={{3,2},{19,18},{11,10},{27,26}} | collective-permute-start | bytes 196616 | tf_op jit(solution)/shard_map/ppermute | solution.py:203
  21.3 5.2 %collective-permute-start.7 = (f32[128,128]{1,0:T(8,128)S(1)}, f32[128,128]{1,0:T(8,128)S(1)}, u32[]{:S(2)}, u32[]{:S(2)}) collective-permute-start(f32[128,128]{1,0:T(8,128)S(1)} %add.20), channel_id=1, source_target_pairs={{3,1},{19,17},{11,9},{27,25},{2,0},{18,16},{10,8},{26,24}} | collective-permute-start | bytes 196616 | tf_op jit(solution)/shard_map/ppermute | solution.py:203
  24.6 11.1 %collective-permute-start.12 = (f32[1024,128]{1,0:T(8,128)S(1)}, f32[1024,128]{1,0:T(8,128)S(1)}, u32[]{:S(2)}, u32[]{:S(2)}) collective-permute-start(f32[1024,128]{1,0:T(8,128)S(1)} %add.21), channel_id=1, source_target_pairs={{1,3},{6,7},{9,11},{14,15},{17,19},{22,23},{25,27},{30,31}} | collective-permute-start | bytes 1572872 | tf_op jit(solution)/shard_map/ppermute | solution.py:203
  26.5 9.1 %collective-permute-start.11 = (f32[1024,128]{1,0:T(8,128)S(1)}, f32[1024,128]{1,0:T(8,128)S(1)}, u32[]{:S(2)}, u32[]{:S(2)}) collective-permute-start(f32[1024,128]{1,0:T(8,128)S(1)} %pad_maximum_fusion.mirror_odd_ref), channel_id=1, source_target_pairs={{4,0},{5,1},{6,2},{7,3},{12,8},{13,9},{14,10},{15,11},{20,16},{21,... | collective-permute-start | bytes 1572872 | tf_op jit(solution)/shard_map/ppermute | solution.py:203
  27.8 4.1 %collective-permute-start.8 = (f32[128,128]{1,0:T(8,128)S(1)}, f32[128,128]{1,0:T(8,128)S(1)}, u32[]{:S(2)}, u32[]{:S(2)}) collective-permute-start(f32[128,128]{1,0:T(8,128)S(1)} %add.22.inverse_ref), channel_id=1, source_target_pairs={{0,4},{1,5},{2,6},{3,7},{8,12},{9,13},{10,14},{11,15},{16,20},{17,... | collective-permute-start | bytes 196616 | tf_op jit(solution)/shard_map/ppermute | solution.py:203

commit v9 on v8

--- a/solution.py
+++ b/solution.py
@@ -10,7 +10,6 @@
 NB = 128
 TILE = 256
 AXES = ("row", "col")
-HIGHEST = lax.Precision.HIGHEST
 TRANS_B = (((1,), (1,)), ((), ()))
 
 
@@ -101,6 +100,20 @@
     return high, low
 
 
+def dot_t(a, b):
+    return lax.dot_general(a, b, TRANS_B, preferred_element_type=jnp.float32)
+
+
+def left_parts(value):
+    high, low = split(value)
+    return jnp.concatenate([high, low, high], axis=1)
+
+
+def right_parts(value):
+    high, low = split(value)
+    return jnp.concatenate([high, high, low], axis=1)
+
+
 def update_kernel(plan, lower_ref, inverse_ref, inverse_from_ref, matrix_ref, mirror_even_ref, mirror_odd_ref, *refs):
     rows_here, cols_here, sources = plan
     panel_refs = refs[:cols_here - 1]
@@ -130,23 +143,14 @@
         def _(c=c):
             panel[...] = panel_refs[c - 1][...]
 
-    inverse = inverse_ref[...] + inverse_from_ref[...]
+    inverse_parts = right_parts(inverse_ref[...] + inverse_from_ref[...])
     for t in range(col_blocks):
         block = (t % sources) * each + (t // sources) * NB
-        part = lax.dot_general(mirror[pl.ds(block, NB), :], inverse, TRANS_B, precision=HIGHEST,
-                               preferred_element_type=jnp.float32)
-        high, low = split(part)
-        at = pl.ds(t * NB, NB)
-        rhs[at, pl.ds(0, NB)] = high
-        rhs[at, pl.ds(NB, NB)] = high
-        rhs[at, pl.ds(2 * NB, NB)] = low
+        rhs[pl.ds(t * NB, NB), :] = right_parts(dot_t(left_parts(mirror[pl.ds(block, NB), :]), inverse_parts))
 
     for i in range(tiles):
-        tall = lax.dot_general(panel[here[i], :], inverse, TRANS_B, precision=HIGHEST,
-                               preferred_element_type=jnp.float32)
-        high, low = split(tall)
-        lhs = jnp.concatenate([high, low, high], axis=1)
-        product = lax.dot_general(lhs, rhs[...], TRANS_B, preferred_element_type=jnp.float32)
+        tall = dot_t(left_parts(panel[here[i], :]), inverse_parts)
+        product = dot_t(left_parts(tall), rhs[...])
         for s in range(TILE // NB):
             row = (i * (TILE // NB) + s) * rows_here + row_index
             down = pl.ds(i * TILE + s * NB, NB)

time: 40.4 us -> 39.2 us (0.970)
  Pallas kernels: 6.57 us -> 5.39 us
    pallas_call x1, Pallas kernels: 4.42 us -> 3.25 us  [update(): pl.pallas_call(functools.partial(update_kernel, plan), out_shape=jax.Shap...]
where the time goes in v9:
time: 39.2 us; the launch traced here: 38.9 us
  starting transfers between devices  17.7 us (45%)
  waiting for transfers between devices  15.4 us (39%)
  Pallas kernels  5.39 us (14%)
    ppermute x13, starting transfers between devices, send(): lax.ppermute(value, AXES, [(a * cols_here + b, c * cols_here + d) for (a,...  17.7 us
    ppermute x13, waiting for transfers between devices, send(): lax.ppermute(value, AXES, [(a * cols_here + b, c * cols_here + d) for (a,...  15.4 us
    pallas_call x1, Pallas kernels, update(): pl.pallas_call(functools.partial(update_kernel, plan), out_shape=jax.Shap...  3.25 us
    pallas_call x1, Pallas kernels, factor(): pl.pallas_call(factor_kernel, out_shape=[square, square, *tall], in_specs...  2.14 us
  transfers between devices with their start and end apart: 13, of which 7 were waited for; matrix products, arithmetic and copies ran while one was open for 0% of the time, Pallas kernels for 0%

profile of v9, /device:TPU:6, one launch (start us, length us, event | category | flops | bytes accessed | tf_op | source)
XLA Modules:
  0.0 38.9 jit_solution(17544594761800752598)
XLA Ops:
  0.0 2.1 %factor.1 = (f32[128,128]{1,0:T(8,128)}, f32[128,128]{1,0:T(8,128)}, f32[1024,128]{1,0:T(8,128)}, f32[512,128]{1,0:T(8,128)}) custom-call(f32[1024,1024]{1,0:T(8,128)} %matrix_ref.3), custom_call_target="tpu_custom_call" | custom-call | flops 4000000 | bytes 200000 | tf_op jit(solution)/shard_map/factor/pallas_call | solution.py:85
  2.2 1.3 %collective-permute-start.1 = (f32[128,128]{1,0:T(8,128)}, f32[128,128]{1,0:T(8,128)S(1)}, u32[]{:S(2)}, u32[]{:S(2)}) collective-permute-start(f32[128,128]{1,0:T(8,128)} %get-tuple-element.15), channel_id=1, source_target_pairs={{0,3}} | collective-permute-start | bytes 196616 | tf_op jit(solution)/shard_map/ppermute | solution.py:207
  3.5 0.7 %collective-permute-start = (f32[512,128]{1,0:T(8,128)}, f32[512,128]{1,0:T(8,128)S(1)}, u32[]{:S(2)}, u32[]{:S(2)}) collective-permute-start(f32[512,128]{1,0:T(8,128)} %get-tuple-element.13), channel_id=1, source_target_pairs={{0,4},{4,5},{8,14},{12,15},{16,20},{20,21},{24,30},{28,31}} | collective-permute-start | bytes 786440 | tf_op jit(solution)/shard_map/ppermute | solution.py:207
  4.1 0.7 %collective-permute-start.6 = (f32[1024,128]{1,0:T(8,128)}, f32[1024,128]{1,0:T(8,128)S(1)}, u32[]{:S(2)}, u32[]{:S(2)}) collective-permute-start(f32[1024,128]{1,0:T(8,128)} %get-tuple-element.17), channel_id=1, source_target_pairs={{0,2},{4,6},{8,10},{12,14},{16,18},{20,22},{24,26},{28,30}} | collective-permute-start | bytes 1572872 | tf_op jit(solution)/shard_map/ppermute | solution.py:207
  4.8 0.7 %collective-permute-start.5 = (f32[1024,128]{1,0:T(8,128)}, f32[1024,128]{1,0:T(8,128)S(1)}, u32[]{:S(2)}, u32[]{:S(2)}) collective-permute-start(f32[1024,128]{1,0:T(8,128)} %get-tuple-element.17), channel_id=1, source_target_pairs={{0,1},{4,5},{8,9},{12,13},{16,17},{20,21},{24,25},{28,29}} | collective-permute-start | bytes 1572872 | tf_op jit(solution)/shard_map/ppermute | solution.py:207
  5.6 0.0 copy-start
  5.6 4.6 %collective-permute-done.1 = f32[128,128]{1,0:T(8,128)S(1)} collective-permute-done((f32[128,128]{1,0:T(8,128)}, f32[128,128]{1,0:T(8,128)S(1)}, u32[]{:S(2)}, u32[]{:S(2)}) %collective-permute-start.1) | collective-permute-done | bytes 65568 | tf_op jit(solution)/shard_map/ppermute | solution.py:207
  10.2 1.3 %collective-permute-start.2 = (f32[128,128]{1,0:T(8,128)S(1)}, f32[128,128]{1,0:T(8,128)S(1)}, u32[]{:S(2)}, u32[]{:S(2)}) collective-permute-start(f32[128,128]{1,0:T(8,128)S(1)} %collective-permute-done.1), channel_id=1, source_target_pairs={{3,19}} | collective-permute-start | bytes 196616 | tf_op jit(solution)/shard_map/ppermute | solution.py:207
  11.5 1.9 %collective-permute-done.2 = f32[128,128]{1,0:T(8,128)S(1)} collective-permute-done((f32[128,128]{1,0:T(8,128)S(1)}, f32[128,128]{1,0:T(8,128)S(1)}, u32[]{:S(2)}, u32[]{:S(2)}) %collective-permute-start.2) | collective-permute-done | bytes 65568 | tf_op jit(solution)/shard_map/ppermute | solution.py:207
  13.4 0.0 collective-permute-done
  13.4 0.7 %collective-permute-start.9 = (f32[512,128]{1,0:T(8,128)S(1)}, f32[512,128]{1,0:T(8,128)S(1)}, u32[]{:S(2)}, u32[]{:S(2)}) collective-permute-start(f32[512,128]{1,0:T(8,128)S(1)} %collective-permute-done), channel_id=1, source_target_pairs={{4,12},{20,28},{5,13},{21,29},{14,6},{30,22},{15,7},{31,23}} | collective-permute-start | bytes 786440 | tf_op jit(solution)/shard_map/ppermute | solution.py:207
  14.1 0.0 collective-permute-done.9
  14.1 0.7 %collective-permute-start.10 = (f32[512,128]{1,0:T(8,128)S(1)}, f32[512,128]{1,0:T(8,128)S(1)}, u32[]{:S(2)}, u32[]{:S(2)}) collective-permute-start(f32[512,128]{1,0:T(8,128)S(1)} %add.23), channel_id=1, source_target_pairs={{20,4},{4,20},{21,5},{5,21},{30,14},{14,30},{31,15},{15,31},{28,12... | collective-permute-start | bytes 786440 | tf_op jit(solution)/shard_map/ppermute | solution.py:207
  14.8 1.3 %collective-permute-start.3 = (f32[128,128]{1,0:T(8,128)S(1)}, f32[128,128]{1,0:T(8,128)S(1)}, u32[]{:S(2)}, u32[]{:S(2)}) collective-permute-start(f32[128,128]{1,0:T(8,128)S(1)} %add.18), channel_id=1, source_target_pairs={{3,11},{19,27}} | collective-permute-start | bytes 196616 | tf_op jit(solution)/shard_map/ppermute | solution.py:207
  16.1 1.9 %collective-permute-done.3 = f32[128,128]{1,0:T(8,128)S(1)} collective-permute-done((f32[128,128]{1,0:T(8,128)S(1)}, f32[128,128]{1,0:T(8,128)S(1)}, u32[]{:S(2)}, u32[]{:S(2)}) %collective-permute-start.3) | collective-permute-done | bytes 65568 | tf_op jit(solution)/shard_map/ppermute | solution.py:207
  18.0 1.3 %collective-permute-start.4 = (f32[128,128]{1,0:T(8,128)S(1)}, f32[128,128]{1,0:T(8,128)S(1)}, u32[]{:S(2)}, u32[]{:S(2)}) collective-permute-start(f32[128,128]{1,0:T(8,128)S(1)} %add.19), channel_id=1, source_target_pairs={{3,2},{19,18},{11,10},{27,26}} | collective-permute-start | bytes 196616 | tf_op jit(solution)/shard_map/ppermute | solution.py:207
  19.3 1.9 %collective-permute-done.4 = f32[128,128]{1,0:T(8,128)S(1)} collective-permute-done((f32[128,128]{1,0:T(8,128)S(1)}, f32[128,128]{1,0:T(8,128)S(1)}, u32[]{:S(2)}, u32[]{:S(2)}) %collective-permute-start.4) | collective-permute-done | bytes 65568 | tf_op jit(solution)/shard_map/ppermute | solution.py:207
  21.2 0.0 collective-permute-done.6.refs_1_
  21.2 0.0 collective-permute-done.5.refs_0_
  21.2 0.1 add.21
  21.3 3.3 %collective-permute-start.7 = (f32[128,128]{1,0:T(8,128)S(1)}, f32[128,128]{1,0:T(8,128)S(1)}, u32[]{:S(2)}, u32[]{:S(2)}) collective-permute-start(f32[128,128]{1,0:T(8,128)S(1)} %add.20), channel_id=1, source_target_pairs={{3,1},{19,17},{11,9},{27,25},{2,0},{18,16},{10,8},{26,24}} | collective-permute-start | bytes 196616 | tf_op jit(solution)/shard_map/ppermute | solution.py:207
  24.6 1.3 %collective-permute-start.12 = (f32[1024,128]{1,0:T(8,128)S(1)}, f32[1024,128]{1,0:T(8,128)S(1)}, u32[]{:S(2)}, u32[]{:S(2)}) collective-permute-start(f32[1024,128]{1,0:T(8,128)S(1)} %add.21), channel_id=1, source_target_pairs={{1,3},{6,7},{9,11},{14,15},{17,19},{22,23},{25,27},{30,31}} | collective-permute-start | bytes 1572872 | tf_op jit(solution)/shard_map/ppermute | solution.py:207
  25.9 0.6 %collective-permute-done.7 = f32[128,128]{1,0:T(8,128)S(1)} collective-permute-done((f32[128,128]{1,0:T(8,128)S(1)}, f32[128,128]{1,0:T(8,128)S(1)}, u32[]{:S(2)}, u32[]{:S(2)}) %collective-permute-start.7) | collective-permute-done | bytes 65568 | tf_op jit(solution)/shard_map/ppermute | solution.py:207
  26.5 0.0 collective-permute-done.10
  26.5 1.3 %collective-permute-start.11 = (f32[1024,128]{1,0:T(8,128)S(1)}, f32[1024,128]{1,0:T(8,128)S(1)}, u32[]{:S(2)}, u32[]{:S(2)}) collective-permute-start(f32[1024,128]{1,0:T(8,128)S(1)} %pad_maximum_fusion.mirror_odd_ref), channel_id=1, source_target_pairs={{4,0},{5,1},{6,2},{7,3},{12,8},{13,9},{14,10},{15,11},{20,16},{21,... | collective-permute-start | bytes 1572872 | tf_op jit(solution)/shard_map/ppermute | solution.py:207
  27.8 3.2 %collective-permute-start.8 = (f32[128,128]{1,0:T(8,128)S(1)}, f32[128,128]{1,0:T(8,128)S(1)}, u32[]{:S(2)}, u32[]{:S(2)}) collective-permute-start(f32[128,128]{1,0:T(8,128)S(1)} %add.22.inverse_ref), channel_id=1, source_target_pairs={{0,4},{1,5},{2,6},{3,7},{8,12},{9,13},{10,14},{11,15},{16,20},{17,... | collective-permute-start | bytes 196616 | tf_op jit(solution)/shard_map/ppermute | solution.py:207
  31.1 0.9 %collective-permute-done.8.inverse_from_ref = f32[128,128]{1,0:T(8,128)S(1)} collective-permute-done((f32[128,128]{1,0:T(8,128)S(1)}, f32[128,128]{1,0:T(8,128)S(1)}, u32[]{:S(2)}, u32[]{:S(2)}) %collective-permute-start.8) | collective-permute-done | bytes 65568 | tf_op jit(solution)/shard_map/ppermute | solution.py:207
  32.0 3.7 %collective-permute-done.12.refs_2_ = f32[1024,128]{1,0:T(8,128)S(1)} collective-permute-done((f32[1024,128]{1,0:T(8,128)S(1)}, f32[1024,128]{1,0:T(8,128)S(1)}, u32[]{:S(2)}, u32[]{:S(2)}) %collective-permute-start.12) | collective-permute-done | bytes 524320 | tf_op jit(solution)/shard_map/ppermute | solution.py:207
  35.7 0.0 collective-permute-done.11.mirror_even_ref
  35.7 0.0 copy-done
  35.7 3.2 %update.1 = f32[1024,1024]{1,0:T(8,128)} custom-call(f32[128,128]{1,0:T(8,128)S(1)} %broadcast_select_fusion.lower_ref, f32[128,128]{1,0:T(8,128)S(1)} %add.22.inverse_ref, f32[128,128]{1,0:T(8,128)S(1)} %collective-permute-done.8.inverse_from_ref, f32[1024,1024]{1,0:T(8,128)S(1)} %copy-done, f32[1024,128]{1,0:T(8,128)S(1)} %collective-permute-done.11.mirror_even_ref, ...), custom_call_target="tpu_custom_call" | custom-call | flops 805306368 | bytes 8388608 | tf_op jit(solution)/shard_map/update/pallas_call | solution.py:178
  (7 shorter events, 0.1 us)
Async XLA Ops:
  2.2 8.0 %collective-permute-start.1 = (f32[128,128]{1,0:T(8,128)}, f32[128,128]{1,0:T(8,128)S(1)}, u32[]{:S(2)}, u32[]{:S(2)}) collective-permute-start(f32[128,128]{1,0:T(8,128)} %get-tuple-element.15), channel_id=1, source_target_pairs={{0,3}} | collective-permute-start | bytes 196616 | tf_op jit(solution)/shard_map/ppermute | solution.py:207
  3.5 9.9 %collective-permute-start = (f32[512,128]{1,0:T(8,128)}, f32[512,128]{1,0:T(8,128)S(1)}, u32[]{:S(2)}, u32[]{:S(2)}) collective-permute-start(f32[512,128]{1,0:T(8,128)} %get-tuple-element.13), channel_id=1, source_target_pairs={{0,4},{4,5},{8,14},{12,15},{16,20},{20,21},{24,30},{28,31}} | collective-permute-start | bytes 786440 | tf_op jit(solution)/shard_map/ppermute | solution.py:207
  4.1 17.1 %collective-permute-start.6 = (f32[1024,128]{1,0:T(8,128)}, f32[1024,128]{1,0:T(8,128)S(1)}, u32[]{:S(2)}, u32[]{:S(2)}) collective-permute-start(f32[1024,128]{1,0:T(8,128)} %get-tuple-element.17), channel_id=1, source_target_pairs={{0,2},{4,6},{8,10},{12,14},{16,18},{20,22},{24,26},{28,30}} | collective-permute-start | bytes 1572872 | tf_op jit(solution)/shard_map/ppermute | solution.py:207
  4.8 16.4 %collective-permute-start.5 = (f32[1024,128]{1,0:T(8,128)}, f32[1024,128]{1,0:T(8,128)S(1)}, u32[]{:S(2)}, u32[]{:S(2)}) collective-permute-start(f32[1024,128]{1,0:T(8,128)} %get-tuple-element.17), channel_id=1, source_target_pairs={{0,1},{4,5},{8,9},{12,13},{16,17},{20,21},{24,25},{28,29}} | collective-permute-start | bytes 1572872 | tf_op jit(solution)/shard_map/ppermute | solution.py:207
  5.6 30.1 %copy-start = (f32[1024,1024]{1,0:T(8,128)S(1)}, f32[1024,1024]{1,0:T(8,128)}, u32[]{:S(2)}) copy-start(f32[1024,1024]{1,0:T(8,128)} %matrix_ref.3) | copy-start | bytes 12582916
  10.2 3.2 %collective-permute-start.2 = (f32[128,128]{1,0:T(8,128)S(1)}, f32[128,128]{1,0:T(8,128)S(1)}, u32[]{:S(2)}, u32[]{:S(2)}) collective-permute-start(f32[128,128]{1,0:T(8,128)S(1)} %collective-permute-done.1), channel_id=1, source_target_pairs={{3,19}} | collective-permute-start | bytes 196616 | tf_op jit(solution)/shard_map/ppermute | solution.py:207
  13.4 0.7 %collective-permute-start.9 = (f32[512,128]{1,0:T(8,128)S(1)}, f32[512,128]{1,0:T(8,128)S(1)}, u32[]{:S(2)}, u32[]{:S(2)}) collective-permute-start(f32[512,128]{1,0:T(8,128)S(1)} %collective-permute-done), channel_id=1, source_target_pairs={{4,12},{20,28},{5,13},{21,29},{14,6},{30,22},{15,7},{31,23}} | collective-permute-start | bytes 786440 | tf_op jit(solution)/shard_map/ppermute | solution.py:207
  14.1 12.4 %collective-permute-start.10 = (f32[512,128]{1,0:T(8,128)S(1)}, f32[512,128]{1,0:T(8,128)S(1)}, u32[]{:S(2)}, u32[]{:S(2)}) collective-permute-start(f32[512,128]{1,0:T(8,128)S(1)} %add.23), channel_id=1, source_target_pairs={{20,4},{4,20},{21,5},{5,21},{30,14},{14,30},{31,15},{15,31},{28,12... | collective-permute-start | bytes 786440 | tf_op jit(solution)/shard_map/ppermute | solution.py:207
  14.8 3.2 %collective-permute-start.3 = (f32[128,128]{1,0:T(8,128)S(1)}, f32[128,128]{1,0:T(8,128)S(1)}, u32[]{:S(2)}, u32[]{:S(2)}) collective-permute-start(f32[128,128]{1,0:T(8,128)S(1)} %add.18), channel_id=1, source_target_pairs={{3,11},{19,27}} | collective-permute-start | bytes 196616 | tf_op jit(solution)/shard_map/ppermute | solution.py:207
  18.0 3.2 %collective-permute-start.4 = (f32[128,128]{1,0:T(8,128)S(1)}, f32[128,128]{1,0:T(8,128)S(1)}, u32[]{:S(2)}, u32[]{:S(2)}) collective-permute-start(f32[128,128]{1,0:T(8,128)S(1)} %add.19), channel_id=1, source_target_pairs={{3,2},{19,18},{11,10},{27,26}} | collective-permute-start | bytes 196616 | tf_op jit(solution)/shard_map/ppermute | solution.py:207
  21.3 5.2 %collective-permute-start.7 = (f32[128,128]{1,0:T(8,128)S(1)}, f32[128,128]{1,0:T(8,128)S(1)}, u32[]{:S(2)}, u32[]{:S(2)}) collective-permute-start(f32[128,128]{1,0:T(8,128)S(1)} %add.20), channel_id=1, source_target_pairs={{3,1},{19,17},{11,9},{27,25},{2,0},{18,16},{10,8},{26,24}} | collective-permute-start | bytes 196616 | tf_op jit(solution)/shard_map/ppermute | solution.py:207
  24.6 11.1 %collective-permute-start.12 = (f32[1024,128]{1,0:T(8,128)S(1)}, f32[1024,128]{1,0:T(8,128)S(1)}, u32[]{:S(2)}, u32[]{:S(2)}) collective-permute-start(f32[1024,128]{1,0:T(8,128)S(1)} %add.21), channel_id=1, source_target_pairs={{1,3},{6,7},{9,11},{14,15},{17,19},{22,23},{25,27},{30,31}} | collective-permute-start | bytes 1572872 | tf_op jit(solution)/shard_map/ppermute | solution.py:207
  26.5 9.1 %collective-permute-start.11 = (f32[1024,128]{1,0:T(8,128)S(1)}, f32[1024,128]{1,0:T(8,128)S(1)}, u32[]{:S(2)}, u32[]{:S(2)}) collective-permute-start(f32[1024,128]{1,0:T(8,128)S(1)} %pad_maximum_fusion.mirror_odd_ref), channel_id=1, source_target_pairs={{4,0},{5,1},{6,2},{7,3},{12,8},{13,9},{14,10},{15,11},{20,16},{21,... | collective-permute-start | bytes 1572872 | tf_op jit(solution)/shard_map/ppermute | solution.py:207
  27.8 4.1 %collective-permute-start.8 = (f32[128,128]{1,0:T(8,128)S(1)}, f32[128,128]{1,0:T(8,128)S(1)}, u32[]{:S(2)}, u32[]{:S(2)}) collective-permute-start(f32[128,128]{1,0:T(8,128)S(1)} %add.22.inverse_ref), channel_id=1, source_target_pairs={{0,4},{1,5},{2,6},{3,7},{8,12},{9,13},{10,14},{11,15},{16,20},{17,... | collective-permute-start | bytes 196616 | tf_op jit(solution)/shard_map/ppermute | solution.py:207
